TPU v7x, 256 devices: a whole 4x4x8 slice. The times are simulated.
256 devices in a mesh: track: 8 (over x, core), tile: 32 (over z, y).
Axes of the slice: x: 4, y: 4, z: 8, core: 2. Of those that a mesh axis runs over, the one named last changes fastest.
Arguments:
- panels: bfloat16 [262144, 1024], P(('track', 'tile')), may hold values from -6 to 6
- phases: float32 [16384], P(('track', 'tile')), may hold values from -3.140625 to 3.140625
- weight_tiles: bfloat16 [4, 1024, 512], replicated, may hold values from -0.015625 to 0.015625
- tile_class: int32 [1024], P(('track', 'tile')), may hold values from 0 to 3
- send_slots: int32 [196608], P(('track', 'tile')), may hold values from -1 to 1023, as said below
- foot_slot: int32 [1024, 512], P(('track', 'tile')), may hold values from 0 to 767, as said below
- foot_ping: int32 [1024, 512], P(('track', 'tile')), may hold values from 0 to 16383, as said below
- tile_counts: int32 [1024], P(('track', 'tile')), may hold values from 102 to 512, as said below
Outputs:
- image: float32 [1024, 2, 1024], P(('track', 'tile'))
- ping_gradient: float32 [16384], P(('track', 'tile'))
Inputs may be any that keep to these rules, and one draw needn't show every extreme that they name: `send_slots`: entries name local panel rows of the sending device; an entry is -1 exactly where the track group of its offset (offset minus 1) lies outside the slice. `foot_slot`: the entries of one tile are distinct slots, each of which holds a panel. foot_ping[t, f] is the ping of the panel in slot foot_slot[t, f] of tile t's device. `tile_counts`: only the first tile_counts_t entries of tile t's footprint lists are used.
All inputs are finite; a program needn't handle non-finite values.
Results may differ from a plain program's by a relative error of at most 0.0065.
Values may be sent and summed in bfloat16 or wider, within the bound.
No kernel may reach another device: no remote copies, remote signals or barrier semaphores. Data moves between devices by JAX's collectives and lax.ppermute only.
A program may use at most 128 MiB of HBM per device.

v0:
```python
import jax
import jax.numpy as jnp
from jax import lax
from jax.sharding import PartitionSpec as P

BLK = 128


def from_behind_2(block, axis, distance):
    devices = range(lax.axis_size(axis))
    route = [(i - distance, i) for i in devices if i - distance in devices]
    return lax.ppermute(block, axis, route)


def rotate_panels(panels, phases):
    bin_count = panels.shape[1] // 2
    blocks_per_ping = panels.shape[0] // phases.shape[0]
    cos_rows = jnp.repeat(jnp.cos(phases), blocks_per_ping)[:, None]
    sin_rows = jnp.repeat(jnp.sin(phases), blocks_per_ping)[:, None]
    real_part = panels[:, :bin_count].astype(jnp.float32)
    imag_part = panels[:, bin_count:].astype(jnp.float32)
    turned = jnp.concatenate(
        [cos_rows * real_part - sin_rows * imag_part, sin_rows * real_part + cos_rows * imag_part],
        axis=1,
    )
    return turned.astype(jnp.bfloat16)


def phase_terms(ping_ids, tile_global, ping_total, tile_total, track_groups, pixels):
    offset = (2 * ping_ids + 1) * tile_total - (2 * tile_global + 1) * ping_total
    along = offset.astype(jnp.float32) * (track_groups / (2.0 * ping_total * tile_total))
    across = (jnp.arange(pixels, dtype=jnp.int32).astype(jnp.float32) + 0.5) / pixels - 0.5
    angles = 96.0 * across[:, None] * along[None, :] + 8.0 * (along * along)[None, :]
    return (jnp.cos(angles), jnp.sin(angles))


def panels_across(parts):
    from_behind = from_behind_2(parts[2], "track", 1)
    from_ahead = from_behind_2(parts[0], "track", -1)
    return jnp.stack([from_behind, parts[1], from_ahead])


def partials_across(parts):
    from_behind = from_behind_2(parts[2], "track", 1)
    from_ahead = from_behind_2(parts[0], "track", -1)
    return jnp.stack([from_behind, parts[1], from_ahead])


def on_device(
    panels, phases, weight_tiles, tile_class, send_slots, foot_slot, foot_ping, tile_counts
):
    track_devs = lax.axis_size("track")
    tile_devs = lax.axis_size("tile")
    device = lax.axis_index("track") * tile_devs + lax.axis_index("tile")
    ping_local = phases.shape[0]
    row_width = panels.shape[1]
    bin_count = row_width // 2
    tiles_here = tile_counts.shape[0]
    pixels = weight_tiles.shape[1]
    group_slots = send_slots.shape[0] // 3
    slot_cap = group_slots // tile_devs
    ping_total = ping_local * track_devs * tile_devs
    tile_total = tiles_here * track_devs * tile_devs
    rotated = rotate_panels(panels, phases)
    present = send_slots >= 0
    outgoing = jnp.where(
        present[:, None], rotated[jnp.maximum(send_slots, 0)], jnp.zeros((), jnp.bfloat16)
    )
    outgoing = outgoing.reshape(3, tile_devs, slot_cap, row_width)
    arrived = lax.all_to_all(outgoing, "tile", split_axis=1, concat_axis=1, tiled=True)
    arrived = panels_across(arrived)
    received = arrived.reshape(3 * group_slots, row_width)
    positions = jnp.arange(BLK, dtype=jnp.int32)
    slot_partial = jnp.zeros((3 * group_slots,), jnp.float32)
    images = []
    for local_tile in range(tiles_here):
        weight = weight_tiles[tile_class[local_tile]]
        entry_count = tile_counts[local_tile]
        tile_global = device * tiles_here + local_tile
        block_count = (entry_count + BLK - 1) // BLK
        tile_slots = foot_slot[local_tile]
        tile_pings = foot_ping[local_tile]

        def load(
            block,
            tile_slots=tile_slots,
            tile_pings=tile_pings,
            tile_global=tile_global,
            entry_count=entry_count,
        ):
            start = block * BLK
            slot_ids = lax.dynamic_slice_in_dim(tile_slots, start, BLK, 0)
            ping_ids = lax.dynamic_slice_in_dim(tile_pings, start, BLK, 0)
            rows = received[slot_ids].reshape(2 * BLK, bin_count)
            cos_grid, sin_grid = phase_terms(
                ping_ids, tile_global, ping_total, tile_total, track_devs, pixels
            )
            active = (start + positions < entry_count).astype(jnp.float32)
            return (slot_ids, rows, cos_grid, sin_grid, active)

        def forward_step(block, carry, weight=weight, load=load):
            real_sum, imag_sum, stored = carry
            slot_ids, rows, cos_grid, sin_grid, active = load(block)
            product = lax.dot_general(
                weight, rows, (((1,), (1,)), ((), ())), preferred_element_type=jnp.float32
            )
            paired = product.reshape(pixels, BLK, 2)
            real_proj = paired[:, :, 0]
            imag_proj = paired[:, :, 1]
            real_sum = real_sum + jnp.sum(
                (cos_grid * real_proj - sin_grid * imag_proj) * active[None, :], axis=1
            )
            imag_sum = imag_sum + jnp.sum(
                (sin_grid * real_proj + cos_grid * imag_proj) * active[None, :], axis=1
            )
            return (real_sum, imag_sum, stored)

        zero_row = jnp.zeros((pixels,), jnp.float32)
        stored_init = jnp.zeros((1,), jnp.float32)
        real_sum, imag_sum, stored = lax.fori_loop(
            0, block_count, forward_step, (zero_row, zero_row, stored_init)
        )
        intensity = real_sum * real_sum + imag_sum * imag_sum
        heavy_real = intensity * real_sum
        heavy_imag = intensity * imag_sum

        def adjoint_step(
            block,
            partial_value,
            weight=weight,
            load=load,
            stored=stored,
            heavy_real=heavy_real,
            heavy_imag=heavy_imag,
        ):
            slot_ids, rows, cos_grid, sin_grid, active = load(block)
            adj_real = heavy_imag[:, None] * cos_grid - heavy_real[:, None] * sin_grid
            adj_imag = -(heavy_imag[:, None] * sin_grid + heavy_real[:, None] * cos_grid)
            adjoint = (
                jnp.stack([adj_real, adj_imag], axis=2)
                .astype(jnp.bfloat16)
                .reshape(pixels, 2 * BLK)
            )
            pulled = lax.dot_general(
                adjoint, weight, (((0,), (0,)), ((), ())), preferred_element_type=jnp.float32
            )
            correlation = (
                jnp.sum(rows.astype(jnp.float32) * pulled, axis=1).reshape(BLK, 2).sum(axis=1)
            )
            return partial_value.at[slot_ids].add(correlation * active)

        slot_partial = lax.fori_loop(0, block_count, adjoint_step, slot_partial)
        images.append(jnp.stack([real_sum, imag_sum]))
    partial_value = slot_partial.reshape(3, tile_devs, slot_cap)
    returned = partials_across(partial_value)
    returned = lax.all_to_all(returned, "tile", split_axis=1, concat_axis=1, tiled=True)
    flattened = jnp.where(present, returned.reshape(3 * group_slots), 0.0)
    panel_sums = jax.ops.segment_sum(
        flattened, jnp.maximum(send_slots, 0), num_segments=panels.shape[0]
    )
    ping_gradient = panel_sums.reshape(ping_local, -1).sum(axis=1)
    return (jnp.stack(images), ping_gradient)


def solution(mesh):
    in_specs = (
        P(("track", "tile"), None),
        P(("track", "tile")),
        P(),
        P(("track", "tile")),
        P(("track", "tile")),
        P(("track", "tile"), None),
        P(("track", "tile"), None),
        P(("track", "tile")),
    )
    out_specs = (P(("track", "tile"), None, None), P(("track", "tile")))
    return jax.shard_map(
        on_device, mesh=mesh, in_specs=in_specs, out_specs=out_specs, check_vma=False
    )
```

profile of v0, /device:TPU:6, one launch (start us, length us, event | category | flops | bytes accessed | tf_op | source)
XLA Modules:
  0.0 432.6 jit_solution(1390082226042219072)
XLA Ops:
  3.2 2.2 fusion.61
  5.7 3.6 gather_fusion.8
  9.2 2.7 copy_select_fusion
  12.0 11.6 %all-to-all-start = ((bf16[3,32,8,1024]{3,2,0,1:T(8,128)(2,1)}), bf16[3,32,8,1024]{3,2,0,1:T(8,128)(2,1)S(1)}, u32[]{:S(2)}, u32[]{:S(2)}) async-start(bf16[3,32,8,1024]{3,2,0,1:T(8,128)(2,1)} %copy_select_fusion), calls=%async_computation | async-start | bytes 3145728 | tf_op jit(solution)/shard_map/all_to_all | solution.py:70
  31.8 3.9 dynamic-slice_bitcast_fusion.3
  35.8 26.9 %all-to-all-done = bf16[3,32,8,1024]{3,2,0,1:T(8,128)(2,1)S(1)} async-done(((bf16[3,32,8,1024]{3,2,0,1:T(8,128)(2,1)}), bf16[3,32,8,1024]{3,2,0,1:T(8,128)(2,1)S(1)}, u32[]{:S(2)}, u32[]{:S(2)}) %all-to-all-start) | async-done | bytes 1572896 | tf_op jit(solution)/shard_map/all_to_all | solution.py:70
  63.9 1.9 collective-permute-start
  65.8 3.6 collective-permute-start.1
  72.8 1.8 collective-permute-done
  74.6 1.9 collective-permute-done.1
  77.2 1.4 pad_maximum_fusion.5
  78.6 24.6 %while.112 = (s32[]{:T(128)}, f32[1024]{0:T(1024)S(1)}, f32[1024]{0:T(1024)S(1)}, s32[]{:T(128)}, s32[512]{0:T(512)S(1)}, /*index=5*/s32[]{:T(128)}, s32[512]{0:...) while((s32[]{:T(128)}, f32[1024]{0:T(1024)S(1)}, ...), condition=%wide.region_3.4_spmd.clone, body=%wide.region_0.3_spmd.clone.sunk | while | flops 270016256 | bytes 8701639 | solution.py:120
  80.4 2.7 convolution_bitcast_fusion.8
  83.1 2.8 reshape.1419
  86.0 2.5 fusion.130
  88.4 2.5 fusion.131
  92.7 2.7 convolution_bitcast_fusion.8
  95.4 2.8 reshape.1419
  98.2 2.5 fusion.130
  100.7 2.5 fusion.131
  103.2 12.3 %while.113 = (s32[]{:T(128)}, f32[1024]{0:T(1024)S(1)}, f32[1024]{0:T(1024)S(1)}, s32[]{:T(128)}, s32[512]{0:T(512)S(1)}, /*index=5*/s32[]{:T(128)}, s32[512]{0:...) while((s32[]{:T(128)}, f32[1024]{0:T(1024)S(1)}, ...), condition=%wide.region_7.8_spmd.clone, body=%wide.region_4.7_spmd.clone.sunk | while | flops 270016256 | bytes 8701639 | solution.py:120
  105.0 2.7 convolution_bitcast_fusion.9
  107.7 2.8 reshape.1423
  110.5 2.5 fusion.134
  113.0 2.5 fusion.135
  115.5 11.2 %while.115 = (s32[]{:T(128)}, f32[1024]{0:T(1024)S(1)}, f32[1024]{0:T(1024)S(1)}, s32[]{:T(128)}, s32[512]{0:T(512)S(1)}, /*index=5*/s32[]{:T(128)}, s32[512]{0:...) while((s32[]{:T(128)}, f32[1024]{0:T(1024)S(1)}, ...), condition=%wide.region_15.16_spmd.clone, body=%wide.region_12.15_spmd.clone.sunk | while | flops 270016256 | bytes 8701639 | solution.py:120
  117.5 1.5 convolution_bitcast_fusion.11
  119.0 2.8 reshape.1431
  121.8 2.5 fusion.142
  124.2 2.5 fusion.143
  126.8 12.2 %while.114 = (s32[]{:T(128)}, f32[1024]{0:T(1024)S(1)}, f32[1024]{0:T(1024)S(1)}, s32[]{:T(128)}, s32[512]{0:T(512)S(1)}, /*index=5*/s32[]{:T(128)}, s32[512]{0:...) while((s32[]{:T(128)}, f32[1024]{0:T(1024)S(1)}, ...), condition=%wide.region_11.12_spmd.clone, body=%wide.region_8.11_spmd.clone.sunk | while | flops 270016256 | bytes 8701639 | solution.py:120
  128.5 2.7 convolution_bitcast_fusion.10
  131.2 2.8 reshape.1427
  134.1 2.5 fusion.138
  136.5 2.5 fusion.139
  139.0 22.3 %while.116 = (s32[]{:T(128)}, f32[768]{0:T(1024)S(1)}, s32[]{:T(128)}, s32[512]{0:T(512)S(1)}, s32[]{:T(128)}, /*index=5*/bf16[768,1024]{1,0:T(8,128)(2,1)S(1)},...) while((s32[]{:T(128)}, f32[768]{0:T(1024)S(1)}, ...), condition=%wide.region_20.21_spmd.clone, body=%wide.region_16.20_spmd.clone.sunk | while | flops 270409472 | bytes 7110875 | solution.py:152
  141.0 2.5 subtract_convert_fusion.8
  144.7 1.2 convert_element_type.350
  145.9 1.9 fusion.146
  148.7 1.4 scatter_fusion
  152.1 2.5 subtract_convert_fusion.8
  155.8 1.2 convert_element_type.350
  157.1 1.9 fusion.146
  159.9 1.4 scatter_fusion
  161.3 11.1 %while.117 = (s32[]{:T(128)}, f32[768]{0:T(1024)S(1)}, s32[]{:T(128)}, s32[512]{0:T(512)S(1)}, s32[]{:T(128)}, /*index=5*/bf16[768,1024]{1,0:T(8,128)(2,1)S(1)},...) while((s32[]{:T(128)}, f32[768]{0:T(1024)S(1)}, ...), condition=%wide.region_25.26_spmd.clone, body=%wide.region_21.0_spmd.clone.sunk | while | flops 270409472 | bytes 7110875 | solution.py:152
  163.3 2.5 subtract_convert_fusion.9
  167.0 1.2 convert_element_type.352
  168.2 1.9 fusion.149
  171.0 1.4 scatter_fusion.1
  172.4 11.3 %while.118 = (s32[]{:T(128)}, f32[768]{0:T(1024)S(1)}, s32[]{:T(128)}, s32[512]{0:T(512)S(1)}, s32[]{:T(128)}, /*index=5*/bf16[768,1024]{1,0:T(8,128)(2,1)S(1)},...) while((s32[]{:T(128)}, f32[768]{0:T(1024)S(1)}, ...), condition=%wide.region_30.31_spmd.clone, body=%wide.region_26.0_spmd.clone.sunk | while | flops 270409472 | bytes 7110875 | solution.py:152
  174.6 2.5 subtract_convert_fusion.10
  178.3 1.2 convert_element_type.354
  179.5 1.9 fusion.152
  182.3 1.4 scatter_fusion.2
  183.8 10.8 %while.119 = (s32[]{:T(128)}, f32[768]{0:T(1024)S(1)}, s32[]{:T(128)}, s32[512]{0:T(512)S(1)}, s32[]{:T(128)}, /*index=5*/bf16[768,1024]{1,0:T(8,128)(2,1)S(1)},...) while((s32[]{:T(128)}, f32[768]{0:T(1024)S(1)}, ...), condition=%wide.region_35.36_spmd.clone, body=%wide.region_31.35_spmd.clone.sunk | while | flops 270409472 | bytes 7110875 | solution.py:152
  185.7 2.5 subtract_convert_fusion.11
  189.4 1.2 convert_element_type.356
  190.6 1.6 fusion.155
  193.1 1.4 scatter_fusion.3
  194.7 97.1 %collective-permute-start.3 = (f32[32,8]{1,0:T(8,128)S(1)}, f32[32,8]{1,0:T(8,128)S(1)}, u32[]{:S(2)}, u32[]{:S(2)}) collective-permute-start(f32[32,8]{1,0:T(8,128)S(1)} %squeeze.143), channel_id=1, source_target_pairs={{32,0},{64,32},{96,64},{128,96},{160,128},{192,160},{224,192},{33,... | collective-permute-start | bytes 3080 | tf_op jit(solution)/shard_map/ppermute | solution.py:12
  291.8 16.7 %collective-permute-start.2 = (f32[32,8]{1,0:T(8,128)S(1)}, f32[32,8]{1,0:T(8,128)S(1)}, u32[]{:S(2)}, u32[]{:S(2)}) collective-permute-start(f32[32,8]{1,0:T(8,128)S(1)} %squeeze.142), channel_id=1, source_target_pairs={{0,32},{32,64},{64,96},{96,128},{128,160},{160,192},{192,224},{1,3... | collective-permute-start | bytes 3080 | tf_op jit(solution)/shard_map/ppermute | solution.py:12
  310.0 105.9 %all-to-all-start.1 = ((f32[3,32,8]{2,0,1:T(4,128)}), f32[3,32,8]{2,0,1:T(4,128)S(1)}, u32[]{:S(2)}, u32[]{:S(2)}) async-start(f32[3,32,8]{2,0,1:T(4,128)} %copy.53), calls=%async_computation.1 | async-start | bytes 131072 | tf_op jit(solution)/shard_map/all_to_all | solution.py:156
  416.6 9.3 %all-to-all-done.1 = f32[3,32,8]{2,0,1:T(4,128)S(1)} async-done(((f32[3,32,8]{2,0,1:T(4,128)}), f32[3,32,8]{2,0,1:T(4,128)S(1)}, u32[]{:S(2)}, u32[]{:S(2)}) %all-to-all-start.1) | async-done | bytes 3104 | tf_op jit(solution)/shard_map/all_to_all | solution.py:156
  426.0 5.9 %scatter_custom_fusion.4 = f32[1024]{0:T(1024)S(1)} fusion(s32[768]{0:T(1024)S(1)} %broadcast_maximum_fusion, f32[768]{0:T(1024)S(1)} %broadcast_select_fusion, f32[]{:T(128)} %constant.693.clone.1), kind=kCustom, calls=%fused_computation.202 | custom fusion | flops 768 | bytes 4100 | tf_op jit(solution)/shard_map/scatter-add | solution.py:158
  (159 shorter events, 38.1 us)
Async XLA Ops:
  12.0 11.6 %copy-start.5 = (s32[4]{0:T(128)S(1)}, s32[4]{0:T(128)}, u32[]{:S(2)}) copy-start(s32[4]{0:T(128)} %param.27) | copy-start | bytes 52
  12.0 50.7 %all-to-all-start = ((bf16[3,32,8,1024]{3,2,0,1:T(8,128)(2,1)}), bf16[3,32,8,1024]{3,2,0,1:T(8,128)(2,1)S(1)}, u32[]{:S(2)}, u32[]{:S(2)}) async-start(bf16[3,32,8,1024]{3,2,0,1:T(8,128)(2,1)} %copy_select_fusion), calls=%async_computation | async-start | bytes 3145728 | tf_op jit(solution)/shard_map/all_to_all | solution.py:70
  35.8 33.6 %copy-start.6 = (s32[4]{0:T(128)S(1)}, s32[4]{0:T(128)}, u32[]{:S(2)}) copy-start(s32[4]{0:T(128)} %param.31) | copy-start | bytes 52
  35.8 36.9 %copy-start.3 = (s32[4,512]{1,0:T(4,128)S(1)}, s32[4,512]{1,0:T(4,128)}, u32[]{:S(2)}) copy-start(s32[4,512]{1,0:T(4,128)} %param.29) | copy-start | bytes 24580
  35.8 37.0 %copy-start.4 = (s32[4,512]{1,0:T(4,128)S(1)}, s32[4,512]{1,0:T(4,128)}, u32[]{:S(2)}) copy-start(s32[4,512]{1,0:T(4,128)} %param.30) | copy-start | bytes 24580
  63.9 10.7 %collective-permute-start = (bf16[32,8,1024]{2,1,0:T(8,128)(2,1)}, bf16[32,8,1024]{2,1,0:T(8,128)(2,1)S(1)}, u32[]{:S(2)}, u32[]{:S(2)}) collective-permute-start(bf16[32,8,1024]{2,1,0:T(8,128)(2,1)} %get-tuple-element.1624), channel_id=1, source_target_pairs={{0,32},{32,64},{64,96},{96,128},{128,160},{160,192},{192,224},{1,3... | collective-permute-start | bytes 1572872 | tf_op jit(solution)/shard_map/ppermute | solution.py:12
  65.8 10.6 %collective-permute-start.1 = (bf16[32,8,1024]{2,1,0:T(8,128)(2,1)}, bf16[32,8,1024]{2,1,0:T(8,128)(2,1)S(1)}, u32[]{:S(2)}, u32[]{:S(2)}) collective-permute-start(bf16[32,8,1024]{2,1,0:T(8,128)(2,1)} %get-tuple-element.1625), channel_id=1, source_target_pairs={{32,0},{64,32},{96,64},{128,96},{160,128},{192,160},{224,192},{33,... | collective-permute-start | bytes 1572872 | tf_op jit(solution)/shard_map/ppermute | solution.py:12
  74.6 1.9 copy-start
  76.4 0.8 copy-start.1
  183.8 242.2 %copy-start.2 = (s32[768]{0:T(1024)S(1)}, s32[768]{0:T(1024)}, u32[]{:S(2)}) copy-start(s32[768]{0:T(1024)} %param.28) | copy-start | bytes 9220
  194.7 113.9 %collective-permute-start.3 = (f32[32,8]{1,0:T(8,128)S(1)}, f32[32,8]{1,0:T(8,128)S(1)}, u32[]{:S(2)}, u32[]{:S(2)}) collective-permute-start(f32[32,8]{1,0:T(8,128)S(1)} %squeeze.143), channel_id=1, source_target_pairs={{32,0},{64,32},{96,64},{128,96},{160,128},{192,160},{224,192},{33,... | collective-permute-start | bytes 3080 | tf_op jit(solution)/shard_map/ppermute | solution.py:12
  291.8 17.5 %collective-permute-start.2 = (f32[32,8]{1,0:T(8,128)S(1)}, f32[32,8]{1,0:T(8,128)S(1)}, u32[]{:S(2)}, u32[]{:S(2)}) collective-permute-start(f32[32,8]{1,0:T(8,128)S(1)} %squeeze.142), channel_id=1, source_target_pairs={{0,32},{32,64},{64,96},{96,128},{128,160},{160,192},{192,224},{1,3... | collective-permute-start | bytes 3080 | tf_op jit(solution)/shard_map/ppermute | solution.py:12
  310.0 115.9 %all-to-all-start.1 = ((f32[3,32,8]{2,0,1:T(4,128)}), f32[3,32,8]{2,0,1:T(4,128)S(1)}, u32[]{:S(2)}, u32[]{:S(2)}) async-start(f32[3,32,8]{2,0,1:T(4,128)} %copy.53), calls=%async_computation.1 | async-start | bytes 131072 | tf_op jit(solution)/shard_map/all_to_all | solution.py:156
where the time goes:
time: 436 us; the launch traced here: 433 us
  starting transfers between devices  237 us (54%)
  local copies, waits for them, and re-layouts  65.5 us (15%)
  other arithmetic  55.9 us (13%)
  waiting for transfers between devices  40.6 us (9%)
  matrix products  21.4 us (5%)
  between operations  11.2 us (3%)
    ppermute x4, starting transfers between devices, from_behind_2(): return lax.ppermute(block, axis, route)  119 us
    all_to_all x1, starting transfers between devices, on_device(): lax.all_to_all(returned, 'tile', split_axis=1, concat_axis=1, tiled=True)  106 us
    all_to_all x1, waiting for transfers between devices, on_device(): lax.all_to_all(outgoing, 'tile', split_axis=1, concat_axis=1, tiled=True)  26.9 us
    another operation x6, other arithmetic  14.6 us
    reshape x5, local copies, waits for them, and re-layouts, forward_step(): paired = product.reshape(pixels, BLK, 2)  14.1 us
    dot_general x5, matrix products, forward_step(): lax.dot_general(weight, rows, (((1,), (1,)), ((), ())), preferred_element...  12.3 us
    slice x5, local copies, waits for them, and re-layouts, forward_step(): imag_proj = paired[:, :, 1]  12.3 us
    reduce_sum x5, other arithmetic, forward_step(): jnp.sum((sin_grid * real_proj + cos_grid * imag_proj) * active[None, :],...  12.3 us
  transfers between devices with their start and end apart: 6, of which 5 were waited for; matrix products, arithmetic and copies ran while one was open for 1% of the time, Pallas kernels for 0%

commit v1 on v0

v1 whole, which is shorter than its diff:
```python
import jax
import jax.numpy as jnp
from jax import lax
from jax.experimental import pallas as pl
from jax.experimental.pallas import tpu as pltpu
from jax.sharding import PartitionSpec as P

LANES = 128
HALF = 128
VMEM_BYTES = 56 * 1024 * 1024


def shift_along(block, axis, distance):
    devices = range(lax.axis_size(axis))
    route = [(i - distance, i) for i in devices if i - distance in devices]
    return lax.ppermute(block, axis, route)


def whole(shape):
    return pl.BlockSpec(shape, lambda *_: (0,) * len(shape))


def column(row):
    return jnp.broadcast_to(row, (8, row.shape[1])).T[:, :1]


def gather_kernel(panels_ref, phases_ref, slots_ref, out_ref):
    rows_here, width = panels_ref.shape
    bins = width // 2
    pings = phases_ref.shape[1]
    count = out_ref.shape[0]
    slot_row = column(slots_ref[0].astype(jnp.float32)).astype(jnp.int32)
    row_ids = lax.broadcasted_iota(jnp.int32, (count, rows_here), 1)
    pick = jnp.where(row_ids == slot_row, 1.0, 0.0).astype(jnp.bfloat16)
    picked = jnp.dot(pick, panels_ref[...], preferred_element_type=jnp.float32)
    phases = phases_ref[...]
    ping_ids = lax.broadcasted_iota(jnp.int32, (count, pings), 1)
    owned = ping_ids == (slot_row // (rows_here // pings))
    cos_col = jnp.sum(jnp.where(owned, jnp.cos(phases), 0.0), axis=1, keepdims=True)
    sin_col = jnp.sum(jnp.where(owned, jnp.sin(phases), 0.0), axis=1, keepdims=True)
    real_part = picked[:, :bins]
    imag_part = picked[:, bins:]
    out_ref[:, :bins] = (cos_col * real_part - sin_col * imag_part).astype(jnp.bfloat16)
    out_ref[:, bins:] = (sin_col * real_part + cos_col * imag_part).astype(jnp.bfloat16)


def gather_rotated(panels, phases, slots, steps):
    total = slots.shape[0]
    count = total // steps
    return pl.pallas_call(
        gather_kernel,
        grid=(steps,),
        in_specs=[
            whole(panels.shape),
            whole((1, phases.shape[0])),
            pl.BlockSpec((1, 1, count), lambda i: (i, 0, 0)),
        ],
        out_specs=pl.BlockSpec((count, panels.shape[1]), lambda i: (i, 0)),
        out_shape=jax.ShapeDtypeStruct((total, panels.shape[1]), jnp.bfloat16),
        compiler_params=pltpu.CompilerParams(vmem_limit_bytes=VMEM_BYTES),
        name="gather_rotated",
    )(panels, phases.reshape(1, -1), slots.reshape(steps, 1, count))


def make_table_kernel(ping_total, tile_total, track_groups, pixels, tiles_here, slots):
    def table_kernel(base_ref, counts_ref, slot_ref, ping_ref, base_cos, base_sin, step_cos, step_sin):
        tile = pl.program_id(0)
        foot = slot_ref.shape[2]
        count = counts_ref[tile]
        tile_global = base_ref[0] + tile
        slot_ids = lax.broadcasted_iota(jnp.int32, (slots, foot), 0)
        match = jnp.where(slot_ids == slot_ref[0], 1.0, 0.0).astype(jnp.bfloat16)
        pings = ping_ref[0]
        used = jnp.where(lax.broadcasted_iota(jnp.int32, (1, foot), 1) < count, 1.0, 0.0)
        values = jnp.concatenate(
            [
                (pings // HALF).astype(jnp.float32) * used,
                (pings % HALF).astype(jnp.float32) * used,
                used,
                jnp.zeros((5, foot), jnp.float32),
            ],
            axis=0,
        ).astype(jnp.bfloat16)
        found = lax.dot_general(
            match, values, (((1,), (1,)), ((), ())), preferred_element_type=jnp.float32
        )
        ping = (found[:, 0:1] * HALF + found[:, 1:2]).astype(jnp.int32)
        mask = found[:, 2:3]
        offset = (2 * ping + 1) * tile_total - (2 * tile_global + 1) * ping_total
        along = offset.astype(jnp.float32) * (track_groups / (2.0 * ping_total * tile_total))
        lane = lax.broadcasted_iota(jnp.int32, (1, LANES), 1).astype(jnp.float32)
        across = (lane + 0.5) / pixels - 0.5
        angle = 96.0 * across * along + 8.0 * (along * along)
        base_cos[0] = jnp.cos(angle) * mask
        base_sin[0] = jnp.sin(angle) * mask
        step = jnp.broadcast_to((96.0 * LANES / pixels) * along, (slots, 8))
        step_cos[0] = jnp.broadcast_to(jnp.cos(step)[:, :1], (slots, LANES))
        step_sin[0] = jnp.broadcast_to(jnp.sin(step)[:, :1], (slots, LANES))

    return table_kernel


def phase_tables(base, counts, foot_slot, foot_ping, slots, ping_total, tile_total, track_groups, pixels):
    tiles_here, foot = foot_slot.shape
    kernel = make_table_kernel(ping_total, tile_total, track_groups, pixels, tiles_here, slots)
    table = jax.ShapeDtypeStruct((tiles_here, slots, LANES), jnp.float32)
    return pl.pallas_call(
        kernel,
        grid_spec=pltpu.PrefetchScalarGridSpec(
            num_scalar_prefetch=2,
            grid=(tiles_here,),
            in_specs=[pl.BlockSpec((1, 1, foot), lambda t, *_: (t, 0, 0))] * 2,
            out_specs=[pl.BlockSpec((1, slots, LANES), lambda t, *_: (t, 0, 0))] * 4,
        ),
        out_shape=[table] * 4,
        compiler_params=pltpu.CompilerParams(vmem_limit_bytes=VMEM_BYTES),
        name="phase_tables",
    )(base, counts, foot_slot.reshape(tiles_here, 1, foot), foot_ping.reshape(tiles_here, 1, foot))


def make_focus_kernel(slots, pixels, bins, chunk):
    blocks = pixels // LANES

    def focus_kernel(
        class_ref, rows_ref, weight_ref, base_cos, base_sin, step_cos, step_sin,
        image_ref, corr_ref, proj_r, proj_i, turned_r, turned_i, corr_acc,
    ):
        tile = pl.program_id(0)
        weight = weight_ref[0]
        sums = None
        for start in range(0, slots, chunk):
            half = (start // chunk) % 2
            rows = rows_ref[pl.ds(start, chunk), :]
            dims = (((1,), (1,)), ((), ()))
            proj_r[half] = lax.dot_general(rows[:, :bins], weight, dims, preferred_element_type=jnp.float32)
            proj_i[half] = lax.dot_general(rows[:, bins:], weight, dims, preferred_element_type=jnp.float32)

            def group(i, carry, start=start, half=half):
                at = pl.multiple_of(start + i * 8, 8)
                local = pl.multiple_of(i * 8, 8)
                cos_now = base_cos[0, pl.ds(at, 8), :]
                sin_now = base_sin[0, pl.ds(at, 8), :]
                turn_c = step_cos[0, pl.ds(at, 8), :]
                turn_s = step_sin[0, pl.ds(at, 8), :]
                out = []
                for b in range(blocks):
                    lanes = pl.ds(b * LANES, LANES)
                    real = proj_r[half, pl.ds(local, 8), lanes]
                    imag = proj_i[half, pl.ds(local, 8), lanes]
                    new_r = cos_now * real - sin_now * imag
                    new_i = sin_now * real + cos_now * imag
                    turned_r[pl.ds(at, 8), lanes] = new_r
                    turned_i[pl.ds(at, 8), lanes] = new_i
                    out.append(carry[2 * b] + new_r)
                    out.append(carry[2 * b + 1] + new_i)
                    if b + 1 < blocks:
                        cos_now, sin_now = (
                            cos_now * turn_c - sin_now * turn_s,
                            sin_now * turn_c + cos_now * turn_s,
                        )
                return tuple(out)

            if sums is None:
                sums = (jnp.zeros((8, LANES), jnp.float32),) * (2 * blocks)
            sums = lax.fori_loop(0, chunk // 8, group, sums, unroll=2)
        heavy = []
        for b in range(blocks):
            lanes = pl.ds(b * LANES, LANES)
            real = jnp.sum(sums[2 * b], axis=0, keepdims=True)
            imag = jnp.sum(sums[2 * b + 1], axis=0, keepdims=True)
            image_ref[0, 0:1, lanes] = real
            image_ref[0, 1:2, lanes] = imag
            intensity = real * real + imag * imag
            heavy.append(jnp.broadcast_to(intensity * real, (8, LANES)))
            heavy.append(jnp.broadcast_to(intensity * imag, (8, LANES)))

        @pl.when(tile == 0)
        def _():
            corr_acc[...] = jnp.zeros_like(corr_acc)

        def pull(i, _):
            at = pl.multiple_of(i * 8, 8)
            total = corr_acc[pl.ds(at, 8), :]
            for b in range(blocks):
                lanes = pl.ds(b * LANES, LANES)
                total = total + (
                    turned_r[pl.ds(at, 8), lanes] * heavy[2 * b + 1]
                    - turned_i[pl.ds(at, 8), lanes] * heavy[2 * b]
                )
            corr_acc[pl.ds(at, 8), :] = total
            return 0

        lax.fori_loop(0, slots // 8, pull, 0, unroll=2)

        @pl.when(tile == pl.num_programs(0) - 1)
        def _():
            for part in range(slots // LANES):
                block = corr_acc[pl.ds(part * LANES, LANES), :]
                corr_ref[pl.ds(part, 1), :] = jnp.sum(block.T, axis=0, keepdims=True)

    return focus_kernel


def focus(tile_class, received, weight_tiles, tables, chunk):
    slots, width = received.shape
    _, pixels, bins = weight_tiles.shape
    tiles_here = tile_class.shape[0]
    parts = slots // LANES
    table_spec = pl.BlockSpec((1, slots, LANES), lambda t, *_: (t, 0, 0))
    image, corr = pl.pallas_call(
        make_focus_kernel(slots, pixels, bins, chunk),
        grid_spec=pltpu.PrefetchScalarGridSpec(
            num_scalar_prefetch=1,
            grid=(tiles_here,),
            in_specs=[
                whole((slots, width)),
                pl.BlockSpec((1, pixels, bins), lambda t, cls: (cls[t], 0, 0)),
            ]
            + [table_spec] * 4,
            out_specs=[
                pl.BlockSpec((1, 2, pixels), lambda t, *_: (t, 0, 0)),
                whole((parts, LANES)),
            ],
            scratch_shapes=[
                pltpu.VMEM((2, chunk, pixels), jnp.float32),
                pltpu.VMEM((2, chunk, pixels), jnp.float32),
                pltpu.VMEM((slots, pixels), jnp.float32),
                pltpu.VMEM((slots, pixels), jnp.float32),
                pltpu.VMEM((slots, LANES), jnp.float32),
            ],
        ),
        out_shape=[
            jax.ShapeDtypeStruct((tiles_here, 2, pixels), jnp.float32),
            jax.ShapeDtypeStruct((parts, LANES), jnp.float32),
        ],
        compiler_params=pltpu.CompilerParams(
            dimension_semantics=("arbitrary",), vmem_limit_bytes=VMEM_BYTES
        ),
        name="focus",
    )(tile_class, received, weight_tiles, *tables)
    return image, corr.reshape(slots)


def on_device(
    panels, phases, weight_tiles, tile_class, send_slots, foot_slot, foot_ping, tile_counts
):
    track_devs = lax.axis_size("track")
    tile_devs = lax.axis_size("tile")
    device = lax.axis_index("track") * tile_devs + lax.axis_index("tile")
    ping_local = phases.shape[0]
    row_width = panels.shape[1]
    tiles_here = tile_counts.shape[0]
    pixels = weight_tiles.shape[1]
    slots = send_slots.shape[0]
    slot_cap = slots // 3 // tile_devs
    ping_total = ping_local * track_devs * tile_devs
    tile_total = tiles_here * track_devs * tile_devs

    outgoing = gather_rotated(panels, phases, send_slots, 3)
    outgoing = outgoing.reshape(3, tile_devs, slot_cap, row_width)
    behind = shift_along(outgoing[2], "track", 1)
    ahead = shift_along(outgoing[0], "track", -1)
    mixed = jnp.concatenate([behind, outgoing[1], ahead], axis=1)
    arrived = lax.all_to_all(mixed, "tile", split_axis=0, concat_axis=0, tiled=True)
    tables = phase_tables(
        (device * tiles_here).astype(jnp.int32).reshape(1),
        tile_counts, foot_slot, foot_ping, slots,
        ping_total, tile_total, track_devs, pixels,
    )
    received = arrived.reshape(tile_devs, 3, slot_cap, row_width).transpose(1, 0, 2, 3)
    image, corr = focus(tile_class, received.reshape(slots, row_width), weight_tiles, tables, 128)

    partial = corr.reshape(3, tile_devs, slot_cap)
    behind = shift_along(partial[2], "track", 1)
    ahead = shift_along(partial[0], "track", -1)
    back = jnp.concatenate([behind, partial[1], ahead], axis=1)
    back = lax.all_to_all(back, "tile", split_axis=0, concat_axis=0, tiled=True)
    back = back.reshape(tile_devs, 3, slot_cap).transpose(1, 0, 2).reshape(1, slots)
    owner = (send_slots // (panels.shape[0] // ping_local)).reshape(1, slots)
    own = lax.broadcasted_iota(jnp.int32, (ping_local, slots), 0) == owner
    ping_gradient = jnp.sum(jnp.where(own & (send_slots >= 0)[None, :], back, 0.0), axis=1)
    return (image, ping_gradient)


def solution(mesh):
    spread = P(("track", "tile"))
    in_specs = (
        P(("track", "tile"), None), spread, P(), spread, spread,
        P(("track", "tile"), None), P(("track", "tile"), None), spread,
    )
    out_specs = (P(("track", "tile"), None, None), spread)
    return jax.shard_map(
        on_device, mesh=mesh, in_specs=in_specs, out_specs=out_specs, check_vma=False
    )
```

time: 436 us -> 136 us (0.31)
  the two profiles are of different devices: /device:TPU:6 before, /device:TPU:1 now
where the time goes in v1:
time: 136 us; the launch traced here: 135 us
  Pallas kernels  54.6 us (40%)
  waiting for transfers between devices  37 us (27%)
  starting transfers between devices  33.7 us (25%)
  local copies, waits for them, and re-layouts  6.56 us (5%)
  other arithmetic  2.61 us (2%)
    pallas_call x1, Pallas kernels, focus(): pl.pallas_call(make_focus_kernel(slots, pixels, bins, chunk), grid_spec=p...  34 us
    all_to_all x1, waiting for transfers between devices, on_device(): lax.all_to_all(mixed, 'tile', split_axis=0, concat_axis=0, tiled=True)  17 us
    ppermute x4, starting transfers between devices, shift_along(): return lax.ppermute(block, axis, route)  16.8 us
    pallas_call x1, Pallas kernels, phase_tables(): pl.pallas_call(kernel, grid_spec=pltpu.PrefetchScalarGridSpec(num_scalar_...  15.2 us
    ppermute x4, waiting for transfers between devices, shift_along(): return lax.ppermute(block, axis, route)  11.6 us
    all_to_all x1, starting transfers between devices, on_device(): lax.all_to_all(mixed, 'tile', split_axis=0, concat_axis=0, tiled=True)  11.3 us
    all_to_all x1, waiting for transfers between devices, on_device(): back = lax.all_to_all(back, 'tile', split_axis=0, concat_axis=0, tiled=True)  8.42 us
    all_to_all x1, starting transfers between devices, on_device(): back = lax.all_to_all(back, 'tile', split_axis=0, concat_axis=0, tiled=True)  5.53 us
  transfers between devices with their start and end apart: 6, of which 5 were waited for; matrix products, arithmetic and copies ran while one was open for 1% of the time, Pallas kernels for 11%

profile of v1, /device:TPU:1, one launch (start us, length us, event | category | flops | bytes accessed | tf_op | source)
XLA Modules:
  0.0 135.2 jit_solution(15909557681718775594)
XLA Ops:
  0.6 1.3 reshape.50.slots_ref
  1.9 5.4 %gather_rotated.1 = bf16[768,1024]{1,0:T(8,128)(2,1)} custom-call(bf16[1024,1024]{1,0:T(8,128)(2,1)} %panels_ref.1, f32[1,64]{1,0:T(1,128)} %bitcast.21, s32[3,1,256]{2,1,0:T(1,128)} %reshape.50.slots_ref), custom_call_target="tpu_custom_call" | custom-call | tf_op jit(solution)/shard_map/gather_rotated/pallas_call | solution.py:50
  7.3 1.5 %slice_bitcast_fusion.2 = (bf16[32,8,1024]{2,1,0:T(8,128)(2,1)S(1)}, bf16[32,8,1024]{2,1,0:T(8,128)(2,1)S(1)}, bf16[32,8,1024]{2,1,0:T(8,128)(2,1)S(1)}) fusion(bf16[768,1024]{1,0:T(8,128)(2,1)} %gather_rotated.1), kind=kLoop, calls=%fused_computation.3 | loop fusion | bytes 3145728 | tf_op jit(solution)/shard_map/squeeze | solution.py:261
  8.8 4.5 %collective-permute-start = (bf16[32,8,1024]{2,1,0:T(8,128)(2,1)S(1)}, bf16[32,8,1024]{2,1,0:T(8,128)(2,1)S(1)}, u32[]{:S(2)}, u32[]{:S(2)}) collective-permute-start(bf16[32,8,1024]{2,1,0:T(8,128)(2,1)S(1)} %get-tuple-element.14), channel_id=1, source_target_pairs={{0,32},{32,64},{64,96},{96,128},{128,160},{160,192},{192,224},{1,3... | collective-permute-start | bytes 1572872 | tf_op jit(solution)/shard_map/ppermute | solution.py:16
  13.3 1.9 %collective-permute-start.1 = (bf16[32,8,1024]{2,1,0:T(8,128)(2,1)S(1)}, bf16[32,8,1024]{2,1,0:T(8,128)(2,1)S(1)}, u32[]{:S(2)}, u32[]{:S(2)}) collective-permute-start(bf16[32,8,1024]{2,1,0:T(8,128)(2,1)S(1)} %get-tuple-element.15), channel_id=1, source_target_pairs={{32,0},{64,32},{96,64},{128,96},{160,128},{192,160},{224,192},{33,... | collective-permute-start | bytes 1572872 | tf_op jit(solution)/shard_map/ppermute | solution.py:16
  15.3 4.1 %collective-permute-done = bf16[32,8,1024]{2,1,0:T(8,128)(2,1)S(1)} collective-permute-done((bf16[32,8,1024]{2,1,0:T(8,128)(2,1)S(1)}, bf16[32,8,1024]{2,1,0:T(8,128)(2,1)S(1)}, u32[]{:S(2)}, u32[]{:S(2)}) %collective-permute-start) | collective-permute-done | bytes 524320 | tf_op jit(solution)/shard_map/ppermute | solution.py:16
  19.4 4.4 %collective-permute-done.1 = bf16[32,8,1024]{2,1,0:T(8,128)(2,1)S(1)} collective-permute-done((bf16[32,8,1024]{2,1,0:T(8,128)(2,1)S(1)}, bf16[32,8,1024]{2,1,0:T(8,128)(2,1)S(1)}, u32[]{:S(2)}, u32[]{:S(2)}) %collective-permute-start.1) | collective-permute-done | bytes 524320 | tf_op jit(solution)/shard_map/ppermute | solution.py:16
  23.8 1.3 pad_maximum_fusion
  25.1 0.0 copy-start.1
  25.1 0.0 copy-start.2
  25.1 11.3 %all-to-all-start = ((bf16[32,24,1024]{2,1,0:T(8,128)(2,1)}), bf16[32,24,1024]{2,1,0:T(8,128)(2,1)S(1)}, u32[]{:S(2)}, u32[]{:S(2)}) async-start(bf16[32,24,1024]{2,1,0:T(8,128)(2,1)} %pad_maximum_fusion), calls=%async_computation | async-start | bytes 3145728 | tf_op jit(solution)/shard_map/all_to_all | solution.py:264
  36.4 0.0 copy-done.1
  36.4 0.6 reshape.54.slot_ref
  37.1 0.0 copy-done.2
  37.1 0.6 reshape.55.ping_ref
  37.7 15.2 %phase_tables.1 = (f32[4,768,128]{2,1,0:T(8,128)}, f32[4,768,128]{2,1,0:T(8,128)}, f32[4,768,128]{2,1,0:T(8,128)}, f32[4,768,128]{2,1,0:T(8,128)}) custom-call(s32[1]{0:T(128)} %bitcast.7.base_ref, s32[4]{0:T(128)} %counts_ref.1, s32[4,1,512]{2,1,0:T(1,128)} %reshape.54.slot_ref, s32[4,1,512]{2,1,0:T(1,128)} %reshape.55.ping_ref), custom_call_target="tpu_custom_call" | custom-call | tf_op jit(solution)/shard_map/phase_tables/pallas_call | solution.py:107
  52.9 17.0 %all-to-all-done = bf16[32,24,1024]{2,1,0:T(8,128)(2,1)S(1)} async-done(((bf16[32,24,1024]{2,1,0:T(8,128)(2,1)}), bf16[32,24,1024]{2,1,0:T(8,128)(2,1)S(1)}, u32[]{:S(2)}, u32[]{:S(2)}) %all-to-all-start) | async-done | bytes 1572896 | tf_op jit(solution)/shard_map/all_to_all | solution.py:264
  69.9 1.3 copy.17
  71.2 0.0 copy-start
  71.2 34.0 %focus.1 = (f32[4,2,1024]{2,1,0:T(2,128)}, f32[6,128]{1,0:T(8,128)}) custom-call(s32[4]{0:T(128)} %class_ref.1, bf16[768,1024]{1,0:T(8,128)(2,1)} %bitcast.19, bf16[4,1024,512]{2,1,0:T(8,128)(2,1)} %weight_ref.1, f32[4,768,128]{2,1,0:T(8,128)} %get-tuple-element.8.base_cos, f32[4,768,128]{2,1,0:T(8,128)} %get-tuple-element.9.base_sin, ...), custom_call_target="tpu_custom_call" | custom-call | tf_op jit(solution)/shard_map/focus/pallas_call | solution.py:210
  105.2 0.8 fusion.3
  106.0 0.1 squeeze.21
  106.1 8.4 %collective-permute-start.2 = (f32[32,8]{1,0:T(8,128)S(1)}, f32[32,8]{1,0:T(8,128)S(1)}, u32[]{:S(2)}, u32[]{:S(2)}) collective-permute-start(f32[32,8]{1,0:T(8,128)S(1)} %squeeze.21), channel_id=1, source_target_pairs={{0,32},{32,64},{64,96},{96,128},{128,160},{160,192},{192,224},{1,3... | collective-permute-start | bytes 3080 | tf_op jit(solution)/shard_map/ppermute | solution.py:16
  114.5 0.1 squeeze.23
  114.6 1.9 %collective-permute-start.3 = (f32[32,8]{1,0:T(8,128)S(1)}, f32[32,8]{1,0:T(8,128)S(1)}, u32[]{:S(2)}, u32[]{:S(2)}) collective-permute-start(f32[32,8]{1,0:T(8,128)S(1)} %squeeze.23), channel_id=1, source_target_pairs={{32,0},{64,32},{96,64},{128,96},{160,128},{192,160},{224,192},{33,... | collective-permute-start | bytes 3080 | tf_op jit(solution)/shard_map/ppermute | solution.py:16
  116.5 0.0 copy-done
  116.5 0.1 squeeze.22
  116.6 0.0 collective-permute-done.2
  116.6 3.0 %collective-permute-done.3 = f32[32,8]{1,0:T(8,128)S(1)} collective-permute-done((f32[32,8]{1,0:T(8,128)S(1)}, f32[32,8]{1,0:T(8,128)S(1)}, u32[]{:S(2)}, u32[]{:S(2)}) %collective-permute-start.3) | collective-permute-done | bytes 1056 | tf_op jit(solution)/shard_map/ppermute | solution.py:16
  119.6 0.7 pad_maximum_fusion.1
  120.3 5.5 %all-to-all-start.1 = ((f32[32,1,24]{2,1,0:T(1,128)}), f32[32,1,24]{2,1,0:T(1,128)S(1)}, u32[]{:S(2)}, u32[]{:S(2)}) async-start(f32[32,1,24]{2,1,0:T(1,128)} %bitcast.9), calls=%async_computation.1 | async-start | bytes 32768 | tf_op jit(solution)/shard_map/all_to_all | solution.py:277
  125.9 8.4 %all-to-all-done.1 = f32[32,1,24]{2,1,0:T(1,128)S(1)} async-done(((f32[32,1,24]{2,1,0:T(1,128)}), f32[32,1,24]{2,1,0:T(1,128)S(1)}, u32[]{:S(2)}, u32[]{:S(2)}) %all-to-all-start.1) | async-done | bytes 3104 | tf_op jit(solution)/shard_map/all_to_all | solution.py:277
  134.3 0.1 copy.19
  134.3 0.1 copy.20
  134.4 0.1 broadcast_in_dim.15
  134.5 0.7 select_reduce_fusion
  (2 shorter events, 0.0 us)
Async XLA Ops:
  8.8 10.6 %collective-permute-start = (bf16[32,8,1024]{2,1,0:T(8,128)(2,1)S(1)}, bf16[32,8,1024]{2,1,0:T(8,128)(2,1)S(1)}, u32[]{:S(2)}, u32[]{:S(2)}) collective-permute-start(bf16[32,8,1024]{2,1,0:T(8,128)(2,1)S(1)} %get-tuple-element.14), channel_id=1, source_target_pairs={{0,32},{32,64},{64,96},{96,128},{128,160},{160,192},{192,224},{1,3... | collective-permute-start | bytes 1572872 | tf_op jit(solution)/shard_map/ppermute | solution.py:16
  13.3 10.5 %collective-permute-start.1 = (bf16[32,8,1024]{2,1,0:T(8,128)(2,1)S(1)}, bf16[32,8,1024]{2,1,0:T(8,128)(2,1)S(1)}, u32[]{:S(2)}, u32[]{:S(2)}) collective-permute-start(bf16[32,8,1024]{2,1,0:T(8,128)(2,1)S(1)} %get-tuple-element.15), channel_id=1, source_target_pairs={{32,0},{64,32},{96,64},{128,96},{160,128},{192,160},{224,192},{33,... | collective-permute-start | bytes 1572872 | tf_op jit(solution)/shard_map/ppermute | solution.py:16
  25.1 11.3 %copy-start.1 = (s32[4,512]{1,0:T(4,128)S(1)}, s32[4,512]{1,0:T(4,128)}, u32[]{:S(2)}) copy-start(s32[4,512]{1,0:T(4,128)} %param.13) | copy-start | bytes 24580
  25.1 12.0 %copy-start.2 = (s32[4,512]{1,0:T(4,128)S(1)}, s32[4,512]{1,0:T(4,128)}, u32[]{:S(2)}) copy-start(s32[4,512]{1,0:T(4,128)} %param.14) | copy-start | bytes 24580
  25.1 44.8 %all-to-all-start = ((bf16[32,24,1024]{2,1,0:T(8,128)(2,1)}), bf16[32,24,1024]{2,1,0:T(8,128)(2,1)S(1)}, u32[]{:S(2)}, u32[]{:S(2)}) async-start(bf16[32,24,1024]{2,1,0:T(8,128)(2,1)} %pad_maximum_fusion), calls=%async_computation | async-start | bytes 3145728 | tf_op jit(solution)/shard_map/all_to_all | solution.py:264
  71.2 45.3 %copy-start = (s32[768]{0:T(1024)S(1)}, s32[768]{0:T(1024)}, u32[]{:S(2)}) copy-start(s32[768]{0:T(1024)} %param.12) | copy-start | bytes 9220
  106.1 10.5 %collective-permute-start.2 = (f32[32,8]{1,0:T(8,128)S(1)}, f32[32,8]{1,0:T(8,128)S(1)}, u32[]{:S(2)}, u32[]{:S(2)}) collective-permute-start(f32[32,8]{1,0:T(8,128)S(1)} %squeeze.21), channel_id=1, source_target_pairs={{0,32},{32,64},{64,96},{96,128},{128,160},{160,192},{192,224},{1,3... | collective-permute-start | bytes 3080 | tf_op jit(solution)/shard_map/ppermute | solution.py:16
  114.6 5.1 %collective-permute-start.3 = (f32[32,8]{1,0:T(8,128)S(1)}, f32[32,8]{1,0:T(8,128)S(1)}, u32[]{:S(2)}, u32[]{:S(2)}) collective-permute-start(f32[32,8]{1,0:T(8,128)S(1)} %squeeze.23), channel_id=1, source_target_pairs={{32,0},{64,32},{96,64},{128,96},{160,128},{192,160},{224,192},{33,... | collective-permute-start | bytes 3080 | tf_op jit(solution)/shard_map/ppermute | solution.py:16
  120.3 14.0 %all-to-all-start.1 = ((f32[32,1,24]{2,1,0:T(1,128)}), f32[32,1,24]{2,1,0:T(1,128)S(1)}, u32[]{:S(2)}, u32[]{:S(2)}) async-start(f32[32,1,24]{2,1,0:T(1,128)} %bitcast.9), calls=%async_computation.1 | async-start | bytes 32768 | tf_op jit(solution)/shard_map/all_to_all | solution.py:277

commit v2 on v1

v2 whole, which is shorter than its diff:
```python
import jax
import jax.numpy as jnp
from jax import lax
from jax.experimental import pallas as pl
from jax.experimental.pallas import tpu as pltpu
from jax.sharding import PartitionSpec as P

LANES = 128
HALF = 128
VMEM_BYTES = 24 * 1024 * 1024


def shift_along(block, axis, distance):
    devices = range(lax.axis_size(axis))
    route = [(i - distance, i) for i in devices if i - distance in devices]
    return lax.ppermute(block, axis, route)


def whole(shape):
    return pl.BlockSpec(shape, lambda *_: (0,) * len(shape))


def column(row):
    return jnp.broadcast_to(row, (8, row.shape[1])).T[:, :1]


def rotated_rows(panels_ref, phases_ref, slots):
    rows_here, width = panels_ref.shape
    bins = width // 2
    pings = phases_ref.shape[1]
    count = slots.shape[1]
    slot_row = column(slots.astype(jnp.float32)).astype(jnp.int32)
    row_ids = lax.broadcasted_iota(jnp.int32, (count, rows_here), 1)
    pick = jnp.where(row_ids == slot_row, 1.0, 0.0).astype(jnp.bfloat16)
    picked = jnp.dot(pick, panels_ref[...], preferred_element_type=jnp.float32)
    phases = phases_ref[...]
    ping_ids = lax.broadcasted_iota(jnp.int32, (count, pings), 1)
    owned = ping_ids == (slot_row // (rows_here // pings))
    cos_col = jnp.sum(jnp.where(owned, jnp.cos(phases), 0.0), axis=1, keepdims=True)
    sin_col = jnp.sum(jnp.where(owned, jnp.sin(phases), 0.0), axis=1, keepdims=True)
    real_part = picked[:, :bins]
    imag_part = picked[:, bins:]
    return (
        (cos_col * real_part - sin_col * imag_part).astype(jnp.bfloat16),
        (sin_col * real_part + cos_col * imag_part).astype(jnp.bfloat16),
    )


def gather_rotated(panels, phases, slots, offsets):
    count = slots.shape[0] // 3
    width = panels.shape[1]
    bins = width // 2

    def kernel(panels_ref, phases_ref, slots_ref, *outs):
        for offset, out in zip(offsets, outs):
            real_part, imag_part = rotated_rows(
                panels_ref, phases_ref, slots_ref[:, pl.ds(offset * count, count)]
            )
            out[:, :bins] = real_part
            out[:, bins:] = imag_part

    return pl.pallas_call(
        kernel,
        out_shape=[jax.ShapeDtypeStruct((count, width), jnp.bfloat16) for _ in offsets],
        compiler_params=pltpu.CompilerParams(vmem_limit_bytes=VMEM_BYTES),
        name="gather_rotated",
    )(panels, phases.reshape(1, -1), slots.reshape(1, -1))


def make_table_kernel(ping_total, tile_total, track_groups, pixels, tile_devs, slots):
    def table_kernel(base_ref, counts_ref, slot_ref, ping_ref, base_cos, base_sin, step_cos, step_sin):
        tile = pl.program_id(0)
        foot = slot_ref.shape[2]
        count = counts_ref[tile]
        tile_global = base_ref[0] + tile
        slot_ids = lax.broadcasted_iota(jnp.int32, (slots, foot), 0)
        listed = slot_ref[0]
        group = slots // 3
        cap = group // tile_devs
        source = (listed % group) // cap
        placed = (source * 3 + listed // group) * cap + listed % cap
        match = jnp.where(slot_ids == placed, 1.0, 0.0).astype(jnp.bfloat16)
        pings = ping_ref[0]
        used = jnp.where(lax.broadcasted_iota(jnp.int32, (1, foot), 1) < count, 1.0, 0.0)
        values = jnp.concatenate(
            [
                (pings // HALF).astype(jnp.float32) * used,
                (pings % HALF).astype(jnp.float32) * used,
                used,
                jnp.zeros((5, foot), jnp.float32),
            ],
            axis=0,
        ).astype(jnp.bfloat16)
        found = lax.dot_general(
            match, values, (((1,), (1,)), ((), ())), preferred_element_type=jnp.float32
        )
        ping = (found[:, 0:1] * HALF + found[:, 1:2]).astype(jnp.int32)
        mask = found[:, 2:3]
        offset = (2 * ping + 1) * tile_total - (2 * tile_global + 1) * ping_total
        along = offset.astype(jnp.float32) * (track_groups / (2.0 * ping_total * tile_total))
        lane = lax.broadcasted_iota(jnp.int32, (1, LANES), 1).astype(jnp.float32)
        across = (lane + 0.5) / pixels - 0.5
        angle = 96.0 * across * along + 8.0 * (along * along)
        base_cos[0] = jnp.cos(angle) * mask
        base_sin[0] = jnp.sin(angle) * mask
        step = jnp.broadcast_to((96.0 * LANES / pixels) * along, (slots, 8))
        step_cos[0] = jnp.broadcast_to(jnp.cos(step)[:, :1], (slots, LANES))
        step_sin[0] = jnp.broadcast_to(jnp.sin(step)[:, :1], (slots, LANES))

    return table_kernel


def phase_tables(
    base, counts, foot_slot, foot_ping, slots, ping_total, tile_total, track_groups, tile_devs, pixels
):
    tiles_here, foot = foot_slot.shape
    kernel = make_table_kernel(ping_total, tile_total, track_groups, pixels, tile_devs, slots)
    table = jax.ShapeDtypeStruct((tiles_here, slots, LANES), jnp.float32)
    return pl.pallas_call(
        kernel,
        grid_spec=pltpu.PrefetchScalarGridSpec(
            num_scalar_prefetch=2,
            grid=(tiles_here,),
            in_specs=[pl.BlockSpec((1, 1, foot), lambda t, *_: (t, 0, 0))] * 2,
            out_specs=[pl.BlockSpec((1, slots, LANES), lambda t, *_: (t, 0, 0))] * 4,
        ),
        out_shape=[table] * 4,
        compiler_params=pltpu.CompilerParams(vmem_limit_bytes=VMEM_BYTES),
        name="phase_tables",
    )(base, counts, foot_slot.reshape(tiles_here, 1, foot), foot_ping.reshape(tiles_here, 1, foot))


def make_focus_kernel(slots, pixels, bins, tiles, chunk, piece):
    blocks = pixels // LANES
    chunks = slots // chunk

    def focus_kernel(
        class_ref, rows_ref, weight_hbm, base_c, base_s, step_c, step_s,
        image_ref, corr_ref, *scratch,
    ):
        turned_r, turned_i, corr_acc, weight_ref = scratch[2 * chunks : 2 * chunks + 4]
        tables_hbm = (base_c, base_s, step_c, step_s)
        tables = scratch[2 * chunks + 4 : 2 * chunks + 8]
        base_cos, base_sin, step_cos, step_sin = tables
        weight_sem, table_sem = scratch[2 * chunks + 8 :]

        def weight_copy(tile):
            return pltpu.make_async_copy(
                weight_hbm.at[class_ref[tile]], weight_ref.at[tile], weight_sem.at[tile]
            )

        def table_copies(tile):
            return [
                pltpu.make_async_copy(source.at[tile], target.at[tile], table_sem.at[tile, i])
                for i, (source, target) in enumerate(zip(tables_hbm, tables))
            ]

        for tile in range(tiles):
            weight_copy(tile).start()
            for copy in table_copies(tile):
                copy.start()

        def project(tile, part):
            for first in range(0, pixels, piece):
                for half in range(2):
                    scratch[2 * part + half][:, pl.ds(first, piece)] = lax.dot_general(
                        rows_ref[pl.ds(part * chunk, chunk), pl.ds(half * bins, bins)],
                        weight_ref[tile, pl.ds(first, piece), :],
                        (((1,), (1,)), ((), ())),
                        preferred_element_type=jnp.float32,
                    )

        def turn(tile, part, sums):
            sums = list(sums)
            for group in range(chunk // 8):
                local = pl.ds(group * 8, 8)
                at = pl.ds(part * chunk + group * 8, 8)
                cos_now = base_cos[tile, at, :]
                sin_now = base_sin[tile, at, :]
                turn_c = step_cos[tile, at, :]
                turn_s = step_sin[tile, at, :]
                for b in range(blocks):
                    lanes = pl.ds(b * LANES, LANES)
                    real = scratch[2 * part][local, lanes]
                    imag = scratch[2 * part + 1][local, lanes]
                    new_r = cos_now * real - sin_now * imag
                    new_i = sin_now * real + cos_now * imag
                    turned_r[at, lanes] = new_r
                    turned_i[at, lanes] = new_i
                    sums[2 * b] = sums[2 * b] + new_r
                    sums[2 * b + 1] = sums[2 * b + 1] + new_i
                    if b + 1 < blocks:
                        cos_now, sin_now = (
                            cos_now * turn_c - sin_now * turn_s,
                            sin_now * turn_c + cos_now * turn_s,
                        )
            return sums

        def one_tile(tile, _):
            sums = [jnp.zeros((8, LANES), jnp.float32)] * (2 * blocks)
            for copy in table_copies(tile):
                copy.wait()
            for part in range(chunks):
                following = tile
                if part + 1 == chunks:
                    following = jnp.minimum(tile + 1, tiles - 1)

                    @pl.when(tile + 1 < tiles)
                    def _():
                        weight_copy(tile + 1).wait()

                project(following, (part + 1) % chunks)
                sums = turn(tile, part, sums)
            heavy = []
            for b in range(blocks):
                lanes = pl.ds(b * LANES, LANES)
                real = jnp.sum(sums[2 * b], axis=0, keepdims=True)
                imag = jnp.sum(sums[2 * b + 1], axis=0, keepdims=True)
                image_ref[tile, 0:1, lanes] = real
                image_ref[tile, 1:2, lanes] = imag
                intensity = real * real + imag * imag
                heavy.append(jnp.broadcast_to(intensity * real, (8, LANES)))
                heavy.append(jnp.broadcast_to(intensity * imag, (8, LANES)))

            def pull(i, _):
                at = pl.ds(pl.multiple_of(i * 8, 8), 8)
                total = corr_acc[at, :]
                for b in range(blocks):
                    lanes = pl.ds(b * LANES, LANES)
                    total = total + (
                        turned_r[at, lanes] * heavy[2 * b + 1] - turned_i[at, lanes] * heavy[2 * b]
                    )
                corr_acc[at, :] = total
                return 0

            lax.fori_loop(0, slots // 8, pull, 0, unroll=4)
            return 0

        corr_acc[...] = jnp.zeros_like(corr_acc)
        weight_copy(0).wait()
        project(0, 0)
        lax.fori_loop(0, tiles, one_tile, 0)
        for part in range(slots // LANES):
            block = corr_acc[pl.ds(part * LANES, LANES), :]
            corr_ref[pl.ds(part, 1), :] = jnp.sum(block.T, axis=0, keepdims=True)

    return focus_kernel


def focus(tile_class, received, weight_tiles, tables, chunk, piece):
    slots, _ = received.shape
    _, pixels, bins = weight_tiles.shape
    tiles = tile_class.shape[0]
    parts = slots // LANES
    vmem = pl.BlockSpec(memory_space=pltpu.VMEM)
    image, corr = pl.pallas_call(
        make_focus_kernel(slots, pixels, bins, tiles, chunk, piece),
        in_specs=[pl.BlockSpec(memory_space=pltpu.SMEM), vmem]
        + [pl.BlockSpec(memory_space=pltpu.HBM)] * 5,
        out_specs=[vmem] * 2,
        scratch_shapes=[pltpu.VMEM((chunk, pixels), jnp.float32)] * (2 * (slots // chunk))
        + [
            pltpu.VMEM((slots, pixels), jnp.float32),
            pltpu.VMEM((slots, pixels), jnp.float32),
            pltpu.VMEM((slots, LANES), jnp.float32),
            pltpu.VMEM((tiles, pixels, bins), jnp.bfloat16),
        ]
        + [pltpu.VMEM((tiles, slots, LANES), jnp.float32)] * 4
        + [pltpu.SemaphoreType.DMA((tiles,)), pltpu.SemaphoreType.DMA((tiles, 4))],
        out_shape=[
            jax.ShapeDtypeStruct((tiles, 2, pixels), jnp.float32),
            jax.ShapeDtypeStruct((parts, LANES), jnp.float32),
        ],
        compiler_params=pltpu.CompilerParams(vmem_limit_bytes=48 * 1024 * 1024),
        name="focus",
    )(tile_class, received, weight_tiles, *tables)
    return image, corr.reshape(slots)


def on_device(
    panels, phases, weight_tiles, tile_class, send_slots, foot_slot, foot_ping, tile_counts
):
    track_devs = lax.axis_size("track")
    tile_devs = lax.axis_size("tile")
    device = lax.axis_index("track") * tile_devs + lax.axis_index("tile")
    ping_local = phases.shape[0]
    row_width = panels.shape[1]
    tiles_here = tile_counts.shape[0]
    pixels = weight_tiles.shape[1]
    slots = send_slots.shape[0]
    slot_cap = slots // 3 // tile_devs
    ping_total = ping_local * track_devs * tile_devs
    tile_total = tiles_here * track_devs * tile_devs

    blocks = (tile_devs, slot_cap, row_width)
    to_next, to_last = gather_rotated(panels, phases, send_slots, (2, 0))
    behind = shift_along(to_next.reshape(blocks), "track", 1)
    ahead = shift_along(to_last.reshape(blocks), "track", -1)
    (own,) = gather_rotated(panels, phases, send_slots, (1,))
    mixed = jnp.concatenate([behind, own.reshape(blocks), ahead], axis=1)
    arrived = lax.all_to_all(mixed, "tile", split_axis=0, concat_axis=0, tiled=True)
    tables = phase_tables(
        (device * tiles_here).astype(jnp.int32).reshape(1),
        tile_counts, foot_slot, foot_ping, slots,
        ping_total, tile_total, track_devs, tile_devs, pixels,
    )
    image, corr = focus(
        tile_class, arrived.reshape(slots, row_width), weight_tiles, tables, slots // 3, 256
    )

    partial = corr.reshape(tile_devs, 3, slot_cap)
    behind = shift_along(partial[:, 2], "track", 1)
    ahead = shift_along(partial[:, 0], "track", -1)
    back = jnp.concatenate([behind, partial[:, 1], ahead], axis=1)
    back = lax.all_to_all(back, "tile", split_axis=0, concat_axis=0, tiled=True)
    back = back.reshape(tile_devs, 3, slot_cap).transpose(1, 0, 2).reshape(1, slots)
    owner = (send_slots // (panels.shape[0] // ping_local)).reshape(1, slots)
    mine = lax.broadcasted_iota(jnp.int32, (ping_local, slots), 0) == owner
    ping_gradient = jnp.sum(jnp.where(mine & (send_slots >= 0)[None, :], back, 0.0), axis=1)
    return (image, ping_gradient)


def solution(mesh):
    spread = P(("track", "tile"))
    in_specs = (
        P(("track", "tile"), None), spread, P(), spread, spread,
        P(("track", "tile"), None), P(("track", "tile"), None), spread,
    )
    out_specs = (P(("track", "tile"), None, None), spread)
    return jax.shard_map(
        on_device, mesh=mesh, in_specs=in_specs, out_specs=out_specs, check_vma=False
    )
```

time: 136 us -> 115 us (0.85)
  Pallas kernels: 54.6 us -> 34 us
  local copies, waits for them, and re-layouts: 6.56 us -> 8.24 us
  waiting for transfers between devices: 37 us -> 35.4 us
    pallas_call x2 -> x3, Pallas kernels: 39.4 us -> 20.5 us  [the longest x1 17.9 us: focus(): pl.pallas_call(make_focus_kernel(slots, pixels, bins, tiles, chunk, piece...]
    unnamed x6 -> x22, local copies, waits for them, and re-layouts: 0.01 us -> 7.16 us
    squeeze x4 -> x0, local copies, waits for them, and re-layouts: 1.73 us -> none  [the longest x1 1.49 us: on_device(): behind = shift_along(outgoing[2], 'track', 1)]
    pallas_call x1, Pallas kernels: 15.2 us -> 13.5 us  [phase_tables(): pl.pallas_call(kernel, grid_spec=pltpu.PrefetchScalarGridSpec(num_scalar_...]
  transfers between devices with their start and end apart: 6 -> 6, of which waited for: 5 -> 5; matrix products, arithmetic and copies ran while one was open for 1% -> 0% of each run, Pallas kernels for 11% -> 13%
where the time goes in v2:
time: 115 us
  waiting for transfers between devices  35.4 us (31%)
  Pallas kernels  34 us (30%)
  starting transfers between devices  33.7 us (29%)
  local copies, waits for them, and re-layouts  8.24 us (7%)
  other arithmetic  2.67 us (2%)
    pallas_call x1, Pallas kernels, focus(): pl.pallas_call(make_focus_kernel(slots, pixels, bins, tiles, chunk, piece...  17.9 us
    ppermute x4, starting transfers between devices, shift_along(): return lax.ppermute(block, axis, route)  16.8 us
    all_to_all x1, waiting for transfers between devices, on_device(): lax.all_to_all(mixed, 'tile', split_axis=0, concat_axis=0, tiled=True)  16.4 us
    pallas_call x1, Pallas kernels, phase_tables(): pl.pallas_call(kernel, grid_spec=pltpu.PrefetchScalarGridSpec(num_scalar_...  13.5 us
    all_to_all x1, starting transfers between devices, on_device(): lax.all_to_all(mixed, 'tile', split_axis=0, concat_axis=0, tiled=True)  11.3 us
    ppermute x4, waiting for transfers between devices, shift_along(): return lax.ppermute(block, axis, route)  10.7 us
    all_to_all x1, waiting for transfers between devices, on_device(): back = lax.all_to_all(back, 'tile', split_axis=0, concat_axis=0, tiled=True)  8.42 us
    unnamed x22, local copies, waits for them, and re-layouts  7.16 us
  transfers between devices with their start and end apart: 6, of which 5 were waited for; matrix products, arithmetic and copies ran while one was open for 0% of the time, Pallas kernels for 13%

profile of v2, /device:TPU:1, one launch (start us, length us, event | category | flops | bytes accessed | tf_op | source)
XLA Modules:
  0.0 114.8 jit_solution(11454879729136743622)
XLA Ops:
  0.6 0.7 reshape.45.slots_ref
  1.3 0.0 copy-start
  1.3 1.6 %copy-done = bf16[1024,1024]{1,0:T(8,128)(2,1)S(1)} copy-done((bf16[1024,1024]{1,0:T(8,128)(2,1)S(1)}, bf16[1024,1024]{1,0:T(8,128)(2,1)}, u32[]{:S(2)}) %copy-start) | copy-done | bytes 2097176
  2.9 0.0 copy-start.5
  2.9 0.7 copy-done.5
  3.6 1.6 %gather_rotated.2 = (bf16[256,1024]{1,0:T(8,128)(2,1)S(1)}, bf16[256,1024]{1,0:T(8,128)(2,1)S(1)}) custom-call(bf16[1024,1024]{1,0:T(8,128)(2,1)S(1)} %copy-done, f32[1,64]{1,0:T(1,128)S(1)} %bitcast.21, s32[1,768]{1,0:T(1,128)S(1)} %reshape.45.slots_ref), custom_call_target="tpu_custom_call" | custom-call | tf_op jit(solution)/shard_map/gather_rotated/pallas_call | solution.py:62
  5.2 4.5 %collective-permute-start = (bf16[32,8,1024]{2,1,0:T(8,128)(2,1)S(1)}, bf16[32,8,1024]{2,1,0:T(8,128)(2,1)S(1)}, u32[]{:S(2)}, u32[]{:S(2)}) collective-permute-start(bf16[32,8,1024]{2,1,0:T(8,128)(2,1)S(1)} %bitcast.24), channel_id=1, source_target_pairs={{0,32},{32,64},{64,96},{96,128},{128,160},{160,192},{192,224},{1,3... | collective-permute-start | bytes 1572872 | tf_op jit(solution)/shard_map/ppermute | solution.py:16
  9.7 2.0 %collective-permute-start.1 = (bf16[32,8,1024]{2,1,0:T(8,128)(2,1)S(1)}, bf16[32,8,1024]{2,1,0:T(8,128)(2,1)S(1)}, u32[]{:S(2)}, u32[]{:S(2)}) collective-permute-start(bf16[32,8,1024]{2,1,0:T(8,128)(2,1)S(1)} %bitcast.23), channel_id=1, source_target_pairs={{32,0},{64,32},{96,64},{128,96},{160,128},{192,160},{224,192},{33,... | collective-permute-start | bytes 1572872 | tf_op jit(solution)/shard_map/ppermute | solution.py:16
  11.7 1.0 gather_rotated.3
  12.7 3.2 %collective-permute-done = bf16[32,8,1024]{2,1,0:T(8,128)(2,1)S(1)} collective-permute-done((bf16[32,8,1024]{2,1,0:T(8,128)(2,1)S(1)}, bf16[32,8,1024]{2,1,0:T(8,128)(2,1)S(1)}, u32[]{:S(2)}, u32[]{:S(2)}) %collective-permute-start) | collective-permute-done | bytes 524320 | tf_op jit(solution)/shard_map/ppermute | solution.py:16
  15.8 4.4 %collective-permute-done.1 = bf16[32,8,1024]{2,1,0:T(8,128)(2,1)S(1)} collective-permute-done((bf16[32,8,1024]{2,1,0:T(8,128)(2,1)S(1)}, bf16[32,8,1024]{2,1,0:T(8,128)(2,1)S(1)}, u32[]{:S(2)}, u32[]{:S(2)}) %collective-permute-start.1) | collective-permute-done | bytes 524320 | tf_op jit(solution)/shard_map/ppermute | solution.py:16
  20.2 1.3 %pad_maximum_fusion = bf16[32,24,1024]{2,1,0:T(8,128)(2,1)} fusion(bf16[32,8,1024]{2,1,0:T(8,128)(2,1)S(1)} %collective-permute-done.1, bf16[32,8,1024]{2,1,0:T(8,128)(2,1)S(1)} %bitcast.20, bf16[32,8,1024]{2,1,0:T(8,128)(2,1)S(1)} %collective-permute-done), kind=kLoop, calls=%fused_computation | loop fusion | flops 4718592 | bytes 3145728 | tf_op jit(solution)/shard_map/concatenate | solution.py:300
  21.6 0.0 copy-start.9
  21.6 0.0 copy-start.10
  21.6 0.0 copy-start.7
  21.6 0.0 copy-start.6
  21.6 11.3 %all-to-all-start = ((bf16[32,24,1024]{2,1,0:T(8,128)(2,1)}), bf16[32,24,1024]{2,1,0:T(8,128)(2,1)S(1)}, u32[]{:S(2)}, u32[]{:S(2)}) async-start(bf16[32,24,1024]{2,1,0:T(8,128)(2,1)} %pad_maximum_fusion), calls=%async_computation | async-start | bytes 3145728 | tf_op jit(solution)/shard_map/all_to_all | solution.py:301
  32.9 0.0 copy-done.9
  32.9 0.0 copy-done.10
  33.0 0.0 copy-done.7
  33.0 13.5 %phase_tables.1 = (f32[4,768,128]{2,1,0:T(8,128)S(1)}, f32[4,768,128]{2,1,0:T(8,128)S(1)}, f32[4,768,128]{2,1,0:T(8,128)S(1)}, f32[4,768,128]{2,1,0:T(8,128)S(1)}) custom-call(s32[1]{0:T(128)} %bitcast.5.base_ref, s32[4]{0:T(128)S(1)} %copy-done.7, s32[4,1,512]{2,1,0:T(1,128)S(1)} %reshape.51.slot_ref, s32[4,1,512]{2,1,0:T(1,128)S(1)} %reshape.52.ping_ref), custom_call_target="tpu_custom_call" | custom-call | tf_op jit(solution)/shard_map/phase_tables/pallas_call | solution.py:119
  46.5 0.0 copy-start.1
  46.5 1.1 copy-done.1
  47.6 0.0 copy-start.3
  47.6 1.2 %copy-done.3 = f32[4,768,128]{2,1,0:T(8,128)} copy-done((f32[4,768,128]{2,1,0:T(8,128)}, f32[4,768,128]{2,1,0:T(8,128)S(1)}, u32[]{:S(2)}) %copy-start.3) | copy-done | bytes 1572888
  48.8 0.0 copy-start.4
  48.8 1.2 %copy-done.4 = f32[4,768,128]{2,1,0:T(8,128)} copy-done((f32[4,768,128]{2,1,0:T(8,128)}, f32[4,768,128]{2,1,0:T(8,128)S(1)}, u32[]{:S(2)}) %copy-start.4) | copy-done | bytes 1572888
  50.0 16.4 %all-to-all-done = bf16[32,24,1024]{2,1,0:T(8,128)(2,1)S(1)} async-done(((bf16[32,24,1024]{2,1,0:T(8,128)(2,1)}), bf16[32,24,1024]{2,1,0:T(8,128)(2,1)S(1)}, u32[]{:S(2)}, u32[]{:S(2)}) %all-to-all-start) | async-done | bytes 1572896 | tf_op jit(solution)/shard_map/all_to_all | solution.py:301
  66.3 0.0 copy-done.6
  66.3 0.0 copy-start.2
  66.3 1.4 %copy-done.2 = f32[4,768,128]{2,1,0:T(8,128)S(1)} copy-done((f32[4,768,128]{2,1,0:T(8,128)S(1)}, f32[4,768,128]{2,1,0:T(8,128)}, u32[]{:S(2)}) %copy-start.2) | copy-done | bytes 1572888
  67.7 0.0 copy-start.8
  67.8 17.9 %focus.1 = (f32[4,2,1024]{2,1,0:T(2,128)}, f32[6,128]{1,0:T(8,128)S(1)}) custom-call(s32[4]{0:T(128)S(1)} %copy-done.6, bf16[768,1024]{1,0:T(8,128)(2,1)S(1)} %bitcast.19, bf16[4,1024,512]{2,1,0:T(8,128)(2,1)} %weight_hbm.1, f32[4,768,128]{2,1,0:T(8,128)S(1)} %get-tuple-element.12.base_c, f32[4,768,128]{2,1,0:T(8,128)S(1)} %copy-done.2, ...), custom_call_target="tpu_custom_call" | custom-call | tf_op jit(solution)/shard_map/focus/pallas_call | solution.py:256
  85.6 0.1 reshape_reshape.3
  85.8 8.4 %collective-permute-start.2 = (f32[32,8]{1,0:T(8,128)S(1)}, f32[32,8]{1,0:T(8,128)S(1)}, u32[]{:S(2)}, u32[]{:S(2)}) collective-permute-start(f32[32,8]{1,0:T(8,128)S(1)} %bitcast.28), channel_id=1, source_target_pairs={{0,32},{32,64},{64,96},{96,128},{128,160},{160,192},{192,224},{1,3... | collective-permute-start | bytes 3080 | tf_op jit(solution)/shard_map/ppermute | solution.py:16
  94.2 1.9 %collective-permute-start.3 = (f32[32,8]{1,0:T(8,128)S(1)}, f32[32,8]{1,0:T(8,128)S(1)}, u32[]{:S(2)}, u32[]{:S(2)}) collective-permute-start(f32[32,8]{1,0:T(8,128)S(1)} %bitcast.27), channel_id=1, source_target_pairs={{32,0},{64,32},{96,64},{128,96},{160,128},{192,160},{224,192},{33,... | collective-permute-start | bytes 3080 | tf_op jit(solution)/shard_map/ppermute | solution.py:16
  96.1 0.0 copy-done.8
  96.2 0.0 collective-permute-done.2
  96.2 3.1 %collective-permute-done.3 = f32[32,8]{1,0:T(8,128)S(1)} collective-permute-done((f32[32,8]{1,0:T(8,128)S(1)}, f32[32,8]{1,0:T(8,128)S(1)}, u32[]{:S(2)}, u32[]{:S(2)}) %collective-permute-start.3) | collective-permute-done | bytes 1056 | tf_op jit(solution)/shard_map/ppermute | solution.py:16
  99.3 0.7 pad_maximum_fusion.1
  99.9 5.5 %all-to-all-start.1 = ((f32[32,1,24]{2,1,0:T(1,128)}), f32[32,1,24]{2,1,0:T(1,128)S(1)}, u32[]{:S(2)}, u32[]{:S(2)}) async-start(f32[32,1,24]{2,1,0:T(1,128)} %bitcast.10), calls=%async_computation.1 | async-start | bytes 32768 | tf_op jit(solution)/shard_map/all_to_all | solution.py:315
  105.5 8.4 %all-to-all-done.1 = f32[32,1,24]{2,1,0:T(1,128)S(1)} async-done(((f32[32,1,24]{2,1,0:T(1,128)}), f32[32,1,24]{2,1,0:T(1,128)S(1)}, u32[]{:S(2)}, u32[]{:S(2)}) %all-to-all-start.1) | async-done | bytes 3104 | tf_op jit(solution)/shard_map/all_to_all | solution.py:315
  113.9 0.1 copy.24
  114.0 0.1 copy.25
  114.1 0.1 broadcast_in_dim.15
  114.2 0.7 select_reduce_fusion
  (5 shorter events, 0.1 us)
Async XLA Ops:
  1.3 1.6 %copy-start = (bf16[1024,1024]{1,0:T(8,128)(2,1)S(1)}, bf16[1024,1024]{1,0:T(8,128)(2,1)}, u32[]{:S(2)}) copy-start(bf16[1024,1024]{1,0:T(8,128)(2,1)} %panels_ref.3) | copy-start | bytes 6291460
  2.9 0.7 copy-start.5
  5.2 10.6 %collective-permute-start = (bf16[32,8,1024]{2,1,0:T(8,128)(2,1)S(1)}, bf16[32,8,1024]{2,1,0:T(8,128)(2,1)S(1)}, u32[]{:S(2)}, u32[]{:S(2)}) collective-permute-start(bf16[32,8,1024]{2,1,0:T(8,128)(2,1)S(1)} %bitcast.24), channel_id=1, source_target_pairs={{0,32},{32,64},{64,96},{96,128},{128,160},{160,192},{192,224},{1,3... | collective-permute-start | bytes 1572872 | tf_op jit(solution)/shard_map/ppermute | solution.py:16
  9.7 10.5 %collective-permute-start.1 = (bf16[32,8,1024]{2,1,0:T(8,128)(2,1)S(1)}, bf16[32,8,1024]{2,1,0:T(8,128)(2,1)S(1)}, u32[]{:S(2)}, u32[]{:S(2)}) collective-permute-start(bf16[32,8,1024]{2,1,0:T(8,128)(2,1)S(1)} %bitcast.23), channel_id=1, source_target_pairs={{32,0},{64,32},{96,64},{128,96},{160,128},{192,160},{224,192},{33,... | collective-permute-start | bytes 1572872 | tf_op jit(solution)/shard_map/ppermute | solution.py:16
  21.6 11.4 %copy-start.9 = (s32[4,512]{1,0:T(4,128)S(1)}, s32[4,512]{1,0:T(4,128)}, u32[]{:S(2)}) copy-start(s32[4,512]{1,0:T(4,128)} %param.13) | copy-start | bytes 24580
  21.6 11.4 %copy-start.10 = (s32[4,512]{1,0:T(4,128)S(1)}, s32[4,512]{1,0:T(4,128)}, u32[]{:S(2)}) copy-start(s32[4,512]{1,0:T(4,128)} %param.14) | copy-start | bytes 24580
  21.6 11.4 %copy-start.7 = (s32[4]{0:T(128)S(1)}, s32[4]{0:T(128)}, u32[]{:S(2)}) copy-start(s32[4]{0:T(128)} %counts_ref.1) | copy-start | bytes 52
  21.6 44.8 %copy-start.6 = (s32[4]{0:T(128)S(1)}, s32[4]{0:T(128)}, u32[]{:S(2)}) copy-start(s32[4]{0:T(128)} %class_ref.1) | copy-start | bytes 52
  21.6 44.8 %all-to-all-start = ((bf16[32,24,1024]{2,1,0:T(8,128)(2,1)}), bf16[32,24,1024]{2,1,0:T(8,128)(2,1)S(1)}, u32[]{:S(2)}, u32[]{:S(2)}) async-start(bf16[32,24,1024]{2,1,0:T(8,128)(2,1)} %pad_maximum_fusion), calls=%async_computation | async-start | bytes 3145728 | tf_op jit(solution)/shard_map/all_to_all | solution.py:301
  46.5 1.1 copy-start.1
  47.6 1.2 %copy-start.3 = (f32[4,768,128]{2,1,0:T(8,128)}, f32[4,768,128]{2,1,0:T(8,128)S(1)}, u32[]{:S(2)}) copy-start(f32[4,768,128]{2,1,0:T(8,128)S(1)} %get-tuple-element.14.step_c) | copy-start | bytes 4718596
  48.8 1.2 %copy-start.4 = (f32[4,768,128]{2,1,0:T(8,128)}, f32[4,768,128]{2,1,0:T(8,128)S(1)}, u32[]{:S(2)}) copy-start(f32[4,768,128]{2,1,0:T(8,128)S(1)} %get-tuple-element.15.step_s) | copy-start | bytes 4718596
  66.3 1.4 %copy-start.2 = (f32[4,768,128]{2,1,0:T(8,128)S(1)}, f32[4,768,128]{2,1,0:T(8,128)}, u32[]{:S(2)}) copy-start(f32[4,768,128]{2,1,0:T(8,128)} %copy-done.1) | copy-start | bytes 4718596
  67.7 28.4 %copy-start.8 = (s32[768]{0:T(1024)S(1)}, s32[768]{0:T(1024)}, u32[]{:S(2)}) copy-start(s32[768]{0:T(1024)} %param.12) | copy-start | bytes 9220
  85.8 10.4 %collective-permute-start.2 = (f32[32,8]{1,0:T(8,128)S(1)}, f32[32,8]{1,0:T(8,128)S(1)}, u32[]{:S(2)}, u32[]{:S(2)}) collective-permute-start(f32[32,8]{1,0:T(8,128)S(1)} %bitcast.28), channel_id=1, source_target_pairs={{0,32},{32,64},{64,96},{96,128},{128,160},{160,192},{192,224},{1,3... | collective-permute-start | bytes 3080 | tf_op jit(solution)/shard_map/ppermute | solution.py:16
  94.2 5.1 %collective-permute-start.3 = (f32[32,8]{1,0:T(8,128)S(1)}, f32[32,8]{1,0:T(8,128)S(1)}, u32[]{:S(2)}, u32[]{:S(2)}) collective-permute-start(f32[32,8]{1,0:T(8,128)S(1)} %bitcast.27), channel_id=1, source_target_pairs={{32,0},{64,32},{96,64},{128,96},{160,128},{192,160},{224,192},{33,... | collective-permute-start | bytes 3080 | tf_op jit(solution)/shard_map/ppermute | solution.py:16
  99.9 14.0 %all-to-all-start.1 = ((f32[32,1,24]{2,1,0:T(1,128)}), f32[32,1,24]{2,1,0:T(1,128)S(1)}, u32[]{:S(2)}, u32[]{:S(2)}) async-start(f32[32,1,24]{2,1,0:T(1,128)} %bitcast.10), calls=%async_computation.1 | async-start | bytes 32768 | tf_op jit(solution)/shard_map/all_to_all | solution.py:315

commit v3 on v2

v3 whole, which is shorter than its diff:
```python
import functools
import math

import jax
import jax.numpy as jnp
from jax import lax
from jax.experimental import pallas as pl
from jax.experimental.pallas import tpu as pltpu
from jax.sharding import PartitionSpec as P

LANES = 128
HALF = 128
VMEM_BYTES = 24 * 1024 * 1024
ALL_VMEM = 60 * 1024 * 1024


def shift_along(block, axis, distance):
    devices = range(lax.axis_size(axis))
    route = [(i - distance, i) for i in devices if i - distance in devices]
    return lax.ppermute(block, axis, route)


def whole(shape):
    return pl.BlockSpec(shape, lambda *_: (0,) * len(shape))


def column(row):
    return jnp.broadcast_to(row, (8, row.shape[1])).T[:, :1]


def rotated_rows(panels_ref, phases_ref, slots):
    rows_here, width = panels_ref.shape
    bins = width // 2
    pings = phases_ref.shape[1]
    count = slots.shape[1]
    slot_row = column(slots.astype(jnp.float32)).astype(jnp.int32)
    row_ids = lax.broadcasted_iota(jnp.int32, (count, rows_here), 1)
    pick = jnp.where(row_ids == slot_row, 1.0, 0.0).astype(jnp.bfloat16)
    picked = jnp.dot(pick, panels_ref[...], preferred_element_type=jnp.float32)
    phases = phases_ref[...]
    ping_ids = lax.broadcasted_iota(jnp.int32, (count, pings), 1)
    owned = ping_ids == (slot_row // (rows_here // pings))
    cos_col = jnp.sum(jnp.where(owned, jnp.cos(phases), 0.0), axis=1, keepdims=True)
    sin_col = jnp.sum(jnp.where(owned, jnp.sin(phases), 0.0), axis=1, keepdims=True)
    real_part = picked[:, :bins]
    imag_part = picked[:, bins:]
    return (
        (cos_col * real_part - sin_col * imag_part).astype(jnp.bfloat16),
        (sin_col * real_part + cos_col * imag_part).astype(jnp.bfloat16),
    )


def gather_rotated(panels, phases, slots, offsets):
    count = slots.shape[0] // 3
    width = panels.shape[1]
    bins = width // 2

    def kernel(panels_ref, phases_ref, slots_ref, *outs):
        for offset, out in zip(offsets, outs):
            real_part, imag_part = rotated_rows(
                panels_ref, phases_ref, slots_ref[:, pl.ds(offset * count, count)]
            )
            out[:, :bins] = real_part
            out[:, bins:] = imag_part

    return pl.pallas_call(
        kernel,
        out_shape=[jax.ShapeDtypeStruct((count, width), jnp.bfloat16) for _ in offsets],
        compiler_params=pltpu.CompilerParams(vmem_limit_bytes=VMEM_BYTES),
        name="gather_rotated",
    )(panels, phases.reshape(1, -1), slots.reshape(1, -1))


def cos_sin(angle):
    turns = jnp.round(angle * (2.0 / math.pi))
    rest = angle - turns * 1.5703125
    rest = rest - turns * 4.837512969970703125e-4
    rest = rest - turns * 7.549789948768648e-8
    square = rest * rest
    sine = (-1.9515295891e-4 * square + 8.3321608736e-3) * square - 1.6666654611e-1
    sine = sine * square * rest + rest
    cosine = (2.443315711809948e-5 * square - 1.388731625493765e-3) * square
    cosine = (cosine + 4.166664568298827e-2) * square * square - 0.5 * square + 1.0
    quarter = turns.astype(jnp.int32)
    odd = (quarter & 1) == 1
    cos_out = jnp.where(odd, sine, cosine)
    sin_out = jnp.where(odd, cosine, sine)
    cos_out = jnp.where(((quarter + 1) & 2) == 2, -cos_out, cos_out)
    sin_out = jnp.where((quarter & 2) == 2, -sin_out, sin_out)
    return cos_out, sin_out


def make_table_kernel(ping_total, tile_total, track_groups, pixels, tile_devs, slots, tiles):
    def table_kernel(base_ref, counts_ref, slot_ref, ping_ref, base_cos, base_sin, step_cos, step_sin):
        foot = slot_ref.shape[1]
        group = slots // 3
        cap = group // tile_devs
        slot_ids = lax.broadcasted_iota(jnp.int32, (slots, foot), 0)
        lane = lax.broadcasted_iota(jnp.int32, (1, LANES), 1)
        across = (lane.astype(jnp.float32) + 0.5) / pixels - 0.5
        step_angle = jnp.zeros((slots, LANES), jnp.float32)
        for tile in range(tiles):
            listed = slot_ref[tile : tile + 1, :]
            offset = listed // group
            source = (listed % group) // cap
            place = listed % cap
            placed = jnp.where(
                offset == 1,
                2 * group + source * cap + place,
                (source * 2 + offset // 2) * cap + place,
            )
            match = jnp.where(slot_ids == placed, 1.0, 0.0).astype(jnp.bfloat16)
            pings = ping_ref[tile : tile + 1, :]
            entry = lax.broadcasted_iota(jnp.int32, (1, foot), 1)
            used = jnp.where(entry < counts_ref[tile], 1.0, 0.0)
            values = jnp.concatenate(
                [
                    (pings // HALF).astype(jnp.float32) * used,
                    (pings % HALF).astype(jnp.float32) * used,
                    used,
                    jnp.zeros((5, foot), jnp.float32),
                ],
                axis=0,
            ).astype(jnp.bfloat16)
            found = lax.dot_general(
                match, values, (((1,), (1,)), ((), ())), preferred_element_type=jnp.float32
            )
            ping = (found[:, 0:1] * HALF + found[:, 1:2]).astype(jnp.int32)
            mask = found[:, 2:3]
            gap = (2 * ping + 1) * tile_total - (2 * (base_ref[0] + tile) + 1) * ping_total
            along = gap.astype(jnp.float32) * (track_groups / (2.0 * ping_total * tile_total))
            cosine, sine = cos_sin(96.0 * across * along + 8.0 * (along * along))
            base_cos[tile] = cosine * mask
            base_sin[tile] = sine * mask
            step_angle = jnp.where(lane == tile, (96.0 * LANES / pixels) * along, step_angle)
        cosine, sine = cos_sin(step_angle)
        for tile in range(tiles):
            step_cos[tile] = jnp.broadcast_to(cosine[:, tile : tile + 1], (slots, LANES))
            step_sin[tile] = jnp.broadcast_to(sine[:, tile : tile + 1], (slots, LANES))

    return table_kernel


def phase_tables(
    base, counts, foot_slot, foot_ping, slots, ping_total, tile_total, track_groups, tile_devs, pixels
):
    tiles, foot = foot_slot.shape
    kernel = make_table_kernel(ping_total, tile_total, track_groups, pixels, tile_devs, slots, tiles)
    table = jax.ShapeDtypeStruct((tiles, slots, LANES), jnp.float32)
    smem = pl.BlockSpec(memory_space=pltpu.SMEM)
    vmem = pl.BlockSpec(memory_space=pltpu.VMEM)
    return pl.pallas_call(
        kernel,
        in_specs=[smem, smem, vmem, vmem],
        out_specs=[vmem] * 4,
        out_shape=[table] * 4,
        compiler_params=pltpu.CompilerParams(vmem_limit_bytes=ALL_VMEM),
        name="phase_tables",
    )(base, counts, foot_slot, foot_ping)


def turn_rows(real_ref, imag_ref, rows, cos_now, sin_now, turn_c, turn_s, out_r, out_i, sums):
    blocks = len(sums) // 2
    sums = list(sums)
    for b in range(blocks):
        lanes = pl.ds(b * LANES, LANES)
        real = real_ref[rows, lanes]
        imag = imag_ref[rows, lanes]
        new_r = cos_now * real - sin_now * imag
        new_i = sin_now * real + cos_now * imag
        out_r(lanes, new_r)
        out_i(lanes, new_i)
        sums[2 * b] = sums[2 * b] + new_r
        sums[2 * b + 1] = sums[2 * b + 1] + new_i
        if b + 1 < blocks:
            cos_now, sin_now = (
                cos_now * turn_c - sin_now * turn_s,
                sin_now * turn_c + cos_now * turn_s,
            )
    return sums


def project_rows(rows_ref, first_row, count, weight, out_r, out_i, bins, pixels, piece):
    for first in range(0, pixels, piece):
        for half, out in enumerate((out_r, out_i)):
            out[:, pl.ds(first, piece)] = lax.dot_general(
                rows_ref[pl.ds(first_row, count), pl.ds(half * bins, bins)],
                weight(first, piece),
                (((1,), (1,)), ((), ())),
                preferred_element_type=jnp.float32,
            )


def own_forward(tile_class, own, weight_tiles, tables, first_slot):
    count, width = own.shape
    _, pixels, bins = weight_tiles.shape
    tiles = tile_class.shape[0]
    blocks = pixels // LANES
    block_at = first_slot // count

    def kernel(class_ref, rows_ref, weight_ref, base_c, base_s, step_c, step_s, turned_r, turned_i, sums_ref, proj_r, proj_i):
        project_rows(
            rows_ref, 0, count, lambda first, size: weight_ref[0, pl.ds(first, size), :],
            proj_r, proj_i, bins, pixels, pixels,
        )

        def group(i, sums):
            at = pl.ds(pl.multiple_of(i * 8, 8), 8)

            def put(ref):
                def store(lanes, value):
                    ref[0, at, lanes] = value

                return store

            return tuple(
                turn_rows(
                    proj_r, proj_i, at, base_c[0, at, :], base_s[0, at, :], step_c[0, at, :],
                    step_s[0, at, :], put(turned_r), put(turned_i), sums,
                )
            )

        sums = (jnp.zeros((8, LANES), jnp.float32),) * (2 * blocks)
        sums = lax.fori_loop(0, count // 8, group, sums, unroll=4)
        for b in range(blocks):
            for half in range(2):
                sums_ref[0, half, :, pl.ds(b * LANES, LANES)] = sums[2 * b + half]

    table_spec = pl.BlockSpec((1, count, LANES), lambda t, *_: (t, block_at, 0))
    turned = jax.ShapeDtypeStruct((tiles, count, pixels), jnp.float32)
    turned_spec = pl.BlockSpec((1, count, pixels), lambda t, *_: (t, 0, 0))
    return pl.pallas_call(
        kernel,
        grid_spec=pltpu.PrefetchScalarGridSpec(
            num_scalar_prefetch=1,
            grid=(tiles,),
            in_specs=[
                pl.BlockSpec((count, width), lambda t, *_: (0, 0)),
                pl.BlockSpec((1, pixels, bins), lambda t, cls: (cls[t], 0, 0)),
            ]
            + [table_spec] * 4,
            out_specs=[
                turned_spec,
                turned_spec,
                pl.BlockSpec((1, 2, 8, pixels), lambda t, *_: (t, 0, 0, 0)),
            ],
            scratch_shapes=[pltpu.VMEM((count, pixels), jnp.float32)] * 2,
        ),
        out_shape=[turned, turned, jax.ShapeDtypeStruct((tiles, 2, 8, pixels), jnp.float32)],
        compiler_params=pltpu.CompilerParams(vmem_limit_bytes=ALL_VMEM),
        name="own_forward",
    )(tile_class, own, weight_tiles, *tables)


def make_focus_kernel(mixed, own, pixels, bins, tiles, chunk, piece):
    blocks = pixels // LANES
    chunks = mixed // chunk

    def focus_kernel(
        class_ref, rows_ref, sums_ref, weight_hbm, base_c, base_s, step_c, step_s, own_r, own_i,
        image_ref, corr_ref, *scratch,
    ):
        proj = scratch[: 2 * chunks]
        turned_r, turned_i, corr_acc, weight_ref = scratch[2 * chunks : 2 * chunks + 4]
        base_cos, base_sin, step_cos, step_sin, far_r, far_i = scratch[
            2 * chunks + 4 : 2 * chunks + 10
        ]
        weight_sem, table_sem, own_sem = scratch[2 * chunks + 10 :]

        def weight_copy(tile):
            return pltpu.make_async_copy(
                weight_hbm.at[class_ref[tile]], weight_ref.at[tile], weight_sem.at[tile]
            )

        def table_copies(tile):
            pairs = (base_c, base_cos), (base_s, base_sin), (step_c, step_cos), (step_s, step_sin)
            return [
                pltpu.make_async_copy(
                    source.at[tile, pl.ds(0, mixed)], target.at[tile], table_sem.at[tile, i]
                )
                for i, (source, target) in enumerate(pairs)
            ]

        def own_copies(tile):
            return [
                pltpu.make_async_copy(source.at[tile], target.at[tile], own_sem.at[tile, i])
                for i, (source, target) in enumerate(((own_r, far_r), (own_i, far_i)))
            ]

        for tile in range(tiles):
            for copy in [weight_copy(tile)] + table_copies(tile) + own_copies(tile):
                copy.start()

        def project(tile, part):
            project_rows(
                rows_ref, part * chunk, chunk,
                lambda first, size: weight_ref[tile, pl.ds(first, size), :],
                proj[2 * part], proj[2 * part + 1], bins, pixels, piece,
            )

        def turn(tile, part, sums):
            for group in range(chunk // 8):
                at = pl.ds(part * chunk + group * 8, 8)

                def put(ref, at=at):
                    def store(lanes, value):
                        ref[at, lanes] = value

                    return store

                sums = turn_rows(
                    proj[2 * part], proj[2 * part + 1], pl.ds(group * 8, 8),
                    base_cos[tile, at, :], base_sin[tile, at, :],
                    step_cos[tile, at, :], step_sin[tile, at, :],
                    put(turned_r), put(turned_i), sums,
                )
            return sums

        def one_tile(tile, _):
            sums = []
            for b in range(blocks):
                for half in range(2):
                    sums.append(sums_ref[tile, half, :, pl.ds(b * LANES, LANES)])
            for copy in table_copies(tile):
                copy.wait()
            for part in range(chunks):
                following = tile
                if part + 1 == chunks:
                    following = jnp.minimum(tile + 1, tiles - 1)

                    @pl.when(tile + 1 < tiles)
                    def _():
                        weight_copy(tile + 1).wait()

                project(following, (part + 1) % chunks)
                sums = turn(tile, part, sums)
            heavy = []
            for b in range(blocks):
                lanes = pl.ds(b * LANES, LANES)
                real = jnp.sum(sums[2 * b], axis=0, keepdims=True)
                imag = jnp.sum(sums[2 * b + 1], axis=0, keepdims=True)
                image_ref[tile, 0:1, lanes] = real
                image_ref[tile, 1:2, lanes] = imag
                intensity = real * real + imag * imag
                heavy.append(jnp.broadcast_to(intensity * real, (8, LANES)))
                heavy.append(jnp.broadcast_to(intensity * imag, (8, LANES)))
            for copy in own_copies(tile):
                copy.wait()

            def pull(i, _, real_of, imag_of, first):
                row = pl.multiple_of(i * 8, 8)
                at = pl.ds(pl.multiple_of(first + i * 8, 8), 8)
                total = corr_acc[at, :]
                for b in range(blocks):
                    lanes = pl.ds(b * LANES, LANES)
                    total = total + (
                        real_of(row, lanes) * heavy[2 * b + 1] - imag_of(row, lanes) * heavy[2 * b]
                    )
                corr_acc[at, :] = total
                return 0

            near = functools.partial(
                pull,
                real_of=lambda row, lanes: turned_r[pl.ds(row, 8), lanes],
                imag_of=lambda row, lanes: turned_i[pl.ds(row, 8), lanes],
                first=0,
            )
            far = functools.partial(
                pull,
                real_of=lambda row, lanes: far_r[tile, pl.ds(row, 8), lanes],
                imag_of=lambda row, lanes: far_i[tile, pl.ds(row, 8), lanes],
                first=mixed,
            )
            lax.fori_loop(0, mixed // 8, near, 0, unroll=4)
            lax.fori_loop(0, own // 8, far, 0, unroll=4)
            return 0

        corr_acc[...] = jnp.zeros_like(corr_acc)
        weight_copy(0).wait()
        project(0, 0)
        lax.fori_loop(0, tiles, one_tile, 0)
        for part in range((mixed + own) // LANES):
            block = corr_acc[pl.ds(part * LANES, LANES), :]
            corr_ref[pl.ds(part, 1), :] = jnp.sum(block.T, axis=0, keepdims=True)

    return focus_kernel


def focus(tile_class, arrived, weight_tiles, tables, own_parts, chunk, piece):
    turned_own_r, turned_own_i, own_sums = own_parts
    mixed, _ = arrived.shape
    own = turned_own_r.shape[1]
    slots = mixed + own
    _, pixels, bins = weight_tiles.shape
    tiles = tile_class.shape[0]
    vmem = pl.BlockSpec(memory_space=pltpu.VMEM)
    hbm = pl.BlockSpec(memory_space=pltpu.HBM)
    image, corr = pl.pallas_call(
        make_focus_kernel(mixed, own, pixels, bins, tiles, chunk, piece),
        in_specs=[pl.BlockSpec(memory_space=pltpu.SMEM), vmem, vmem] + [hbm] * 7,
        out_specs=[vmem] * 2,
        scratch_shapes=[pltpu.VMEM((chunk, pixels), jnp.float32)] * (2 * (mixed // chunk))
        + [
            pltpu.VMEM((mixed, pixels), jnp.float32),
            pltpu.VMEM((mixed, pixels), jnp.float32),
            pltpu.VMEM((slots, LANES), jnp.float32),
            pltpu.VMEM((tiles, pixels, bins), jnp.bfloat16),
        ]
        + [pltpu.VMEM((tiles, mixed, LANES), jnp.float32)] * 4
        + [pltpu.VMEM((tiles, own, pixels), jnp.float32)] * 2
        + [
            pltpu.SemaphoreType.DMA((tiles,)),
            pltpu.SemaphoreType.DMA((tiles, 4)),
            pltpu.SemaphoreType.DMA((tiles, 2)),
        ],
        out_shape=[
            jax.ShapeDtypeStruct((tiles, 2, pixels), jnp.float32),
            jax.ShapeDtypeStruct((slots // LANES, LANES), jnp.float32),
        ],
        compiler_params=pltpu.CompilerParams(vmem_limit_bytes=ALL_VMEM),
        name="focus",
    )(tile_class, arrived, own_sums, weight_tiles, *tables, turned_own_r, turned_own_i)
    return image, corr.reshape(slots)


def on_device(
    panels, phases, weight_tiles, tile_class, send_slots, foot_slot, foot_ping, tile_counts
):
    track_devs = lax.axis_size("track")
    tile_devs = lax.axis_size("tile")
    device = lax.axis_index("track") * tile_devs + lax.axis_index("tile")
    ping_local = phases.shape[0]
    row_width = panels.shape[1]
    tiles_here = tile_counts.shape[0]
    pixels = weight_tiles.shape[1]
    slots = send_slots.shape[0]
    slot_cap = slots // 3 // tile_devs
    ping_total = ping_local * track_devs * tile_devs
    tile_total = tiles_here * track_devs * tile_devs

    blocks = (tile_devs, slot_cap, row_width)
    group = slots // 3
    (own,) = gather_rotated(panels, phases, send_slots, (1,))
    own_arrived = lax.all_to_all(
        own.reshape(blocks), "tile", split_axis=0, concat_axis=0, tiled=True
    )
    to_next, to_last = gather_rotated(panels, phases, send_slots, (2, 0))
    behind = shift_along(to_next.reshape(blocks), "track", 1)
    ahead = shift_along(to_last.reshape(blocks), "track", -1)
    mixed = jnp.concatenate([behind, ahead], axis=1)
    mixed, own_arrived = lax.optimization_barrier((mixed, own_arrived))
    arrived = lax.all_to_all(mixed, "tile", split_axis=0, concat_axis=0, tiled=True)
    tables = phase_tables(
        (device * tiles_here).astype(jnp.int32).reshape(1),
        tile_counts, foot_slot, foot_ping, slots,
        ping_total, tile_total, track_devs, tile_devs, pixels,
    )
    own_parts = own_forward(
        tile_class, own_arrived.reshape(group, row_width), weight_tiles, tables, 2 * group
    )
    image, corr = focus(
        tile_class, arrived.reshape(2 * group, row_width), weight_tiles, tables, own_parts, group, 256
    )

    partial = corr[: 2 * group].reshape(tile_devs, 2, slot_cap)
    near = corr[2 * group :].reshape(tile_devs, slot_cap)
    behind = shift_along(partial[:, 1], "track", 1)
    ahead = shift_along(partial[:, 0], "track", -1)
    back = jnp.concatenate([behind, near, ahead], axis=1)
    back = lax.all_to_all(back, "tile", split_axis=0, concat_axis=0, tiled=True)
    back = back.reshape(tile_devs, 3, slot_cap).transpose(1, 0, 2).reshape(1, slots)
    owner = (send_slots // (panels.shape[0] // ping_local)).reshape(1, slots)
    mine = lax.broadcasted_iota(jnp.int32, (ping_local, slots), 0) == owner
    ping_gradient = jnp.sum(jnp.where(mine & (send_slots >= 0)[None, :], back, 0.0), axis=1)
    return (image, ping_gradient)


def solution(mesh):
    spread = P(("track", "tile"))
    in_specs = (
        P(("track", "tile"), None), spread, P(), spread, spread,
        P(("track", "tile"), None), P(("track", "tile"), None), spread,
    )
    out_specs = (P(("track", "tile"), None, None), spread)
    return jax.shard_map(
        on_device, mesh=mesh, in_specs=in_specs, out_specs=out_specs, check_vma=False
    )
```

time: 115 us -> 115 us (level); the launches traced: 115 us -> 113 us
  waiting for transfers between devices: 35.4 us -> 25.9 us
  Pallas kernels: 34 us -> 39.6 us
  starting transfers between devices: 33.7 us -> 38.4 us
  local copies, waits for them, and re-layouts: 8.24 us -> 5.78 us
    all_to_all x0 -> x1, starting transfers between devices: none -> 12 us  [on_device(): lax.all_to_all(own.reshape(blocks), 'tile', split_axis=0, concat_axis=0,...]
    all_to_all x1, waiting for transfers between devices: 16.4 us -> 9.66 us  [on_device(): lax.all_to_all(mixed, 'tile', split_axis=0, concat_axis=0, tiled=True)]
    pallas_call x2 -> x3, Pallas kernels: 31.4 us -> 36.2 us  [the longest x1 18.3 us: focus(): pl.pallas_call(make_focus_kernel(mixed, own, pixels, bins, tiles, chunk,...]
    ppermute x4, starting transfers between devices: 16.8 us -> 12 us  [shift_along(): return lax.ppermute(block, axis, route)]
    ppermute x4, waiting for transfers between devices: 10.7 us -> 6.15 us  [shift_along(): return lax.ppermute(block, axis, route)]
    unnamed x22 -> x14, local copies, waits for them, and re-layouts: 7.16 us -> 3.25 us
    all_to_all x1, starting transfers between devices: 11.3 us -> 8.14 us  [on_device(): lax.all_to_all(mixed, 'tile', split_axis=0, concat_axis=0, tiled=True)]
    all_to_all x0 -> x1, waiting for transfers between devices: none -> 1.54 us  [on_device(): lax.all_to_all(own.reshape(blocks), 'tile', split_axis=0, concat_axis=0,...]
  transfers between devices with their start and end apart: 6 -> 7, of which waited for: 5 -> 5; matrix products, arithmetic and copies ran while one was open for 0% -> 2% of each run, Pallas kernels for 13% -> 17%
where the time goes in v3:
time: 115 us; the launch traced here: 113 us
  Pallas kernels  39.6 us (34%)
  starting transfers between devices  38.4 us (33%)
  waiting for transfers between devices  25.9 us (23%)
  local copies, waits for them, and re-layouts  5.78 us (5%)
  other arithmetic  2.42 us (2%)
    pallas_call x1, Pallas kernels, focus(): pl.pallas_call(make_focus_kernel(mixed, own, pixels, bins, tiles, chunk,...  18.3 us
    all_to_all x1, starting transfers between devices, on_device(): lax.all_to_all(own.reshape(blocks), 'tile', split_axis=0, concat_axis=0,...  12 us
    ppermute x4, starting transfers between devices, shift_along(): return lax.ppermute(block, axis, route)  12 us
    pallas_call x1, Pallas kernels, own_forward(): pl.pallas_call(kernel, grid_spec=pltpu.PrefetchScalarGridSpec(num_scalar_...  9.95 us
    all_to_all x1, waiting for transfers between devices, on_device(): lax.all_to_all(mixed, 'tile', split_axis=0, concat_axis=0, tiled=True)  9.66 us
    all_to_all x1, waiting for transfers between devices, on_device(): back = lax.all_to_all(back, 'tile', split_axis=0, concat_axis=0, tiled=True)  8.58 us
    all_to_all x1, starting transfers between devices, on_device(): lax.all_to_all(mixed, 'tile', split_axis=0, concat_axis=0, tiled=True)  8.14 us
    pallas_call x1, Pallas kernels, phase_tables(): pl.pallas_call(kernel, in_specs=[smem, smem, vmem, vmem], out_specs=[vmem...  7.92 us
  transfers between devices with their start and end apart: 7, of which 5 were waited for; matrix products, arithmetic and copies ran while one was open for 2% of the time, Pallas kernels for 17%

profile of v3, /device:TPU:1, one launch (start us, length us, event | category | flops | bytes accessed | tf_op | source)
XLA Modules:
  0.0 112.9 jit_solution(2826820898275680453)
XLA Ops:
  0.6 0.0 copy-start.3
  0.6 0.7 reshape.53.slots_ref
  1.3 0.0 copy-start
  1.3 1.6 %copy-done = bf16[1024,1024]{1,0:T(8,128)(2,1)S(1)} copy-done((bf16[1024,1024]{1,0:T(8,128)(2,1)S(1)}, bf16[1024,1024]{1,0:T(8,128)(2,1)}, u32[]{:S(2)}) %copy-start) | copy-done | bytes 2097176
  2.9 0.0 copy-start.2
  2.9 0.7 copy-done.2
  3.6 0.0 copy-start.1
  3.6 1.8 %gather_rotated.3 = bf16[256,1024]{1,0:T(8,128)(2,1)} custom-call(bf16[1024,1024]{1,0:T(8,128)(2,1)S(1)} %copy-done, f32[1,64]{1,0:T(1,128)S(1)} %bitcast.17, s32[1,768]{1,0:T(1,128)S(1)} %reshape.53.slots_ref), custom_call_target="tpu_custom_call" | custom-call | tf_op jit(solution)/shard_map/gather_rotated/pallas_call | solution.py:66
  5.4 12.0 %all-to-all-start = ((bf16[32,8,1024]{2,1,0:T(8,128)(2,1)}), bf16[32,8,1024]{2,1,0:T(8,128)(2,1)S(1)}, u32[]{:S(2)}, u32[]{:S(2)}) async-start(bf16[32,8,1024]{2,1,0:T(8,128)(2,1)} %bitcast.3), calls=%async_computation | async-start | bytes 1048576 | tf_op jit(solution)/shard_map/all_to_all | solution.py:444
  17.4 0.0 copy-done.3
  17.4 0.0 copy-done.1
  17.4 1.6 %gather_rotated.2 = (bf16[256,1024]{1,0:T(8,128)(2,1)S(1)}, bf16[256,1024]{1,0:T(8,128)(2,1)S(1)}) custom-call(bf16[1024,1024]{1,0:T(8,128)(2,1)S(1)} %copy-done.1, f32[1,64]{1,0:T(1,128)S(1)} %bitcast.18, s32[1,768]{1,0:T(1,128)S(1)} %reshape.53.slots_ref), custom_call_target="tpu_custom_call" | custom-call | tf_op jit(solution)/shard_map/gather_rotated/pallas_call | solution.py:66
  19.1 2.9 %collective-permute-start.1 = (bf16[32,8,1024]{2,1,0:T(8,128)(2,1)S(1)}, bf16[32,8,1024]{2,1,0:T(8,128)(2,1)S(1)}, u32[]{:S(2)}, u32[]{:S(2)}) collective-permute-start(bf16[32,8,1024]{2,1,0:T(8,128)(2,1)S(1)} %bitcast.20), channel_id=1, source_target_pairs={{32,0},{64,32},{96,64},{128,96},{160,128},{192,160},{224,192},{33,... | collective-permute-start | bytes 1572872 | tf_op jit(solution)/shard_map/ppermute | solution.py:20
  21.9 3.0 %collective-permute-start = (bf16[32,8,1024]{2,1,0:T(8,128)(2,1)S(1)}, bf16[32,8,1024]{2,1,0:T(8,128)(2,1)S(1)}, u32[]{:S(2)}, u32[]{:S(2)}) collective-permute-start(bf16[32,8,1024]{2,1,0:T(8,128)(2,1)S(1)} %bitcast.19), channel_id=1, source_target_pairs={{0,32},{32,64},{64,96},{96,128},{128,160},{160,192},{192,224},{1,3... | collective-permute-start | bytes 1572872 | tf_op jit(solution)/shard_map/ppermute | solution.py:20
  25.0 5.2 %collective-permute-done.1 = bf16[32,8,1024]{2,1,0:T(8,128)(2,1)S(1)} collective-permute-done((bf16[32,8,1024]{2,1,0:T(8,128)(2,1)S(1)}, bf16[32,8,1024]{2,1,0:T(8,128)(2,1)S(1)}, u32[]{:S(2)}, u32[]{:S(2)}) %collective-permute-start.1) | collective-permute-done | bytes 524320 | tf_op jit(solution)/shard_map/ppermute | solution.py:20
  30.2 0.9 collective-permute-done
  31.1 1.1 pad_maximum_fusion
  32.1 1.5 %all-to-all-done = bf16[32,8,1024]{2,1,0:T(8,128)(2,1)S(1)} async-done(((bf16[32,8,1024]{2,1,0:T(8,128)(2,1)}), bf16[32,8,1024]{2,1,0:T(8,128)(2,1)S(1)}, u32[]{:S(2)}, u32[]{:S(2)}) %all-to-all-start) | async-done | bytes 524320 | tf_op jit(solution)/shard_map/all_to_all | solution.py:444
  33.7 0.0 copy-start.5
  33.7 8.1 %all-to-all-start.1 = ((bf16[32,16,1024]{2,1,0:T(8,128)(2,1)}), bf16[32,16,1024]{2,1,0:T(8,128)(2,1)S(1)}, u32[]{:S(2)}, u32[]{:S(2)}) async-start(bf16[32,16,1024]{2,1,0:T(8,128)(2,1)} %pad_maximum_fusion), calls=%async_computation.1 | async-start | bytes 2097152 | tf_op jit(solution)/shard_map/all_to_all | solution.py:452
  41.8 7.9 %phase_tables.1 = (f32[4,768,128]{2,1,0:T(8,128)}, f32[4,768,128]{2,1,0:T(8,128)}, f32[4,768,128]{2,1,0:T(8,128)}, f32[4,768,128]{2,1,0:T(8,128)}) custom-call(s32[1]{0:T(128)} %bitcast.6.base_ref, s32[4]{0:T(128)} %counts_ref.1, s32[4,512]{1,0:T(4,128)} %slot_ref.1, s32[4,512]{1,0:T(4,128)} %ping_ref.1), custom_call_target="tpu_custom_call" | custom-call | tf_op jit(solution)/shard_map/phase_tables/pallas_call | solution.py:152
  49.8 0.0 copy-done.5
  49.8 9.9 %own_forward.1 = (f32[4,256,1024]{2,1,0:T(8,128)}, f32[4,256,1024]{2,1,0:T(8,128)}, f32[4,2,8,1024]{3,2,1,0:T(8,128)}) custom-call(s32[4]{0:T(128)} %class_ref.3, bf16[256,1024]{1,0:T(8,128)(2,1)} %bitcast.22, bf16[4,1024,512]{2,1,0:T(8,128)(2,1)} %weight_hbm.1, f32[4,768,128]{2,1,0:T(8,128)} %get-tuple-element.19.base_c, ...), custom_call_target="tpu_custom_call" | custom-call | tf_op jit(solution)/shard_map/own_forward/pallas_call | solution.py:232
  59.7 9.7 %all-to-all-done.1 = bf16[32,16,1024]{2,1,0:T(8,128)(2,1)S(1)} async-done(((bf16[32,16,1024]{2,1,0:T(8,128)(2,1)}), bf16[32,16,1024]{2,1,0:T(8,128)(2,1)S(1)}, u32[]{:S(2)}, u32[]{:S(2)}) %all-to-all-start.1) | async-done | bytes 1048608 | tf_op jit(solution)/shard_map/all_to_all | solution.py:452
  69.4 0.0 copy-start.4
  69.4 1.0 copy-done.4
  70.3 0.0 copy-start.6
  70.3 18.3 %focus.1 = (f32[4,2,1024]{2,1,0:T(2,128)}, f32[6,128]{1,0:T(8,128)}) custom-call(s32[4]{0:T(128)} %class_ref.3, bf16[512,1024]{1,0:T(8,128)(2,1)} %bitcast.21, f32[4,2,8,1024]{3,2,1,0:T(8,128)} %get-tuple-element.23.sums_ref, bf16[4,1024,512]{2,1,0:T(8,128)(2,1)} %weight_hbm.1, f32[4,768,128]{2,1,0:T(8,128)} %get-tuple-element.19.base_c, ...), custom_call_target="tpu_custom_call" | custom-call | tf_op jit(solution)/shard_map/focus/pallas_call | solution.py:398
  88.7 0.7 slice.14
  89.4 0.1 reshape.60
  89.5 2.5 %collective-permute-start.3 = (f32[32,8]{1,0:T(8,128)S(1)}, f32[32,8]{1,0:T(8,128)S(1)}, u32[]{:S(2)}, u32[]{:S(2)}) collective-permute-start(f32[32,8]{1,0:T(8,128)S(1)} %bitcast.25), channel_id=1, source_target_pairs={{32,0},{64,32},{96,64},{128,96},{160,128},{192,160},{224,192},{33,... | collective-permute-start | bytes 3080 | tf_op jit(solution)/shard_map/ppermute | solution.py:20
  92.0 3.6 %collective-permute-start.2 = (f32[32,8]{1,0:T(8,128)S(1)}, f32[32,8]{1,0:T(8,128)S(1)}, u32[]{:S(2)}, u32[]{:S(2)}) collective-permute-start(f32[32,8]{1,0:T(8,128)S(1)} %bitcast.24), channel_id=1, source_target_pairs={{0,32},{32,64},{64,96},{96,128},{128,160},{160,192},{192,224},{1,3... | collective-permute-start | bytes 3080 | tf_op jit(solution)/shard_map/ppermute | solution.py:20
  95.6 0.0 copy-done.6
  95.7 0.7 slice.16
  96.4 0.1 reshape.61
  96.4 0.0 collective-permute-done.3
  96.4 0.0 collective-permute-done.2
  96.5 0.7 pad_maximum_fusion.1
  97.2 6.2 %all-to-all-start.2 = ((f32[32,1,24]{2,1,0:T(1,128)}), f32[32,1,24]{2,1,0:T(1,128)S(1)}, u32[]{:S(2)}, u32[]{:S(2)}) async-start(f32[32,1,24]{2,1,0:T(1,128)} %bitcast.10), calls=%async_computation.2 | async-start | bytes 32768 | tf_op jit(solution)/shard_map/all_to_all | solution.py:470
  103.4 8.6 %all-to-all-done.2 = f32[32,1,24]{2,1,0:T(1,128)S(1)} async-done(((f32[32,1,24]{2,1,0:T(1,128)}), f32[32,1,24]{2,1,0:T(1,128)S(1)}, u32[]{:S(2)}, u32[]{:S(2)}) %all-to-all-start.2) | async-done | bytes 3104 | tf_op jit(solution)/shard_map/all_to_all | solution.py:470
  112.0 0.1 copy.21
  112.1 0.1 copy.22
  112.1 0.1 broadcast_in_dim.15
  112.2 0.7 select_reduce_fusion
  (3 shorter events, 0.0 us)
Async XLA Ops:
  0.6 16.8 %copy-start.3 = (f32[64]{0:T(128)S(1)}, f32[64]{0:T(128)}, u32[]{:S(2)}) copy-start(f32[64]{0:T(128)} %param.9) | copy-start | bytes 772
  1.3 1.6 %copy-start = (bf16[1024,1024]{1,0:T(8,128)(2,1)S(1)}, bf16[1024,1024]{1,0:T(8,128)(2,1)}, u32[]{:S(2)}) copy-start(bf16[1024,1024]{1,0:T(8,128)(2,1)} %panels_ref.3) | copy-start | bytes 6291460
  2.9 0.7 copy-start.2
  3.6 13.8 %copy-start.1 = (bf16[1024,1024]{1,0:T(8,128)(2,1)S(1)}, bf16[1024,1024]{1,0:T(8,128)(2,1)}, u32[]{:S(2)}) copy-start(bf16[1024,1024]{1,0:T(8,128)(2,1)} %panels_ref.3) | copy-start | bytes 6291460
  5.4 28.3 %all-to-all-start = ((bf16[32,8,1024]{2,1,0:T(8,128)(2,1)}), bf16[32,8,1024]{2,1,0:T(8,128)(2,1)S(1)}, u32[]{:S(2)}, u32[]{:S(2)}) async-start(bf16[32,8,1024]{2,1,0:T(8,128)(2,1)} %bitcast.3), calls=%async_computation | async-start | bytes 1048576 | tf_op jit(solution)/shard_map/all_to_all | solution.py:444
  19.1 11.1 %collective-permute-start.1 = (bf16[32,8,1024]{2,1,0:T(8,128)(2,1)S(1)}, bf16[32,8,1024]{2,1,0:T(8,128)(2,1)S(1)}, u32[]{:S(2)}, u32[]{:S(2)}) collective-permute-start(bf16[32,8,1024]{2,1,0:T(8,128)(2,1)S(1)} %bitcast.20), channel_id=1, source_target_pairs={{32,0},{64,32},{96,64},{128,96},{160,128},{192,160},{224,192},{33,... | collective-permute-start | bytes 1572872 | tf_op jit(solution)/shard_map/ppermute | solution.py:20
  21.9 9.1 %collective-permute-start = (bf16[32,8,1024]{2,1,0:T(8,128)(2,1)S(1)}, bf16[32,8,1024]{2,1,0:T(8,128)(2,1)S(1)}, u32[]{:S(2)}, u32[]{:S(2)}) collective-permute-start(bf16[32,8,1024]{2,1,0:T(8,128)(2,1)S(1)} %bitcast.19), channel_id=1, source_target_pairs={{0,32},{32,64},{64,96},{96,128},{128,160},{160,192},{192,224},{1,3... | collective-permute-start | bytes 1572872 | tf_op jit(solution)/shard_map/ppermute | solution.py:20
  33.7 16.1 %copy-start.5 = (bf16[32,8,1024]{2,1,0:T(8,128)(2,1)}, bf16[32,8,1024]{2,1,0:T(8,128)(2,1)S(1)}, u32[]{:S(2)}) copy-start(bf16[32,8,1024]{2,1,0:T(8,128)(2,1)S(1)} %all-to-all-done) | copy-start | bytes 1572868
  33.7 35.7 %all-to-all-start.1 = ((bf16[32,16,1024]{2,1,0:T(8,128)(2,1)}), bf16[32,16,1024]{2,1,0:T(8,128)(2,1)S(1)}, u32[]{:S(2)}, u32[]{:S(2)}) async-start(bf16[32,16,1024]{2,1,0:T(8,128)(2,1)} %pad_maximum_fusion), calls=%async_computation.1 | async-start | bytes 2097152 | tf_op jit(solution)/shard_map/all_to_all | solution.py:452
  69.4 1.0 copy-start.4
  70.3 25.3 %copy-start.6 = (s32[768]{0:T(1024)S(1)}, s32[768]{0:T(1024)}, u32[]{:S(2)}) copy-start(s32[768]{0:T(1024)} %param.12) | copy-start | bytes 9220
  89.5 6.9 %collective-permute-start.3 = (f32[32,8]{1,0:T(8,128)S(1)}, f32[32,8]{1,0:T(8,128)S(1)}, u32[]{:S(2)}, u32[]{:S(2)}) collective-permute-start(f32[32,8]{1,0:T(8,128)S(1)} %bitcast.25), channel_id=1, source_target_pairs={{32,0},{64,32},{96,64},{128,96},{160,128},{192,160},{224,192},{33,... | collective-permute-start | bytes 3080 | tf_op jit(solution)/shard_map/ppermute | solution.py:20
  92.0 4.4 %collective-permute-start.2 = (f32[32,8]{1,0:T(8,128)S(1)}, f32[32,8]{1,0:T(8,128)S(1)}, u32[]{:S(2)}, u32[]{:S(2)}) collective-permute-start(f32[32,8]{1,0:T(8,128)S(1)} %bitcast.24), channel_id=1, source_target_pairs={{0,32},{32,64},{64,96},{96,128},{128,160},{160,192},{192,224},{1,3... | collective-permute-start | bytes 3080 | tf_op jit(solution)/shard_map/ppermute | solution.py:20
  97.2 14.8 %all-to-all-start.2 = ((f32[32,1,24]{2,1,0:T(1,128)}), f32[32,1,24]{2,1,0:T(1,128)S(1)}, u32[]{:S(2)}, u32[]{:S(2)}) async-start(f32[32,1,24]{2,1,0:T(1,128)} %bitcast.10), calls=%async_computation.2 | async-start | bytes 32768 | tf_op jit(solution)/shard_map/all_to_all | solution.py:470

commit v4 on v3

--- a/solution.py
+++ b/solution.py
@@ -10,7 +10,6 @@
 
 LANES = 128
 HALF = 128
-VMEM_BYTES = 24 * 1024 * 1024
 ALL_VMEM = 60 * 1024 * 1024
 
 
@@ -28,12 +27,15 @@
     return jnp.broadcast_to(row, (8, row.shape[1])).T[:, :1]
 
 
-def rotated_rows(panels_ref, phases_ref, slots):
+def rotated_rows(panels_ref, phases_ref, slots_ref, first, count):
     rows_here, width = panels_ref.shape
     bins = width // 2
     pings = phases_ref.shape[1]
-    count = slots.shape[1]
-    slot_row = column(slots.astype(jnp.float32)).astype(jnp.int32)
+    columns = [
+        column(slots_ref[pl.ds(row, 1), :].astype(jnp.float32))
+        for row in range(first // LANES, (first + count) // LANES)
+    ]
+    slot_row = jnp.concatenate(columns, axis=0).astype(jnp.int32)
     row_ids = lax.broadcasted_iota(jnp.int32, (count, rows_here), 1)
     pick = jnp.where(row_ids == slot_row, 1.0, 0.0).astype(jnp.bfloat16)
     picked = jnp.dot(pick, panels_ref[...], preferred_element_type=jnp.float32)
@@ -58,7 +60,7 @@
     def kernel(panels_ref, phases_ref, slots_ref, *outs):
         for offset, out in zip(offsets, outs):
             real_part, imag_part = rotated_rows(
-                panels_ref, phases_ref, slots_ref[:, pl.ds(offset * count, count)]
+                panels_ref, phases_ref, slots_ref, offset * count, count
             )
             out[:, :bins] = real_part
             out[:, bins:] = imag_part
@@ -66,9 +68,9 @@
     return pl.pallas_call(
         kernel,
         out_shape=[jax.ShapeDtypeStruct((count, width), jnp.bfloat16) for _ in offsets],
-        compiler_params=pltpu.CompilerParams(vmem_limit_bytes=VMEM_BYTES),
+        compiler_params=pltpu.CompilerParams(vmem_limit_bytes=ALL_VMEM),
         name="gather_rotated",
-    )(panels, phases.reshape(1, -1), slots.reshape(1, -1))
+    )(panels, phases.reshape(1, -1), slots.reshape(-1, LANES))
 
 
 def cos_sin(angle):
@@ -257,20 +259,15 @@
     chunks = mixed // chunk
 
     def focus_kernel(
-        class_ref, rows_ref, sums_ref, weight_hbm, base_c, base_s, step_c, step_s, own_r, own_i,
+        class_ref, rows_ref, sums_ref, weight_ref, base_c, base_s, step_c, step_s, own_r, own_i,
         image_ref, corr_ref, *scratch,
     ):
         proj = scratch[: 2 * chunks]
-        turned_r, turned_i, corr_acc, weight_ref = scratch[2 * chunks : 2 * chunks + 4]
+        turned_r, turned_i, corr_acc = scratch[2 * chunks : 2 * chunks + 3]
         base_cos, base_sin, step_cos, step_sin, far_r, far_i = scratch[
-            2 * chunks + 4 : 2 * chunks + 10
+            2 * chunks + 3 : 2 * chunks + 9
         ]
-        weight_sem, table_sem, own_sem = scratch[2 * chunks + 10 :]
-
-        def weight_copy(tile):
-            return pltpu.make_async_copy(
-                weight_hbm.at[class_ref[tile]], weight_ref.at[tile], weight_sem.at[tile]
-            )
+        table_sem, own_sem = scratch[2 * chunks + 9 :]
 
         def table_copies(tile):
             pairs = (base_c, base_cos), (base_s, base_sin), (step_c, step_cos), (step_s, step_sin)
@@ -288,13 +285,13 @@
             ]
 
         for tile in range(tiles):
-            for copy in [weight_copy(tile)] + table_copies(tile) + own_copies(tile):
+            for copy in table_copies(tile) + own_copies(tile):
                 copy.start()
 
         def project(tile, part):
             project_rows(
                 rows_ref, part * chunk, chunk,
-                lambda first, size: weight_ref[tile, pl.ds(first, size), :],
+                lambda first, size: weight_ref[class_ref[tile], pl.ds(first, size), :],
                 proj[2 * part], proj[2 * part + 1], bins, pixels, piece,
             )
 
@@ -327,11 +324,6 @@
                 following = tile
                 if part + 1 == chunks:
                     following = jnp.minimum(tile + 1, tiles - 1)
-
-                    @pl.when(tile + 1 < tiles)
-                    def _():
-                        weight_copy(tile + 1).wait()
-
                 project(following, (part + 1) % chunks)
                 sums = turn(tile, part, sums)
             heavy = []
@@ -376,7 +368,6 @@
             return 0
 
         corr_acc[...] = jnp.zeros_like(corr_acc)
-        weight_copy(0).wait()
         project(0, 0)
         lax.fori_loop(0, tiles, one_tile, 0)
         for part in range((mixed + own) // LANES):
@@ -397,19 +388,17 @@
     hbm = pl.BlockSpec(memory_space=pltpu.HBM)
     image, corr = pl.pallas_call(
         make_focus_kernel(mixed, own, pixels, bins, tiles, chunk, piece),
-        in_specs=[pl.BlockSpec(memory_space=pltpu.SMEM), vmem, vmem] + [hbm] * 7,
+        in_specs=[pl.BlockSpec(memory_space=pltpu.SMEM), vmem, vmem, vmem] + [hbm] * 6,
         out_specs=[vmem] * 2,
         scratch_shapes=[pltpu.VMEM((chunk, pixels), jnp.float32)] * (2 * (mixed // chunk))
         + [
             pltpu.VMEM((mixed, pixels), jnp.float32),
             pltpu.VMEM((mixed, pixels), jnp.float32),
             pltpu.VMEM((slots, LANES), jnp.float32),
-            pltpu.VMEM((tiles, pixels, bins), jnp.bfloat16),
         ]
         + [pltpu.VMEM((tiles, mixed, LANES), jnp.float32)] * 4
         + [pltpu.VMEM((tiles, own, pixels), jnp.float32)] * 2
         + [
-            pltpu.SemaphoreType.DMA((tiles,)),
             pltpu.SemaphoreType.DMA((tiles, 4)),
             pltpu.SemaphoreType.DMA((tiles, 2)),
         ],
@@ -462,13 +451,17 @@
         tile_class, arrived.reshape(2 * group, row_width), weight_tiles, tables, own_parts, group, 256
     )
 
-    partial = corr[: 2 * group].reshape(tile_devs, 2, slot_cap)
-    near = corr[2 * group :].reshape(tile_devs, slot_cap)
-    behind = shift_along(partial[:, 1], "track", 1)
-    ahead = shift_along(partial[:, 0], "track", -1)
-    back = jnp.concatenate([behind, near, ahead], axis=1)
-    back = lax.all_to_all(back, "tile", split_axis=0, concat_axis=0, tiled=True)
-    back = back.reshape(tile_devs, 3, slot_cap).transpose(1, 0, 2).reshape(1, slots)
+    mixed_corr = corr[: 2 * group].reshape(tile_devs, 2, slot_cap)
+    own_corr = corr[2 * group :].reshape(tile_devs, slot_cap)
+    track = lax.axis_index("track")
+    spread = jnp.zeros((track_devs + 2, tile_devs, slot_cap), jnp.float32)
+    spread = lax.dynamic_update_slice_in_dim(
+        spread, jnp.stack([mixed_corr[:, 0], own_corr, mixed_corr[:, 1]]), track, 0
+    )
+    spread = spread[1 : track_devs + 1].reshape(track_devs * tile_devs, slot_cap)
+    back = lax.all_to_all(spread, ("track", "tile"), split_axis=0, concat_axis=0, tiled=True)
+    back = jnp.pad(back.reshape(track_devs, tile_devs, slot_cap), ((1, 1), (0, 0), (0, 0)))
+    back = lax.dynamic_slice_in_dim(back, track, 3, 0).reshape(1, slots)
     owner = (send_slots // (panels.shape[0] // ping_local)).reshape(1, slots)
     mine = lax.broadcasted_iota(jnp.int32, (ping_local, slots), 0) == owner
     ping_gradient = jnp.sum(jnp.where(mine & (send_slots >= 0)[None, :], back, 0.0), axis=1)

time: 115 us -> 111 us (0.965); the launches traced: 113 us -> 110 us
  local copies, waits for them, and re-layouts: 5.78 us -> 3.35 us
    ppermute x4 -> x2, starting transfers between devices: 12 us -> 5.85 us  [shift_along(): return lax.ppermute(block, axis, route)]
    all_to_all x1, starting transfers between devices: 6.22 us -> 11.7 us  [on_device(): lax.all_to_all(spread, ('track', 'tile'), split_axis=0, concat_axis=0, ti...]
    pallas_call x1, Pallas kernels: 18.3 us -> 13.5 us  [focus(): pl.pallas_call(make_focus_kernel(mixed, own, pixels, bins, tiles, chunk,...]
    pallas_call x2, Pallas kernels: 3.4 us -> 7.48 us  [gather_rotated(): pl.pallas_call(kernel, out_shape=[jax.ShapeDtypeStruct((count, width), jn...]
    all_to_all x1, waiting for transfers between devices: 8.58 us -> 12.6 us  [on_device(): lax.all_to_all(spread, ('track', 'tile'), split_axis=0, concat_axis=0, ti...]
    all_to_all x1, waiting for transfers between devices: 9.66 us -> 7.3 us  [on_device(): lax.all_to_all(mixed, 'tile', split_axis=0, concat_axis=0, tiled=True)]
    unnamed x14 -> x6, local copies, waits for them, and re-layouts: 3.25 us -> 0.99 us
    all_to_all x1, waiting for transfers between devices: 1.54 us -> 0.01 us  [on_device(): lax.all_to_all(own.reshape(blocks), 'tile', split_axis=0, concat_axis=0,...]
  transfers between devices with their start and end apart: 7 -> 5, of which waited for: 5 -> 4; matrix products, arithmetic and copies ran while one was open for 2% -> 1% of each run, Pallas kernels for 17% -> 20%
where the time goes in v4:
time: 111 us; the launch traced here: 110 us
  starting transfers between devices  39.1 us (35%)
  Pallas kernels  38.8 us (35%)
  waiting for transfers between devices  26.3 us (24%)
  local copies, waits for them, and re-layouts  3.35 us (3%)
  other arithmetic  1.75 us (2%)
    pallas_call x1, Pallas kernels, focus(): pl.pallas_call(make_focus_kernel(mixed, own, pixels, bins, tiles, chunk,...  13.5 us
    all_to_all x1, waiting for transfers between devices, on_device(): lax.all_to_all(spread, ('track', 'tile'), split_axis=0, concat_axis=0, ti...  12.6 us
    all_to_all x1, starting transfers between devices, on_device(): lax.all_to_all(own.reshape(blocks), 'tile', split_axis=0, concat_axis=0,...  12 us
    all_to_all x1, starting transfers between devices, on_device(): lax.all_to_all(spread, ('track', 'tile'), split_axis=0, concat_axis=0, ti...  11.7 us
    pallas_call x1, Pallas kernels, own_forward(): pl.pallas_call(kernel, grid_spec=pltpu.PrefetchScalarGridSpec(num_scalar_...  9.98 us
    all_to_all x1, starting transfers between devices, on_device(): lax.all_to_all(mixed, 'tile', split_axis=0, concat_axis=0, tiled=True)  9.5 us
    pallas_call x1, Pallas kernels, phase_tables(): pl.pallas_call(kernel, in_specs=[smem, smem, vmem, vmem], out_specs=[vmem...  7.91 us
    pallas_call x2, Pallas kernels, gather_rotated(): pl.pallas_call(kernel, out_shape=[jax.ShapeDtypeStruct((count, width), jn...  7.48 us
  transfers between devices with their start and end apart: 5, of which 4 were waited for; matrix products, arithmetic and copies ran while one was open for 1% of the time, Pallas kernels for 20%

profile of v4, /device:TPU:1, one launch (start us, length us, event | category | flops | bytes accessed | tf_op | source)
XLA Modules:
  0.0 110.1 jit_solution(7710826077399460430)
XLA Ops:
  0.6 3.4 %gather_rotated.3 = bf16[256,1024]{1,0:T(8,128)(2,1)} custom-call(bf16[1024,1024]{1,0:T(8,128)(2,1)} %panels_ref.3, f32[1,64]{1,0:T(1,128)} %bitcast.22, s32[6,128]{1,0:T(8,128)} %bitcast.18), custom_call_target="tpu_custom_call" | custom-call | tf_op jit(solution)/shard_map/gather_rotated/pallas_call | solution.py:68
  4.0 12.0 %all-to-all-start = ((bf16[32,8,1024]{2,1,0:T(8,128)(2,1)}), bf16[32,8,1024]{2,1,0:T(8,128)(2,1)S(1)}, u32[]{:S(2)}, u32[]{:S(2)}) async-start(bf16[32,8,1024]{2,1,0:T(8,128)(2,1)} %bitcast.16), calls=%async_computation | async-start | bytes 1048576 | tf_op jit(solution)/shard_map/all_to_all | solution.py:433
  16.1 4.1 %gather_rotated.2 = (bf16[256,1024]{1,0:T(8,128)(2,1)}, bf16[256,1024]{1,0:T(8,128)(2,1)}) custom-call(bf16[1024,1024]{1,0:T(8,128)(2,1)} %panels_ref.3, f32[1,64]{1,0:T(1,128)} %bitcast.23, s32[6,128]{1,0:T(8,128)} %bitcast.19), custom_call_target="tpu_custom_call" | custom-call | tf_op jit(solution)/shard_map/gather_rotated/pallas_call | solution.py:68
  20.1 2.8 %collective-permute-start.1 = (bf16[32,8,1024]{2,1,0:T(8,128)(2,1)}, bf16[32,8,1024]{2,1,0:T(8,128)(2,1)S(1)}, u32[]{:S(2)}, u32[]{:S(2)}) collective-permute-start(bf16[32,8,1024]{2,1,0:T(8,128)(2,1)} %bitcast.25), channel_id=1, source_target_pairs={{32,0},{64,32},{96,64},{128,96},{160,128},{192,160},{224,192},{33,... | collective-permute-start | bytes 1572872 | tf_op jit(solution)/shard_map/ppermute | solution.py:19
  23.0 0.0 copy-start.2
  23.0 3.0 %collective-permute-start = (bf16[32,8,1024]{2,1,0:T(8,128)(2,1)}, bf16[32,8,1024]{2,1,0:T(8,128)(2,1)S(1)}, u32[]{:S(2)}, u32[]{:S(2)}) collective-permute-start(bf16[32,8,1024]{2,1,0:T(8,128)(2,1)} %bitcast.24), channel_id=1, source_target_pairs={{0,32},{32,64},{64,96},{96,128},{128,160},{160,192},{192,224},{1,3... | collective-permute-start | bytes 1572872 | tf_op jit(solution)/shard_map/ppermute | solution.py:19
  26.0 5.4 %collective-permute-done.1 = bf16[32,8,1024]{2,1,0:T(8,128)(2,1)S(1)} collective-permute-done((bf16[32,8,1024]{2,1,0:T(8,128)(2,1)}, bf16[32,8,1024]{2,1,0:T(8,128)(2,1)S(1)}, u32[]{:S(2)}, u32[]{:S(2)}) %collective-permute-start.1) | collective-permute-done | bytes 524320 | tf_op jit(solution)/shard_map/ppermute | solution.py:19
  31.4 1.0 collective-permute-done
  32.5 1.1 pad_maximum_fusion
  33.5 0.0 all-to-all-done
  33.5 0.0 copy-start.1
  33.5 9.5 %all-to-all-start.1 = ((bf16[32,16,1024]{2,1,0:T(8,128)(2,1)}), bf16[32,16,1024]{2,1,0:T(8,128)(2,1)S(1)}, u32[]{:S(2)}, u32[]{:S(2)}) async-start(bf16[32,16,1024]{2,1,0:T(8,128)(2,1)} %pad_maximum_fusion), calls=%async_computation.1 | async-start | bytes 2097152 | tf_op jit(solution)/shard_map/all_to_all | solution.py:441
  43.0 7.9 %phase_tables.1 = (f32[4,768,128]{2,1,0:T(8,128)}, f32[4,768,128]{2,1,0:T(8,128)}, f32[4,768,128]{2,1,0:T(8,128)}, f32[4,768,128]{2,1,0:T(8,128)}) custom-call(s32[1]{0:T(128)} %bitcast.7.base_ref, s32[4]{0:T(128)} %counts_ref.1, s32[4,512]{1,0:T(4,128)} %slot_ref.1, s32[4,512]{1,0:T(4,128)} %ping_ref.1), custom_call_target="tpu_custom_call" | custom-call | tf_op jit(solution)/shard_map/phase_tables/pallas_call | solution.py:154
  51.0 0.0 copy-done.2
  51.0 0.0 copy-done.1
  51.0 10.0 %own_forward.1 = (f32[4,256,1024]{2,1,0:T(8,128)}, f32[4,256,1024]{2,1,0:T(8,128)}, f32[4,2,8,1024]{3,2,1,0:T(8,128)}) custom-call(s32[4]{0:T(128)} %class_ref.3, bf16[256,1024]{1,0:T(8,128)(2,1)} %bitcast.15, bf16[4,1024,512]{2,1,0:T(8,128)(2,1)} %weight_ref.3, f32[4,768,128]{2,1,0:T(8,128)} %get-tuple-element.19.base_c, ...), custom_call_target="tpu_custom_call" | custom-call | tf_op jit(solution)/shard_map/own_forward/pallas_call | solution.py:234
  61.0 7.3 %all-to-all-done.1 = bf16[32,16,1024]{2,1,0:T(8,128)(2,1)S(1)} async-done(((bf16[32,16,1024]{2,1,0:T(8,128)(2,1)}), bf16[32,16,1024]{2,1,0:T(8,128)(2,1)S(1)}, u32[]{:S(2)}, u32[]{:S(2)}) %all-to-all-start.1) | async-done | bytes 1048608 | tf_op jit(solution)/shard_map/all_to_all | solution.py:441
  68.3 0.0 copy-start
  68.3 1.0 copy-done
  69.2 13.5 %focus.1 = (f32[4,2,1024]{2,1,0:T(2,128)}, f32[6,128]{1,0:T(8,128)}) custom-call(s32[4]{0:T(128)} %class_ref.3, bf16[512,1024]{1,0:T(8,128)(2,1)} %bitcast.14, f32[4,2,8,1024]{3,2,1,0:T(8,128)} %get-tuple-element.23.sums_ref, bf16[4,1024,512]{2,1,0:T(8,128)(2,1)} %weight_ref.3, f32[4,768,128]{2,1,0:T(8,128)} %get-tuple-element.19.base_c, ...), custom_call_target="tpu_custom_call" | custom-call | tf_op jit(solution)/shard_map/focus/pallas_call | solution.py:389
  82.7 0.7 slice.17
  83.4 0.7 slice.19
  84.1 0.1 reshape.59
  84.2 0.1 stack_reshape.3
  84.4 0.7 slice.24
  85.0 11.7 %all-to-all-start.2 = ((f32[256,1,8]{2,1,0:T(1,128)}), f32[256,1,8]{2,1,0:T(1,128)S(1)}, u32[]{:S(2)}, u32[]{:S(2)}) async-start(f32[256,1,8]{2,1,0:T(1,128)} %bitcast.10), calls=%async_computation.2 | async-start | bytes 262144 | tf_op jit(solution)/shard_map/all_to_all | solution.py:462
  96.8 12.6 %all-to-all-done.2 = f32[256,1,8]{2,1,0:T(1,128)S(1)} async-done(((f32[256,1,8]{2,1,0:T(1,128)}), f32[256,1,8]{2,1,0:T(1,128)S(1)}, u32[]{:S(2)}, u32[]{:S(2)}) %all-to-all-start.2) | async-done | bytes 8224 | tf_op jit(solution)/shard_map/all_to_all | solution.py:462
  109.4 0.1 broadcast_in_dim.19
  109.5 0.7 select_reduce_fusion
  (6 shorter events, 0.1 us)
Async XLA Ops:
  4.0 29.5 %all-to-all-start = ((bf16[32,8,1024]{2,1,0:T(8,128)(2,1)}), bf16[32,8,1024]{2,1,0:T(8,128)(2,1)S(1)}, u32[]{:S(2)}, u32[]{:S(2)}) async-start(bf16[32,8,1024]{2,1,0:T(8,128)(2,1)} %bitcast.16), calls=%async_computation | async-start | bytes 1048576 | tf_op jit(solution)/shard_map/all_to_all | solution.py:433
  20.1 11.3 %collective-permute-start.1 = (bf16[32,8,1024]{2,1,0:T(8,128)(2,1)}, bf16[32,8,1024]{2,1,0:T(8,128)(2,1)S(1)}, u32[]{:S(2)}, u32[]{:S(2)}) collective-permute-start(bf16[32,8,1024]{2,1,0:T(8,128)(2,1)} %bitcast.25), channel_id=1, source_target_pairs={{32,0},{64,32},{96,64},{128,96},{160,128},{192,160},{224,192},{33,... | collective-permute-start | bytes 1572872 | tf_op jit(solution)/shard_map/ppermute | solution.py:19
  23.0 28.0 %copy-start.2 = (s32[768]{0:T(1024)S(1)}, s32[768]{0:T(1024)}, u32[]{:S(2)}) copy-start(s32[768]{0:T(1024)} %param.12) | copy-start | bytes 9220
  23.0 9.4 %collective-permute-start = (bf16[32,8,1024]{2,1,0:T(8,128)(2,1)}, bf16[32,8,1024]{2,1,0:T(8,128)(2,1)S(1)}, u32[]{:S(2)}, u32[]{:S(2)}) collective-permute-start(bf16[32,8,1024]{2,1,0:T(8,128)(2,1)} %bitcast.24), channel_id=1, source_target_pairs={{0,32},{32,64},{64,96},{96,128},{128,160},{160,192},{192,224},{1,3... | collective-permute-start | bytes 1572872 | tf_op jit(solution)/shard_map/ppermute | solution.py:19
  33.5 17.4 %copy-start.1 = (bf16[32,8,1024]{2,1,0:T(8,128)(2,1)}, bf16[32,8,1024]{2,1,0:T(8,128)(2,1)S(1)}, u32[]{:S(2)}) copy-start(bf16[32,8,1024]{2,1,0:T(8,128)(2,1)S(1)} %all-to-all-done) | copy-start | bytes 1572868
  33.5 34.7 %all-to-all-start.1 = ((bf16[32,16,1024]{2,1,0:T(8,128)(2,1)}), bf16[32,16,1024]{2,1,0:T(8,128)(2,1)S(1)}, u32[]{:S(2)}, u32[]{:S(2)}) async-start(bf16[32,16,1024]{2,1,0:T(8,128)(2,1)} %pad_maximum_fusion), calls=%async_computation.1 | async-start | bytes 2097152 | tf_op jit(solution)/shard_map/all_to_all | solution.py:441
  68.3 1.0 copy-start
  85.0 24.3 %all-to-all-start.2 = ((f32[256,1,8]{2,1,0:T(1,128)}), f32[256,1,8]{2,1,0:T(1,128)S(1)}, u32[]{:S(2)}, u32[]{:S(2)}) async-start(f32[256,1,8]{2,1,0:T(1,128)} %bitcast.10), calls=%async_computation.2 | async-start | bytes 262144 | tf_op jit(solution)/shard_map/all_to_all | solution.py:462

commit v5 on v4

--- a/solution.py
+++ b/solution.py
@@ -200,7 +200,7 @@
     blocks = pixels // LANES
     block_at = first_slot // count
 
-    def kernel(class_ref, rows_ref, weight_ref, base_c, base_s, step_c, step_s, turned_r, turned_i, sums_ref, proj_r, proj_i):
+    def kernel(class_ref, rows_ref, weight_ref, base_c, base_s, step_c, step_s, turned_r, turned_i, proj_r, proj_i):
         project_rows(
             rows_ref, 0, count, lambda first, size: weight_ref[0, pl.ds(first, size), :],
             proj_r, proj_i, bins, pixels, pixels,
@@ -226,11 +226,13 @@
         sums = lax.fori_loop(0, count // 8, group, sums, unroll=4)
         for b in range(blocks):
             for half in range(2):
-                sums_ref[0, half, :, pl.ds(b * LANES, LANES)] = sums[2 * b + half]
+                total = jnp.sum(sums[2 * b + half], axis=0, keepdims=True)
+                store = turned_i if half else turned_r
+                store[0, pl.ds(count, 8), pl.ds(b * LANES, LANES)] = jnp.broadcast_to(total, (8, LANES))
 
     table_spec = pl.BlockSpec((1, count, LANES), lambda t, *_: (t, block_at, 0))
-    turned = jax.ShapeDtypeStruct((tiles, count, pixels), jnp.float32)
-    turned_spec = pl.BlockSpec((1, count, pixels), lambda t, *_: (t, 0, 0))
+    turned = jax.ShapeDtypeStruct((tiles, count + 8, pixels), jnp.float32)
+    turned_spec = pl.BlockSpec((1, count + 8, pixels), lambda t, *_: (t, 0, 0))
     return pl.pallas_call(
         kernel,
         grid_spec=pltpu.PrefetchScalarGridSpec(
@@ -241,25 +243,21 @@
                 pl.BlockSpec((1, pixels, bins), lambda t, cls: (cls[t], 0, 0)),
             ]
             + [table_spec] * 4,
-            out_specs=[
-                turned_spec,
-                turned_spec,
-                pl.BlockSpec((1, 2, 8, pixels), lambda t, *_: (t, 0, 0, 0)),
-            ],
+            out_specs=[turned_spec, turned_spec],
             scratch_shapes=[pltpu.VMEM((count, pixels), jnp.float32)] * 2,
         ),
-        out_shape=[turned, turned, jax.ShapeDtypeStruct((tiles, 2, 8, pixels), jnp.float32)],
+        out_shape=[turned, turned],
         compiler_params=pltpu.CompilerParams(vmem_limit_bytes=ALL_VMEM),
         name="own_forward",
     )(tile_class, own, weight_tiles, *tables)
 
 
-def make_focus_kernel(mixed, own, pixels, bins, tiles, chunk, piece):
+def make_focus_kernel(mixed, own, pixels, bins, tiles, chunk, piece, tracks, cap):
     blocks = pixels // LANES
     chunks = mixed // chunk
 
     def focus_kernel(
-        class_ref, rows_ref, sums_ref, weight_ref, base_c, base_s, step_c, step_s, own_r, own_i,
+        class_ref, track_ref, rows_ref, weight_ref, base_c, base_s, step_c, step_s, own_r, own_i,
         image_ref, corr_ref, *scratch,
     ):
         proj = scratch[: 2 * chunks]
@@ -288,12 +286,17 @@
             for copy in table_copies(tile) + own_copies(tile):
                 copy.start()
 
-        def project(tile, part):
-            project_rows(
-                rows_ref, part * chunk, chunk,
-                lambda first, size: weight_ref[class_ref[tile], pl.ds(first, size), :],
-                proj[2 * part], proj[2 * part + 1], bins, pixels, piece,
-            )
+        pieces = 2 * (pixels // piece)
+
+        def project(tile, part, low, high):
+            for index in range(low, high):
+                first, half = (index // 2) * piece, index % 2
+                proj[2 * part + half][:, pl.ds(first, piece)] = lax.dot_general(
+                    rows_ref[pl.ds(part * chunk, chunk), pl.ds(half * bins, bins)],
+                    weight_ref[class_ref[tile], pl.ds(first, piece), :],
+                    (((1,), (1,)), ((), ())),
+                    preferred_element_type=jnp.float32,
+                )
 
         def turn(tile, part, sums):
             for group in range(chunk // 8):
@@ -314,81 +317,75 @@
             return sums
 
         def one_tile(tile, _):
-            sums = []
-            for b in range(blocks):
-                for half in range(2):
-                    sums.append(sums_ref[tile, half, :, pl.ds(b * LANES, LANES)])
+            sums = [jnp.zeros((8, LANES), jnp.float32)] * (2 * blocks)
             for copy in table_copies(tile):
                 copy.wait()
             for part in range(chunks):
-                following = tile
-                if part + 1 == chunks:
-                    following = jnp.minimum(tile + 1, tiles - 1)
-                project(following, (part + 1) % chunks)
+                last = part + 1 == chunks
+                following = jnp.minimum(tile + 1, tiles - 1) if last else tile
+                project(following, (part + 1) % chunks, 0, pieces)
                 sums = turn(tile, part, sums)
+            for copy in own_copies(tile):
+                copy.wait()
             heavy = []
             for b in range(blocks):
                 lanes = pl.ds(b * LANES, LANES)
-                real = jnp.sum(sums[2 * b], axis=0, keepdims=True)
-                imag = jnp.sum(sums[2 * b + 1], axis=0, keepdims=True)
+                real = far_r[tile, own : own + 1, lanes] + jnp.sum(sums[2 * b], axis=0, keepdims=True)
+                imag = far_i[tile, own : own + 1, lanes] + jnp.sum(sums[2 * b + 1], axis=0, keepdims=True)
                 image_ref[tile, 0:1, lanes] = real
                 image_ref[tile, 1:2, lanes] = imag
                 intensity = real * real + imag * imag
                 heavy.append(jnp.broadcast_to(intensity * real, (8, LANES)))
                 heavy.append(jnp.broadcast_to(intensity * imag, (8, LANES)))
-            for copy in own_copies(tile):
-                copy.wait()
-
-            def pull(i, _, real_of, imag_of, first):
-                row = pl.multiple_of(i * 8, 8)
-                at = pl.ds(pl.multiple_of(first + i * 8, 8), 8)
+            for group in range((mixed + own) // 8):
+                at = pl.ds(group * 8, 8)
                 total = corr_acc[at, :]
                 for b in range(blocks):
                     lanes = pl.ds(b * LANES, LANES)
-                    total = total + (
-                        real_of(row, lanes) * heavy[2 * b + 1] - imag_of(row, lanes) * heavy[2 * b]
-                    )
+                    if group * 8 < mixed:
+                        real, imag = turned_r[at, lanes], turned_i[at, lanes]
+                    else:
+                        near = pl.ds(group * 8 - mixed, 8)
+                        real, imag = far_r[tile, near, lanes], far_i[tile, near, lanes]
+                    total = total + (real * heavy[2 * b + 1] - imag * heavy[2 * b])
                 corr_acc[at, :] = total
-                return 0
-
-            near = functools.partial(
-                pull,
-                real_of=lambda row, lanes: turned_r[pl.ds(row, 8), lanes],
-                imag_of=lambda row, lanes: turned_i[pl.ds(row, 8), lanes],
-                first=0,
-            )
-            far = functools.partial(
-                pull,
-                real_of=lambda row, lanes: far_r[tile, pl.ds(row, 8), lanes],
-                imag_of=lambda row, lanes: far_i[tile, pl.ds(row, 8), lanes],
-                first=mixed,
-            )
-            lax.fori_loop(0, mixed // 8, near, 0, unroll=4)
-            lax.fori_loop(0, own // 8, far, 0, unroll=4)
             return 0
 
         corr_acc[...] = jnp.zeros_like(corr_acc)
-        project(0, 0)
+        project(0, 0, 0, pieces)
         lax.fori_loop(0, tiles, one_tile, 0)
-        for part in range((mixed + own) // LANES):
-            block = corr_acc[pl.ds(part * LANES, LANES), :]
-            corr_ref[pl.ds(part, 1), :] = jnp.sum(block.T, axis=0, keepdims=True)
+        totals = jnp.sum(corr_acc[...], axis=1, keepdims=True)
+        row = lax.broadcasted_iota(jnp.int32, (mixed + own, LANES), 0)
+        lane = lax.broadcasted_iota(jnp.int32, (mixed + own, LANES), 1)
+        placed = jnp.where(row % cap == lane, totals, 0.0)
+        placed = jnp.sum(placed.reshape((mixed + own) // cap, cap, LANES), axis=1)
+        corr_acc[pl.ds(0, (mixed + own) // cap), :] = placed
+        corr_ref[...] = jnp.zeros_like(corr_ref)
+        track = track_ref[0]
+        sources = own // cap
+        cuts = (pl.ds(0, sources, stride=2), pl.ds(2 * sources, sources), pl.ds(1, sources, stride=2))
+        for k, cut in enumerate(cuts):
+
+            @pl.when((track + k >= 1) & (track + k <= tracks))
+            def _(k=k, cut=cut):
+                target = pl.ds(pl.multiple_of((track + k - 1) * sources, sources), sources)
+                corr_ref[target, :] = corr_acc[cut, :][:, :cap]
 
     return focus_kernel
 
 
-def focus(tile_class, arrived, weight_tiles, tables, own_parts, chunk, piece):
-    turned_own_r, turned_own_i, own_sums = own_parts
+def focus(tile_class, track, arrived, weight_tiles, tables, own_parts, chunk, piece, tracks, cap):
+    turned_own_r, turned_own_i = own_parts
     mixed, _ = arrived.shape
-    own = turned_own_r.shape[1]
+    own = turned_own_r.shape[1] - 8
     slots = mixed + own
     _, pixels, bins = weight_tiles.shape
     tiles = tile_class.shape[0]
     vmem = pl.BlockSpec(memory_space=pltpu.VMEM)
     hbm = pl.BlockSpec(memory_space=pltpu.HBM)
     image, corr = pl.pallas_call(
-        make_focus_kernel(mixed, own, pixels, bins, tiles, chunk, piece),
-        in_specs=[pl.BlockSpec(memory_space=pltpu.SMEM), vmem, vmem, vmem] + [hbm] * 6,
+        make_focus_kernel(mixed, own, pixels, bins, tiles, chunk, piece, tracks, cap),
+        in_specs=[pl.BlockSpec(memory_space=pltpu.SMEM)] * 2 + [vmem] * 2 + [hbm] * 6,
         out_specs=[vmem] * 2,
         scratch_shapes=[pltpu.VMEM((chunk, pixels), jnp.float32)] * (2 * (mixed // chunk))
         + [
@@ -397,19 +394,19 @@
             pltpu.VMEM((slots, LANES), jnp.float32),
         ]
         + [pltpu.VMEM((tiles, mixed, LANES), jnp.float32)] * 4
-        + [pltpu.VMEM((tiles, own, pixels), jnp.float32)] * 2
+        + [pltpu.VMEM((tiles, own + 8, pixels), jnp.float32)] * 2
         + [
             pltpu.SemaphoreType.DMA((tiles, 4)),
             pltpu.SemaphoreType.DMA((tiles, 2)),
         ],
         out_shape=[
             jax.ShapeDtypeStruct((tiles, 2, pixels), jnp.float32),
-            jax.ShapeDtypeStruct((slots // LANES, LANES), jnp.float32),
+            jax.ShapeDtypeStruct((tracks * own // cap, cap), jnp.float32),
         ],
-        compiler_params=pltpu.CompilerParams(vmem_limit_bytes=ALL_VMEM),
+        compiler_params=pltpu.CompilerParams(vmem_limit_bytes=52 * 1024 * 1024),
         name="focus",
-    )(tile_class, arrived, own_sums, weight_tiles, *tables, turned_own_r, turned_own_i)
-    return image, corr.reshape(slots)
+    )(tile_class, track, arrived, weight_tiles, *tables, turned_own_r, turned_own_i)
+    return image, corr
 
 
 def on_device(
@@ -447,19 +444,12 @@
     own_parts = own_forward(
         tile_class, own_arrived.reshape(group, row_width), weight_tiles, tables, 2 * group
     )
+    track = lax.axis_index("track")
     image, corr = focus(
-        tile_class, arrived.reshape(2 * group, row_width), weight_tiles, tables, own_parts, group, 256
-    )
-
-    mixed_corr = corr[: 2 * group].reshape(tile_devs, 2, slot_cap)
-    own_corr = corr[2 * group :].reshape(tile_devs, slot_cap)
-    track = lax.axis_index("track")
-    spread = jnp.zeros((track_devs + 2, tile_devs, slot_cap), jnp.float32)
-    spread = lax.dynamic_update_slice_in_dim(
-        spread, jnp.stack([mixed_corr[:, 0], own_corr, mixed_corr[:, 1]]), track, 0
-    )
-    spread = spread[1 : track_devs + 1].reshape(track_devs * tile_devs, slot_cap)
-    back = lax.all_to_all(spread, ("track", "tile"), split_axis=0, concat_axis=0, tiled=True)
+        tile_class, track.astype(jnp.int32).reshape(1), arrived.reshape(2 * group, row_width),
+        weight_tiles, tables, own_parts, group, 256, track_devs, slot_cap,
+    )
+    back = lax.all_to_all(corr, ("track", "tile"), split_axis=0, concat_axis=0, tiled=True)
     back = jnp.pad(back.reshape(track_devs, tile_devs, slot_cap), ((1, 1), (0, 0), (0, 0)))
     back = lax.dynamic_slice_in_dim(back, track, 3, 0).reshape(1, slots)
     owner = (send_slots // (panels.shape[0] // ping_local)).reshape(1, slots)

time: 111 us -> 106 us (0.955)
  local copies, waits for them, and re-layouts: 3.35 us -> 0.11 us
    slice x4 -> x0, local copies, waits for them, and re-layouts: 2.06 us -> none  [the longest x1 0.68 us: on_device(): mixed_corr = corr[:2 * group].reshape(tile_devs, 2, slot_cap)]
    pallas_call x1, Pallas kernels: 13.5 us -> 12.2 us  [focus(): pl.pallas_call(make_focus_kernel(mixed, own, pixels, bins, tiles, chunk,...]
  transfers between devices with their start and end apart: 5 -> 5, of which waited for: 4 -> 4; matrix products, arithmetic and copies ran while one was open for 1% -> 1% of each run, Pallas kernels for 20% -> 21%
where the time goes in v5:
time: 106 us
  starting transfers between devices  39.1 us (37%)
  Pallas kernels  37.8 us (36%)
  waiting for transfers between devices  26.2 us (25%)
  other arithmetic  1.77 us (2%)
    all_to_all x1, waiting for transfers between devices, on_device(): lax.all_to_all(corr, ('track', 'tile'), split_axis=0, concat_axis=0, tile...  12.6 us
    pallas_call x1, Pallas kernels, focus(): pl.pallas_call(make_focus_kernel(mixed, own, pixels, bins, tiles, chunk,...  12.2 us
    all_to_all x1, starting transfers between devices, on_device(): lax.all_to_all(own.reshape(blocks), 'tile', split_axis=0, concat_axis=0,...  12 us
    all_to_all x1, starting transfers between devices, on_device(): lax.all_to_all(corr, ('track', 'tile'), split_axis=0, concat_axis=0, tile...  11.7 us
    pallas_call x1, Pallas kernels, own_forward(): pl.pallas_call(kernel, grid_spec=pltpu.PrefetchScalarGridSpec(num_scalar_...  10.2 us
    all_to_all x1, starting transfers between devices, on_device(): lax.all_to_all(mixed, 'tile', split_axis=0, concat_axis=0, tiled=True)  9.5 us
    pallas_call x1, Pallas kernels, phase_tables(): pl.pallas_call(kernel, in_specs=[smem, smem, vmem, vmem], out_specs=[vmem...  7.9 us
    pallas_call x2, Pallas kernels, gather_rotated(): pl.pallas_call(kernel, out_shape=[jax.ShapeDtypeStruct((count, width), jn...  7.47 us
  transfers between devices with their start and end apart: 5, of which 4 were waited for; matrix products, arithmetic and copies ran while one was open for 1% of the time, Pallas kernels for 21%

profile of v5, /device:TPU:1, one launch (start us, length us, event | category | flops | bytes accessed | tf_op | source)
XLA Modules:
  0.0 105.6 jit_solution(2353057291723303122)
XLA Ops:
  0.6 3.4 %gather_rotated.3 = bf16[256,1024]{1,0:T(8,128)(2,1)} custom-call(bf16[1024,1024]{1,0:T(8,128)(2,1)} %panels_ref.3, f32[1,64]{1,0:T(1,128)} %bitcast.19, s32[6,128]{1,0:T(8,128)} %bitcast.17), custom_call_target="tpu_custom_call" | custom-call | tf_op jit(solution)/shard_map/gather_rotated/pallas_call | solution.py:68
  4.0 12.0 %all-to-all-start = ((bf16[32,8,1024]{2,1,0:T(8,128)(2,1)}), bf16[32,8,1024]{2,1,0:T(8,128)(2,1)S(1)}, u32[]{:S(2)}, u32[]{:S(2)}) async-start(bf16[32,8,1024]{2,1,0:T(8,128)(2,1)} %bitcast.15), calls=%async_computation | async-start | bytes 1048576 | tf_op jit(solution)/shard_map/all_to_all | solution.py:430
  16.1 4.1 %gather_rotated.2 = (bf16[256,1024]{1,0:T(8,128)(2,1)}, bf16[256,1024]{1,0:T(8,128)(2,1)}) custom-call(bf16[1024,1024]{1,0:T(8,128)(2,1)} %panels_ref.3, f32[1,64]{1,0:T(1,128)} %bitcast.20, s32[6,128]{1,0:T(8,128)} %bitcast.18), custom_call_target="tpu_custom_call" | custom-call | tf_op jit(solution)/shard_map/gather_rotated/pallas_call | solution.py:68
  20.1 2.8 %collective-permute-start.1 = (bf16[32,8,1024]{2,1,0:T(8,128)(2,1)}, bf16[32,8,1024]{2,1,0:T(8,128)(2,1)S(1)}, u32[]{:S(2)}, u32[]{:S(2)}) collective-permute-start(bf16[32,8,1024]{2,1,0:T(8,128)(2,1)} %bitcast.22), channel_id=1, source_target_pairs={{32,0},{64,32},{96,64},{128,96},{160,128},{192,160},{224,192},{33,... | collective-permute-start | bytes 1572872 | tf_op jit(solution)/shard_map/ppermute | solution.py:19
  23.0 0.0 copy-start.2
  23.0 3.0 %collective-permute-start = (bf16[32,8,1024]{2,1,0:T(8,128)(2,1)}, bf16[32,8,1024]{2,1,0:T(8,128)(2,1)S(1)}, u32[]{:S(2)}, u32[]{:S(2)}) collective-permute-start(bf16[32,8,1024]{2,1,0:T(8,128)(2,1)} %bitcast.21), channel_id=1, source_target_pairs={{0,32},{32,64},{64,96},{96,128},{128,160},{160,192},{192,224},{1,3... | collective-permute-start | bytes 1572872 | tf_op jit(solution)/shard_map/ppermute | solution.py:19
  26.0 5.4 %collective-permute-done.1 = bf16[32,8,1024]{2,1,0:T(8,128)(2,1)S(1)} collective-permute-done((bf16[32,8,1024]{2,1,0:T(8,128)(2,1)}, bf16[32,8,1024]{2,1,0:T(8,128)(2,1)S(1)}, u32[]{:S(2)}, u32[]{:S(2)}) %collective-permute-start.1) | collective-permute-done | bytes 524320 | tf_op jit(solution)/shard_map/ppermute | solution.py:19
  31.4 1.0 collective-permute-done
  32.4 1.1 %pad_maximum_fusion = bf16[32,16,1024]{2,1,0:T(8,128)(2,1)} fusion(bf16[32,8,1024]{2,1,0:T(8,128)(2,1)S(1)} %collective-permute-done.1, bf16[32,8,1024]{2,1,0:T(8,128)(2,1)S(1)} %collective-permute-done), kind=kLoop, calls=%fused_computation | loop fusion | flops 2097152 | bytes 2097152 | tf_op jit(solution)/shard_map/concatenate | solution.py:436
  33.5 0.0 all-to-all-done
  33.5 0.0 copy-start.1
  33.6 9.5 %all-to-all-start.1 = ((bf16[32,16,1024]{2,1,0:T(8,128)(2,1)}), bf16[32,16,1024]{2,1,0:T(8,128)(2,1)S(1)}, u32[]{:S(2)}, u32[]{:S(2)}) async-start(bf16[32,16,1024]{2,1,0:T(8,128)(2,1)} %pad_maximum_fusion), calls=%async_computation.1 | async-start | bytes 2097152 | tf_op jit(solution)/shard_map/all_to_all | solution.py:438
  43.1 7.9 %phase_tables.1 = (f32[4,768,128]{2,1,0:T(8,128)}, f32[4,768,128]{2,1,0:T(8,128)}, f32[4,768,128]{2,1,0:T(8,128)}, f32[4,768,128]{2,1,0:T(8,128)}) custom-call(s32[1]{0:T(128)} %bitcast.7.base_ref, s32[4]{0:T(128)} %counts_ref.1, s32[4,512]{1,0:T(4,128)} %slot_ref.1, s32[4,512]{1,0:T(4,128)} %ping_ref.1), custom_call_target="tpu_custom_call" | custom-call | tf_op jit(solution)/shard_map/phase_tables/pallas_call | solution.py:154
  51.0 0.0 copy-done.2
  51.0 0.0 copy-done.1
  51.0 0.0 copy-start
  51.0 10.2 %own_forward.1 = (f32[4,264,1024]{2,1,0:T(8,128)}, f32[4,264,1024]{2,1,0:T(8,128)}) custom-call(s32[4]{0:T(128)} %class_ref.3, bf16[256,1024]{1,0:T(8,128)(2,1)} %bitcast.14, bf16[4,1024,512]{2,1,0:T(8,128)(2,1)} %weight_ref.3, f32[4,768,128]{2,1,0:T(8,128)} %get-tuple-element.17.base_c, f32[4,768,128]{2,1,0:T(8,128)} %get-tuple-element.18.base_s, ...), custom_call_target="tpu_custom_call" | custom-call | tf_op jit(solution)/shard_map/own_forward/pallas_call | solution.py:236
  61.2 7.2 %all-to-all-done.1 = bf16[32,16,1024]{2,1,0:T(8,128)(2,1)S(1)} async-done(((bf16[32,16,1024]{2,1,0:T(8,128)(2,1)}), bf16[32,16,1024]{2,1,0:T(8,128)(2,1)S(1)}, u32[]{:S(2)}, u32[]{:S(2)}) %all-to-all-start.1) | async-done | bytes 1048608 | tf_op jit(solution)/shard_map/all_to_all | solution.py:438
  68.4 0.0 copy-done
  68.4 12.2 %focus.1 = (f32[4,2,1024]{2,1,0:T(2,128)}, f32[256,8]{1,0:T(8,128)}) custom-call(s32[4]{0:T(128)S(1)} %copy-done, s32[1]{0:T(128)} %bitcast.track_ref, bf16[512,1024]{1,0:T(8,128)(2,1)S(1)} %bitcast.13, bf16[4,1024,512]{2,1,0:T(8,128)(2,1)} %weight_ref.3, f32[4,768,128]{2,1,0:T(8,128)} %get-tuple-element.17.base_c, f32[4,768,128]{2,1,0:T(8,128)} %get-tuple-element.18.base_s, ...), custom_call_target="tpu_custom_call" | custom-call | tf_op jit(solution)/shard_map/focus/pallas_call | solution.py:386
  80.6 11.7 %all-to-all-start.2 = ((f32[256,1,8]{2,1,0:T(1,128)}), f32[256,1,8]{2,1,0:T(1,128)S(1)}, u32[]{:S(2)}, u32[]{:S(2)}) async-start(f32[256,1,8]{2,1,0:T(1,128)} %bitcast.10), calls=%async_computation.2 | async-start | bytes 262144 | tf_op jit(solution)/shard_map/all_to_all | solution.py:452
  92.3 12.6 %all-to-all-done.2 = f32[256,1,8]{2,1,0:T(1,128)S(1)} async-done(((f32[256,1,8]{2,1,0:T(1,128)}), f32[256,1,8]{2,1,0:T(1,128)S(1)}, u32[]{:S(2)}, u32[]{:S(2)}) %all-to-all-start.2) | async-done | bytes 8224 | tf_op jit(solution)/shard_map/all_to_all | solution.py:452
  104.9 0.1 broadcast_in_dim.15
  105.0 0.7 select_reduce_fusion
  (3 shorter events, 0.0 us)
Async XLA Ops:
  4.0 29.5 %all-to-all-start = ((bf16[32,8,1024]{2,1,0:T(8,128)(2,1)}), bf16[32,8,1024]{2,1,0:T(8,128)(2,1)S(1)}, u32[]{:S(2)}, u32[]{:S(2)}) async-start(bf16[32,8,1024]{2,1,0:T(8,128)(2,1)} %bitcast.15), calls=%async_computation | async-start | bytes 1048576 | tf_op jit(solution)/shard_map/all_to_all | solution.py:430
  20.1 11.3 %collective-permute-start.1 = (bf16[32,8,1024]{2,1,0:T(8,128)(2,1)}, bf16[32,8,1024]{2,1,0:T(8,128)(2,1)S(1)}, u32[]{:S(2)}, u32[]{:S(2)}) collective-permute-start(bf16[32,8,1024]{2,1,0:T(8,128)(2,1)} %bitcast.22), channel_id=1, source_target_pairs={{32,0},{64,32},{96,64},{128,96},{160,128},{192,160},{224,192},{33,... | collective-permute-start | bytes 1572872 | tf_op jit(solution)/shard_map/ppermute | solution.py:19
  23.0 28.0 %copy-start.2 = (s32[768]{0:T(1024)S(1)}, s32[768]{0:T(1024)}, u32[]{:S(2)}) copy-start(s32[768]{0:T(1024)} %param.12) | copy-start | bytes 9220
  23.0 9.4 %collective-permute-start = (bf16[32,8,1024]{2,1,0:T(8,128)(2,1)}, bf16[32,8,1024]{2,1,0:T(8,128)(2,1)S(1)}, u32[]{:S(2)}, u32[]{:S(2)}) collective-permute-start(bf16[32,8,1024]{2,1,0:T(8,128)(2,1)} %bitcast.21), channel_id=1, source_target_pairs={{0,32},{32,64},{64,96},{96,128},{128,160},{160,192},{192,224},{1,3... | collective-permute-start | bytes 1572872 | tf_op jit(solution)/shard_map/ppermute | solution.py:19
  33.5 17.4 %copy-start.1 = (bf16[32,8,1024]{2,1,0:T(8,128)(2,1)}, bf16[32,8,1024]{2,1,0:T(8,128)(2,1)S(1)}, u32[]{:S(2)}) copy-start(bf16[32,8,1024]{2,1,0:T(8,128)(2,1)S(1)} %all-to-all-done) | copy-start | bytes 1572868
  33.6 34.8 %all-to-all-start.1 = ((bf16[32,16,1024]{2,1,0:T(8,128)(2,1)}), bf16[32,16,1024]{2,1,0:T(8,128)(2,1)S(1)}, u32[]{:S(2)}, u32[]{:S(2)}) async-start(bf16[32,16,1024]{2,1,0:T(8,128)(2,1)} %pad_maximum_fusion), calls=%async_computation.1 | async-start | bytes 2097152 | tf_op jit(solution)/shard_map/all_to_all | solution.py:438
  51.0 17.4 %copy-start = (s32[4]{0:T(128)S(1)}, s32[4]{0:T(128)}, u32[]{:S(2)}) copy-start(s32[4]{0:T(128)} %class_ref.3) | copy-start | bytes 52
  80.6 24.3 %all-to-all-start.2 = ((f32[256,1,8]{2,1,0:T(1,128)}), f32[256,1,8]{2,1,0:T(1,128)S(1)}, u32[]{:S(2)}, u32[]{:S(2)}) async-start(f32[256,1,8]{2,1,0:T(1,128)} %bitcast.10), calls=%async_computation.2 | async-start | bytes 262144 | tf_op jit(solution)/shard_map/all_to_all | solution.py:452

commit v6 on v5

--- a/solution.py
+++ b/solution.py
@@ -426,15 +426,13 @@
 
     blocks = (tile_devs, slot_cap, row_width)
     group = slots // 3
-    (own,) = gather_rotated(panels, phases, send_slots, (1,))
+    to_next, to_last, own = gather_rotated(panels, phases, send_slots, (2, 0, 1))
+    behind = shift_along(to_next.reshape(blocks), "track", 1)
+    ahead = shift_along(to_last.reshape(blocks), "track", -1)
     own_arrived = lax.all_to_all(
         own.reshape(blocks), "tile", split_axis=0, concat_axis=0, tiled=True
     )
-    to_next, to_last = gather_rotated(panels, phases, send_slots, (2, 0))
-    behind = shift_along(to_next.reshape(blocks), "track", 1)
-    ahead = shift_along(to_last.reshape(blocks), "track", -1)
     mixed = jnp.concatenate([behind, ahead], axis=1)
-    mixed, own_arrived = lax.optimization_barrier((mixed, own_arrived))
     arrived = lax.all_to_all(mixed, "tile", split_axis=0, concat_axis=0, tiled=True)
     tables = phase_tables(
         (device * tiles_here).astype(jnp.int32).reshape(1),

time: 106 us -> 104 us (0.981)
  starting transfers between devices: 39.1 us -> 34.4 us
  waiting for transfers between devices: 26.2 us -> 30.8 us
  Pallas kernels: 37.8 us -> 35.1 us
    all_to_all x1, starting transfers between devices: 9.5 us -> 6.67 us  [on_device(): lax.all_to_all(mixed, 'tile', split_axis=0, concat_axis=0, tiled=True)]
    all_to_all x1, waiting for transfers between devices: 0.01 us -> 2.83 us  [on_device(): lax.all_to_all(own.reshape(blocks), 'tile', split_axis=0, concat_axis=0,...]
    pallas_call x2 -> x1, Pallas kernels: 7.47 us -> 4.81 us  [gather_rotated(): pl.pallas_call(kernel, out_shape=[jax.ShapeDtypeStruct((count, width), jn...]
    all_to_all x1, starting transfers between devices: 11.7 us -> 9.87 us  [on_device(): lax.all_to_all(corr, ('track', 'tile'), split_axis=0, concat_axis=0, tile...]
    all_to_all x1, waiting for transfers between devices: 7.18 us -> 8.95 us  [on_device(): lax.all_to_all(mixed, 'tile', split_axis=0, concat_axis=0, tiled=True)]
  transfers between devices with their start and end apart: 5 -> 5, of which waited for: 4 -> 5; matrix products, arithmetic and copies ran while one was open for 1% -> 1% of each run, Pallas kernels for 21% -> 18%
where the time goes in v6:
time: 104 us; the launch traced here: 103 us
  Pallas kernels  35.1 us (34%)
  starting transfers between devices  34.4 us (33%)
  waiting for transfers between devices  30.8 us (30%)
  other arithmetic  1.77 us (2%)
    all_to_all x1, waiting for transfers between devices, on_device(): lax.all_to_all(corr, ('track', 'tile'), split_axis=0, concat_axis=0, tile...  12.6 us
    pallas_call x1, Pallas kernels, focus(): pl.pallas_call(make_focus_kernel(mixed, own, pixels, bins, tiles, chunk,...  12.2 us
    all_to_all x1, starting transfers between devices, on_device(): lax.all_to_all(own.reshape(blocks), 'tile', split_axis=0, concat_axis=0,...  12 us
    pallas_call x1, Pallas kernels, own_forward(): pl.pallas_call(kernel, grid_spec=pltpu.PrefetchScalarGridSpec(num_scalar_...  10.2 us
    all_to_all x1, starting transfers between devices, on_device(): lax.all_to_all(corr, ('track', 'tile'), split_axis=0, concat_axis=0, tile...  9.87 us
    all_to_all x1, waiting for transfers between devices, on_device(): lax.all_to_all(mixed, 'tile', split_axis=0, concat_axis=0, tiled=True)  8.95 us
    pallas_call x1, Pallas kernels, phase_tables(): pl.pallas_call(kernel, in_specs=[smem, smem, vmem, vmem], out_specs=[vmem...  7.9 us
    all_to_all x1, starting transfers between devices, on_device(): lax.all_to_all(mixed, 'tile', split_axis=0, concat_axis=0, tiled=True)  6.67 us
  transfers between devices with their start and end apart: 5, of which 5 were waited for; matrix products, arithmetic and copies ran while one was open for 1% of the time, Pallas kernels for 18%

profile of v6, /device:TPU:1, one launch (start us, length us, event | category | flops | bytes accessed | tf_op | source)
XLA Modules:
  0.0 103.0 jit_solution(10476095522579050013)
XLA Ops:
  0.6 4.8 %gather_rotated.1 = (bf16[256,1024]{1,0:T(8,128)(2,1)}, bf16[256,1024]{1,0:T(8,128)(2,1)}, bf16[256,1024]{1,0:T(8,128)(2,1)}) custom-call(bf16[1024,1024]{1,0:T(8,128)(2,1)} %panels_ref.1, f32[1,64]{1,0:T(1,128)} %bitcast.18, s32[6,128]{1,0:T(8,128)} %bitcast.17), custom_call_target="tpu_custom_call" | custom-call | tf_op jit(solution)/shard_map/gather_rotated/pallas_call | solution.py:68
  5.4 12.0 %all-to-all-start.1 = ((bf16[32,8,1024]{2,1,0:T(8,128)(2,1)}), bf16[32,8,1024]{2,1,0:T(8,128)(2,1)S(1)}, u32[]{:S(2)}, u32[]{:S(2)}) async-start(bf16[32,8,1024]{2,1,0:T(8,128)(2,1)} %bitcast.15), calls=%async_computation.1 | async-start | bytes 1048576 | tf_op jit(solution)/shard_map/all_to_all | solution.py:432
  17.5 2.9 %collective-permute-start.1 = (bf16[32,8,1024]{2,1,0:T(8,128)(2,1)}, bf16[32,8,1024]{2,1,0:T(8,128)(2,1)S(1)}, u32[]{:S(2)}, u32[]{:S(2)}) collective-permute-start(bf16[32,8,1024]{2,1,0:T(8,128)(2,1)} %bitcast.20), channel_id=1, source_target_pairs={{32,0},{64,32},{96,64},{128,96},{160,128},{192,160},{224,192},{33,... | collective-permute-start | bytes 1572872 | tf_op jit(solution)/shard_map/ppermute | solution.py:19
  20.4 0.0 copy-start.2
  20.4 3.0 %collective-permute-start = (bf16[32,8,1024]{2,1,0:T(8,128)(2,1)}, bf16[32,8,1024]{2,1,0:T(8,128)(2,1)S(1)}, u32[]{:S(2)}, u32[]{:S(2)}) collective-permute-start(bf16[32,8,1024]{2,1,0:T(8,128)(2,1)} %bitcast.19), channel_id=1, source_target_pairs={{0,32},{32,64},{64,96},{96,128},{128,160},{160,192},{192,224},{1,3... | collective-permute-start | bytes 1572872 | tf_op jit(solution)/shard_map/ppermute | solution.py:19
  23.4 5.4 %collective-permute-done.1 = bf16[32,8,1024]{2,1,0:T(8,128)(2,1)S(1)} collective-permute-done((bf16[32,8,1024]{2,1,0:T(8,128)(2,1)}, bf16[32,8,1024]{2,1,0:T(8,128)(2,1)S(1)}, u32[]{:S(2)}, u32[]{:S(2)}) %collective-permute-start.1) | collective-permute-done | bytes 524320 | tf_op jit(solution)/shard_map/ppermute | solution.py:19
  28.8 1.0 collective-permute-done
  29.8 1.1 %pad_maximum_fusion = bf16[32,16,1024]{2,1,0:T(8,128)(2,1)} fusion(bf16[32,8,1024]{2,1,0:T(8,128)(2,1)S(1)} %collective-permute-done.1, bf16[32,8,1024]{2,1,0:T(8,128)(2,1)S(1)} %collective-permute-done), kind=kLoop, calls=%fused_computation | loop fusion | flops 2097152 | bytes 2097152 | tf_op jit(solution)/shard_map/concatenate | solution.py:435
  30.9 2.8 %all-to-all-done.1 = bf16[32,8,1024]{2,1,0:T(8,128)(2,1)S(1)} async-done(((bf16[32,8,1024]{2,1,0:T(8,128)(2,1)}), bf16[32,8,1024]{2,1,0:T(8,128)(2,1)S(1)}, u32[]{:S(2)}, u32[]{:S(2)}) %all-to-all-start.1) | async-done | bytes 524320 | tf_op jit(solution)/shard_map/all_to_all | solution.py:432
  33.7 0.0 copy-start.1
  33.8 6.7 %all-to-all-start = ((bf16[32,16,1024]{2,1,0:T(8,128)(2,1)}), bf16[32,16,1024]{2,1,0:T(8,128)(2,1)S(1)}, u32[]{:S(2)}, u32[]{:S(2)}) async-start(bf16[32,16,1024]{2,1,0:T(8,128)(2,1)} %pad_maximum_fusion), calls=%async_computation | async-start | bytes 2097152 | tf_op jit(solution)/shard_map/all_to_all | solution.py:436
  40.4 7.9 %phase_tables.1 = (f32[4,768,128]{2,1,0:T(8,128)}, f32[4,768,128]{2,1,0:T(8,128)}, f32[4,768,128]{2,1,0:T(8,128)}, f32[4,768,128]{2,1,0:T(8,128)}) custom-call(s32[1]{0:T(128)} %bitcast.6.base_ref, s32[4]{0:T(128)} %counts_ref.1, s32[4,512]{1,0:T(4,128)} %slot_ref.1, s32[4,512]{1,0:T(4,128)} %ping_ref.1), custom_call_target="tpu_custom_call" | custom-call | tf_op jit(solution)/shard_map/phase_tables/pallas_call | solution.py:154
  48.3 0.0 copy-done.2
  48.3 0.0 copy-done.1
  48.4 0.0 copy-start
  48.4 10.2 %own_forward.1 = (f32[4,264,1024]{2,1,0:T(8,128)}, f32[4,264,1024]{2,1,0:T(8,128)}) custom-call(s32[4]{0:T(128)} %class_ref.3, bf16[256,1024]{1,0:T(8,128)(2,1)} %bitcast.14, bf16[4,1024,512]{2,1,0:T(8,128)(2,1)} %weight_ref.3, f32[4,768,128]{2,1,0:T(8,128)} %get-tuple-element.15.base_c, f32[4,768,128]{2,1,0:T(8,128)} %get-tuple-element.16.base_s, ...), custom_call_target="tpu_custom_call" | custom-call | tf_op jit(solution)/shard_map/own_forward/pallas_call | solution.py:236
  58.6 9.0 %all-to-all-done = bf16[32,16,1024]{2,1,0:T(8,128)(2,1)S(1)} async-done(((bf16[32,16,1024]{2,1,0:T(8,128)(2,1)}), bf16[32,16,1024]{2,1,0:T(8,128)(2,1)S(1)}, u32[]{:S(2)}, u32[]{:S(2)}) %all-to-all-start) | async-done | bytes 1048608 | tf_op jit(solution)/shard_map/all_to_all | solution.py:436
  67.5 0.0 copy-done
  67.5 12.2 %focus.1 = (f32[4,2,1024]{2,1,0:T(2,128)}, f32[256,8]{1,0:T(8,128)}) custom-call(s32[4]{0:T(128)S(1)} %copy-done, s32[1]{0:T(128)} %bitcast.track_ref, bf16[512,1024]{1,0:T(8,128)(2,1)S(1)} %bitcast.13, bf16[4,1024,512]{2,1,0:T(8,128)(2,1)} %weight_ref.3, f32[4,768,128]{2,1,0:T(8,128)} %get-tuple-element.15.base_c, f32[4,768,128]{2,1,0:T(8,128)} %get-tuple-element.16.base_s, ...), custom_call_target="tpu_custom_call" | custom-call | tf_op jit(solution)/shard_map/focus/pallas_call | solution.py:386
  79.8 9.9 %all-to-all-start.2 = ((f32[256,1,8]{2,1,0:T(1,128)}), f32[256,1,8]{2,1,0:T(1,128)S(1)}, u32[]{:S(2)}, u32[]{:S(2)}) async-start(f32[256,1,8]{2,1,0:T(1,128)} %bitcast.10), calls=%async_computation.2 | async-start | bytes 262144 | tf_op jit(solution)/shard_map/all_to_all | solution.py:450
  89.6 12.6 %all-to-all-done.2 = f32[256,1,8]{2,1,0:T(1,128)S(1)} async-done(((f32[256,1,8]{2,1,0:T(1,128)}), f32[256,1,8]{2,1,0:T(1,128)S(1)}, u32[]{:S(2)}, u32[]{:S(2)}) %all-to-all-start.2) | async-done | bytes 8224 | tf_op jit(solution)/shard_map/all_to_all | solution.py:450
  102.2 0.1 broadcast_in_dim.15
  102.3 0.7 select_reduce_fusion
  (3 shorter events, 0.0 us)
Async XLA Ops:
  5.4 28.3 %all-to-all-start.1 = ((bf16[32,8,1024]{2,1,0:T(8,128)(2,1)}), bf16[32,8,1024]{2,1,0:T(8,128)(2,1)S(1)}, u32[]{:S(2)}, u32[]{:S(2)}) async-start(bf16[32,8,1024]{2,1,0:T(8,128)(2,1)} %bitcast.15), calls=%async_computation.1 | async-start | bytes 1048576 | tf_op jit(solution)/shard_map/all_to_all | solution.py:432
  17.5 11.3 %collective-permute-start.1 = (bf16[32,8,1024]{2,1,0:T(8,128)(2,1)}, bf16[32,8,1024]{2,1,0:T(8,128)(2,1)S(1)}, u32[]{:S(2)}, u32[]{:S(2)}) collective-permute-start(bf16[32,8,1024]{2,1,0:T(8,128)(2,1)} %bitcast.20), channel_id=1, source_target_pairs={{32,0},{64,32},{96,64},{128,96},{160,128},{192,160},{224,192},{33,... | collective-permute-start | bytes 1572872 | tf_op jit(solution)/shard_map/ppermute | solution.py:19
  20.4 28.0 %copy-start.2 = (s32[768]{0:T(1024)S(1)}, s32[768]{0:T(1024)}, u32[]{:S(2)}) copy-start(s32[768]{0:T(1024)} %param.12) | copy-start | bytes 9220
  20.4 9.4 %collective-permute-start = (bf16[32,8,1024]{2,1,0:T(8,128)(2,1)}, bf16[32,8,1024]{2,1,0:T(8,128)(2,1)S(1)}, u32[]{:S(2)}, u32[]{:S(2)}) collective-permute-start(bf16[32,8,1024]{2,1,0:T(8,128)(2,1)} %bitcast.19), channel_id=1, source_target_pairs={{0,32},{32,64},{64,96},{96,128},{128,160},{160,192},{192,224},{1,3... | collective-permute-start | bytes 1572872 | tf_op jit(solution)/shard_map/ppermute | solution.py:19
  33.7 14.6 %copy-start.1 = (bf16[32,8,1024]{2,1,0:T(8,128)(2,1)}, bf16[32,8,1024]{2,1,0:T(8,128)(2,1)S(1)}, u32[]{:S(2)}) copy-start(bf16[32,8,1024]{2,1,0:T(8,128)(2,1)S(1)} %all-to-all-done.1) | copy-start | bytes 1572868
  33.8 33.8 %all-to-all-start = ((bf16[32,16,1024]{2,1,0:T(8,128)(2,1)}), bf16[32,16,1024]{2,1,0:T(8,128)(2,1)S(1)}, u32[]{:S(2)}, u32[]{:S(2)}) async-start(bf16[32,16,1024]{2,1,0:T(8,128)(2,1)} %pad_maximum_fusion), calls=%async_computation | async-start | bytes 2097152 | tf_op jit(solution)/shard_map/all_to_all | solution.py:436
  48.4 19.2 %copy-start = (s32[4]{0:T(128)S(1)}, s32[4]{0:T(128)}, u32[]{:S(2)}) copy-start(s32[4]{0:T(128)} %class_ref.3) | copy-start | bytes 52
  79.8 22.5 %all-to-all-start.2 = ((f32[256,1,8]{2,1,0:T(1,128)}), f32[256,1,8]{2,1,0:T(1,128)S(1)}, u32[]{:S(2)}, u32[]{:S(2)}) async-start(f32[256,1,8]{2,1,0:T(1,128)} %bitcast.10), calls=%async_computation.2 | async-start | bytes 262144 | tf_op jit(solution)/shard_map/all_to_all | solution.py:450

commit v7 on v6

--- a/solution.py
+++ b/solution.py
@@ -27,10 +27,10 @@
     return jnp.broadcast_to(row, (8, row.shape[1])).T[:, :1]
 
 
-def rotated_rows(panels_ref, phases_ref, slots_ref, first, count):
+def rotated_rows(panels_ref, cosine, sine, slots_ref, first, count):
     rows_here, width = panels_ref.shape
     bins = width // 2
-    pings = phases_ref.shape[1]
+    pings = cosine.shape[1]
     columns = [
         column(slots_ref[pl.ds(row, 1), :].astype(jnp.float32))
         for row in range(first // LANES, (first + count) // LANES)
@@ -39,11 +39,10 @@
     row_ids = lax.broadcasted_iota(jnp.int32, (count, rows_here), 1)
     pick = jnp.where(row_ids == slot_row, 1.0, 0.0).astype(jnp.bfloat16)
     picked = jnp.dot(pick, panels_ref[...], preferred_element_type=jnp.float32)
-    phases = phases_ref[...]
     ping_ids = lax.broadcasted_iota(jnp.int32, (count, pings), 1)
     owned = ping_ids == (slot_row // (rows_here // pings))
-    cos_col = jnp.sum(jnp.where(owned, jnp.cos(phases), 0.0), axis=1, keepdims=True)
-    sin_col = jnp.sum(jnp.where(owned, jnp.sin(phases), 0.0), axis=1, keepdims=True)
+    cos_col = jnp.sum(jnp.where(owned, cosine, 0.0), axis=1, keepdims=True)
+    sin_col = jnp.sum(jnp.where(owned, sine, 0.0), axis=1, keepdims=True)
     real_part = picked[:, :bins]
     imag_part = picked[:, bins:]
     return (
@@ -58,9 +57,10 @@
     bins = width // 2
 
     def kernel(panels_ref, phases_ref, slots_ref, *outs):
+        cosine, sine = cos_sin(phases_ref[...])
         for offset, out in zip(offsets, outs):
             real_part, imag_part = rotated_rows(
-                panels_ref, phases_ref, slots_ref, offset * count, count
+                panels_ref, cosine, sine, slots_ref, offset * count, count
             )
             out[:, :bins] = real_part
             out[:, bins:] = imag_part
@@ -354,22 +354,23 @@
         corr_acc[...] = jnp.zeros_like(corr_acc)
         project(0, 0, 0, pieces)
         lax.fori_loop(0, tiles, one_tile, 0)
-        totals = jnp.sum(corr_acc[...], axis=1, keepdims=True)
-        row = lax.broadcasted_iota(jnp.int32, (mixed + own, LANES), 0)
-        lane = lax.broadcasted_iota(jnp.int32, (mixed + own, LANES), 1)
-        placed = jnp.where(row % cap == lane, totals, 0.0)
-        placed = jnp.sum(placed.reshape((mixed + own) // cap, cap, LANES), axis=1)
-        corr_acc[pl.ds(0, (mixed + own) // cap), :] = placed
         corr_ref[...] = jnp.zeros_like(corr_ref)
+        lane = lax.broadcasted_iota(jnp.int32, (cap, LANES), 1)
+        pick = lax.broadcasted_iota(jnp.int32, (cap, LANES), 0) == lane
         track = track_ref[0]
         sources = own // cap
-        cuts = (pl.ds(0, sources, stride=2), pl.ds(2 * sources, sources), pl.ds(1, sources, stride=2))
-        for k, cut in enumerate(cuts):
+        placed = []
+        for source in range((mixed + own) // cap):
+            total = jnp.sum(corr_acc[pl.ds(source * cap, cap), :], axis=1, keepdims=True)
+            placed.append(jnp.sum(jnp.where(pick, total, 0.0), axis=0, keepdims=True))
+        starts = (placed[0 : 2 * sources : 2], placed[2 * sources :], placed[1 : 2 * sources : 2])
+        for k, part in enumerate(starts):
+            block = jnp.concatenate(part, axis=0)[:, :cap]
 
             @pl.when((track + k >= 1) & (track + k <= tracks))
-            def _(k=k, cut=cut):
+            def _(k=k, block=block):
                 target = pl.ds(pl.multiple_of((track + k - 1) * sources, sources), sources)
-                corr_ref[target, :] = corr_acc[cut, :][:, :cap]
+                corr_ref[target, :] = block
 
     return focus_kernel
 

time: 104 us -> 104 us (level)
  no operation moved by 1% of the time
where the time goes in v7:
time: 104 us; the launch traced here: 103 us
  Pallas kernels  35 us (34%)
  starting transfers between devices  34.5 us (33%)
  waiting for transfers between devices  30.8 us (30%)
  other arithmetic  1.77 us (2%)
    all_to_all x1, waiting for transfers between devices, on_device(): lax.all_to_all(corr, ('track', 'tile'), split_axis=0, concat_axis=0, tile...  12.6 us
    pallas_call x1, Pallas kernels, focus(): pl.pallas_call(make_focus_kernel(mixed, own, pixels, bins, tiles, chunk,...  12.2 us
    all_to_all x1, starting transfers between devices, on_device(): lax.all_to_all(own.reshape(blocks), 'tile', split_axis=0, concat_axis=0,...  12 us
    pallas_call x1, Pallas kernels, own_forward(): pl.pallas_call(kernel, grid_spec=pltpu.PrefetchScalarGridSpec(num_scalar_...  10.2 us
    all_to_all x1, starting transfers between devices, on_device(): lax.all_to_all(corr, ('track', 'tile'), split_axis=0, concat_axis=0, tile...  9.9 us
    all_to_all x1, waiting for transfers between devices, on_device(): lax.all_to_all(mixed, 'tile', split_axis=0, concat_axis=0, tiled=True)  8.94 us
    pallas_call x1, Pallas kernels, phase_tables(): pl.pallas_call(kernel, in_specs=[smem, smem, vmem, vmem], out_specs=[vmem...  7.9 us
    all_to_all x1, starting transfers between devices, on_device(): lax.all_to_all(mixed, 'tile', split_axis=0, concat_axis=0, tiled=True)  6.67 us
  transfers between devices with their start and end apart: 5, of which 5 were waited for; matrix products, arithmetic and copies ran while one was open for 1% of the time, Pallas kernels for 18%

profile of v7, /device:TPU:1, one launch (start us, length us, event | category | flops | bytes accessed | tf_op | source)
XLA Modules:
  0.0 102.9 jit_solution(2583316036467959727)
XLA Ops:
  0.6 4.8 %gather_rotated.1 = (bf16[256,1024]{1,0:T(8,128)(2,1)}, bf16[256,1024]{1,0:T(8,128)(2,1)}, bf16[256,1024]{1,0:T(8,128)(2,1)}) custom-call(bf16[1024,1024]{1,0:T(8,128)(2,1)} %panels_ref.1, f32[1,64]{1,0:T(1,128)} %bitcast.18, s32[6,128]{1,0:T(8,128)} %bitcast.17), custom_call_target="tpu_custom_call" | custom-call | tf_op jit(solution)/shard_map/gather_rotated/pallas_call | solution.py:68
  5.4 12.0 %all-to-all-start.1 = ((bf16[32,8,1024]{2,1,0:T(8,128)(2,1)}), bf16[32,8,1024]{2,1,0:T(8,128)(2,1)S(1)}, u32[]{:S(2)}, u32[]{:S(2)}) async-start(bf16[32,8,1024]{2,1,0:T(8,128)(2,1)} %bitcast.15), calls=%async_computation.1 | async-start | bytes 1048576 | tf_op jit(solution)/shard_map/all_to_all | solution.py:433
  17.4 2.9 %collective-permute-start.1 = (bf16[32,8,1024]{2,1,0:T(8,128)(2,1)}, bf16[32,8,1024]{2,1,0:T(8,128)(2,1)S(1)}, u32[]{:S(2)}, u32[]{:S(2)}) collective-permute-start(bf16[32,8,1024]{2,1,0:T(8,128)(2,1)} %bitcast.20), channel_id=1, source_target_pairs={{32,0},{64,32},{96,64},{128,96},{160,128},{192,160},{224,192},{33,... | collective-permute-start | bytes 1572872 | tf_op jit(solution)/shard_map/ppermute | solution.py:19
  20.3 0.0 copy-start.2
  20.3 3.0 %collective-permute-start = (bf16[32,8,1024]{2,1,0:T(8,128)(2,1)}, bf16[32,8,1024]{2,1,0:T(8,128)(2,1)S(1)}, u32[]{:S(2)}, u32[]{:S(2)}) collective-permute-start(bf16[32,8,1024]{2,1,0:T(8,128)(2,1)} %bitcast.19), channel_id=1, source_target_pairs={{0,32},{32,64},{64,96},{96,128},{128,160},{160,192},{192,224},{1,3... | collective-permute-start | bytes 1572872 | tf_op jit(solution)/shard_map/ppermute | solution.py:19
  23.3 5.4 %collective-permute-done.1 = bf16[32,8,1024]{2,1,0:T(8,128)(2,1)S(1)} collective-permute-done((bf16[32,8,1024]{2,1,0:T(8,128)(2,1)}, bf16[32,8,1024]{2,1,0:T(8,128)(2,1)S(1)}, u32[]{:S(2)}, u32[]{:S(2)}) %collective-permute-start.1) | collective-permute-done | bytes 524320 | tf_op jit(solution)/shard_map/ppermute | solution.py:19
  28.8 1.0 collective-permute-done
  29.8 1.1 %pad_maximum_fusion = bf16[32,16,1024]{2,1,0:T(8,128)(2,1)} fusion(bf16[32,8,1024]{2,1,0:T(8,128)(2,1)S(1)} %collective-permute-done.1, bf16[32,8,1024]{2,1,0:T(8,128)(2,1)S(1)} %collective-permute-done), kind=kLoop, calls=%fused_computation | loop fusion | flops 2097152 | bytes 2097152 | tf_op jit(solution)/shard_map/concatenate | solution.py:436
  30.9 2.8 %all-to-all-done.1 = bf16[32,8,1024]{2,1,0:T(8,128)(2,1)S(1)} async-done(((bf16[32,8,1024]{2,1,0:T(8,128)(2,1)}), bf16[32,8,1024]{2,1,0:T(8,128)(2,1)S(1)}, u32[]{:S(2)}, u32[]{:S(2)}) %all-to-all-start.1) | async-done | bytes 524320 | tf_op jit(solution)/shard_map/all_to_all | solution.py:433
  33.7 0.0 copy-start.1
  33.7 6.7 %all-to-all-start = ((bf16[32,16,1024]{2,1,0:T(8,128)(2,1)}), bf16[32,16,1024]{2,1,0:T(8,128)(2,1)S(1)}, u32[]{:S(2)}, u32[]{:S(2)}) async-start(bf16[32,16,1024]{2,1,0:T(8,128)(2,1)} %pad_maximum_fusion), calls=%async_computation | async-start | bytes 2097152 | tf_op jit(solution)/shard_map/all_to_all | solution.py:437
  40.4 7.9 %phase_tables.1 = (f32[4,768,128]{2,1,0:T(8,128)}, f32[4,768,128]{2,1,0:T(8,128)}, f32[4,768,128]{2,1,0:T(8,128)}, f32[4,768,128]{2,1,0:T(8,128)}) custom-call(s32[1]{0:T(128)} %bitcast.6.base_ref, s32[4]{0:T(128)} %counts_ref.1, s32[4,512]{1,0:T(4,128)} %slot_ref.1, s32[4,512]{1,0:T(4,128)} %ping_ref.1), custom_call_target="tpu_custom_call" | custom-call | tf_op jit(solution)/shard_map/phase_tables/pallas_call | solution.py:154
  48.3 0.0 copy-done.2
  48.3 0.0 copy-done.1
  48.3 0.0 copy-start
  48.3 10.2 %own_forward.1 = (f32[4,264,1024]{2,1,0:T(8,128)}, f32[4,264,1024]{2,1,0:T(8,128)}) custom-call(s32[4]{0:T(128)} %class_ref.3, bf16[256,1024]{1,0:T(8,128)(2,1)} %bitcast.14, bf16[4,1024,512]{2,1,0:T(8,128)(2,1)} %weight_ref.3, f32[4,768,128]{2,1,0:T(8,128)} %get-tuple-element.15.base_c, f32[4,768,128]{2,1,0:T(8,128)} %get-tuple-element.16.base_s, ...), custom_call_target="tpu_custom_call" | custom-call | tf_op jit(solution)/shard_map/own_forward/pallas_call | solution.py:236
  58.5 8.9 %all-to-all-done = bf16[32,16,1024]{2,1,0:T(8,128)(2,1)S(1)} async-done(((bf16[32,16,1024]{2,1,0:T(8,128)(2,1)}), bf16[32,16,1024]{2,1,0:T(8,128)(2,1)S(1)}, u32[]{:S(2)}, u32[]{:S(2)}) %all-to-all-start) | async-done | bytes 1048608 | tf_op jit(solution)/shard_map/all_to_all | solution.py:437
  67.5 0.0 copy-done
  67.5 12.2 %focus.1 = (f32[4,2,1024]{2,1,0:T(2,128)}, f32[256,8]{1,0:T(8,128)}) custom-call(s32[4]{0:T(128)S(1)} %copy-done, s32[1]{0:T(128)} %bitcast.track_ref, bf16[512,1024]{1,0:T(8,128)(2,1)S(1)} %bitcast.13, bf16[4,1024,512]{2,1,0:T(8,128)(2,1)} %weight_ref.3, f32[4,768,128]{2,1,0:T(8,128)} %get-tuple-element.15.base_c, f32[4,768,128]{2,1,0:T(8,128)} %get-tuple-element.16.base_s, ...), custom_call_target="tpu_custom_call" | custom-call | tf_op jit(solution)/shard_map/focus/pallas_call | solution.py:387
  79.6 9.9 %all-to-all-start.2 = ((f32[256,1,8]{2,1,0:T(1,128)}), f32[256,1,8]{2,1,0:T(1,128)S(1)}, u32[]{:S(2)}, u32[]{:S(2)}) async-start(f32[256,1,8]{2,1,0:T(1,128)} %bitcast.10), calls=%async_computation.2 | async-start | bytes 262144 | tf_op jit(solution)/shard_map/all_to_all | solution.py:451
  89.5 12.6 %all-to-all-done.2 = f32[256,1,8]{2,1,0:T(1,128)S(1)} async-done(((f32[256,1,8]{2,1,0:T(1,128)}), f32[256,1,8]{2,1,0:T(1,128)S(1)}, u32[]{:S(2)}, u32[]{:S(2)}) %all-to-all-start.2) | async-done | bytes 8224 | tf_op jit(solution)/shard_map/all_to_all | solution.py:451
  102.1 0.1 broadcast_in_dim.15
  102.2 0.7 select_reduce_fusion
  (3 shorter events, 0.0 us)
Async XLA Ops:
  5.4 28.3 %all-to-all-start.1 = ((bf16[32,8,1024]{2,1,0:T(8,128)(2,1)}), bf16[32,8,1024]{2,1,0:T(8,128)(2,1)S(1)}, u32[]{:S(2)}, u32[]{:S(2)}) async-start(bf16[32,8,1024]{2,1,0:T(8,128)(2,1)} %bitcast.15), calls=%async_computation.1 | async-start | bytes 1048576 | tf_op jit(solution)/shard_map/all_to_all | solution.py:433
  17.4 11.3 %collective-permute-start.1 = (bf16[32,8,1024]{2,1,0:T(8,128)(2,1)}, bf16[32,8,1024]{2,1,0:T(8,128)(2,1)S(1)}, u32[]{:S(2)}, u32[]{:S(2)}) collective-permute-start(bf16[32,8,1024]{2,1,0:T(8,128)(2,1)} %bitcast.20), channel_id=1, source_target_pairs={{32,0},{64,32},{96,64},{128,96},{160,128},{192,160},{224,192},{33,... | collective-permute-start | bytes 1572872 | tf_op jit(solution)/shard_map/ppermute | solution.py:19
  20.3 28.0 %copy-start.2 = (s32[768]{0:T(1024)S(1)}, s32[768]{0:T(1024)}, u32[]{:S(2)}) copy-start(s32[768]{0:T(1024)} %param.12) | copy-start | bytes 9220
  20.3 9.4 %collective-permute-start = (bf16[32,8,1024]{2,1,0:T(8,128)(2,1)}, bf16[32,8,1024]{2,1,0:T(8,128)(2,1)S(1)}, u32[]{:S(2)}, u32[]{:S(2)}) collective-permute-start(bf16[32,8,1024]{2,1,0:T(8,128)(2,1)} %bitcast.19), channel_id=1, source_target_pairs={{0,32},{32,64},{64,96},{96,128},{128,160},{160,192},{192,224},{1,3... | collective-permute-start | bytes 1572872 | tf_op jit(solution)/shard_map/ppermute | solution.py:19
  33.7 14.6 %copy-start.1 = (bf16[32,8,1024]{2,1,0:T(8,128)(2,1)}, bf16[32,8,1024]{2,1,0:T(8,128)(2,1)S(1)}, u32[]{:S(2)}) copy-start(bf16[32,8,1024]{2,1,0:T(8,128)(2,1)S(1)} %all-to-all-done.1) | copy-start | bytes 1572868
  33.7 33.8 %all-to-all-start = ((bf16[32,16,1024]{2,1,0:T(8,128)(2,1)}), bf16[32,16,1024]{2,1,0:T(8,128)(2,1)S(1)}, u32[]{:S(2)}, u32[]{:S(2)}) async-start(bf16[32,16,1024]{2,1,0:T(8,128)(2,1)} %pad_maximum_fusion), calls=%async_computation | async-start | bytes 2097152 | tf_op jit(solution)/shard_map/all_to_all | solution.py:437
  48.3 19.1 %copy-start = (s32[4]{0:T(128)S(1)}, s32[4]{0:T(128)}, u32[]{:S(2)}) copy-start(s32[4]{0:T(128)} %class_ref.3) | copy-start | bytes 52
  79.6 22.5 %all-to-all-start.2 = ((f32[256,1,8]{2,1,0:T(1,128)}), f32[256,1,8]{2,1,0:T(1,128)S(1)}, u32[]{:S(2)}, u32[]{:S(2)}) async-start(f32[256,1,8]{2,1,0:T(1,128)} %bitcast.10), calls=%async_computation.2 | async-start | bytes 262144 | tf_op jit(solution)/shard_map/all_to_all | solution.py:451

commit v8 on v6

--- a/solution.py
+++ b/solution.py
@@ -68,7 +68,7 @@
     return pl.pallas_call(
         kernel,
         out_shape=[jax.ShapeDtypeStruct((count, width), jnp.bfloat16) for _ in offsets],
-        compiler_params=pltpu.CompilerParams(vmem_limit_bytes=ALL_VMEM),
+        compiler_params=pltpu.CompilerParams(vmem_limit_bytes=24 * 1024 * 1024),
         name="gather_rotated",
     )(panels, phases.reshape(1, -1), slots.reshape(-1, LANES))
 

time: 104 us -> 105 us (level)
  local copies, waits for them, and re-layouts: 0.11 us -> 3.04 us
  Pallas kernels: 35.1 us -> 33.5 us
    unnamed x6 -> x12, local copies, waits for them, and re-layouts: 0.02 us -> 2.94 us
    pallas_call x1, Pallas kernels: 4.81 us -> 3.2 us  [gather_rotated(): pl.pallas_call(kernel, out_shape=[jax.ShapeDtypeStruct((count, width), jn...]
  transfers between devices with their start and end apart: 5 -> 5, of which waited for: 5 -> 5; matrix products, arithmetic and copies ran while one was open for 1% -> 1% of each run, Pallas kernels for 18% -> 17%
where the time goes in v8:
time: 105 us; the launch traced here: 104 us
  starting transfers between devices  35 us (33%)
  Pallas kernels  33.5 us (32%)
  waiting for transfers between devices  29.9 us (28%)
  local copies, waits for them, and re-layouts  3.04 us (3%)
  other arithmetic  1.77 us (2%)
    all_to_all x1, waiting for transfers between devices, on_device(): lax.all_to_all(corr, ('track', 'tile'), split_axis=0, concat_axis=0, tile...  12.6 us
    pallas_call x1, Pallas kernels, focus(): pl.pallas_call(make_focus_kernel(mixed, own, pixels, bins, tiles, chunk,...  12.2 us
    all_to_all x1, starting transfers between devices, on_device(): lax.all_to_all(own.reshape(blocks), 'tile', split_axis=0, concat_axis=0,...  12 us
    all_to_all x1, starting transfers between devices, on_device(): lax.all_to_all(corr, ('track', 'tile'), split_axis=0, concat_axis=0, tile...  10.7 us
    pallas_call x1, Pallas kernels, own_forward(): pl.pallas_call(kernel, grid_spec=pltpu.PrefetchScalarGridSpec(num_scalar_...  10.2 us
    all_to_all x1, waiting for transfers between devices, on_device(): lax.all_to_all(mixed, 'tile', split_axis=0, concat_axis=0, tiled=True)  8.11 us
    pallas_call x1, Pallas kernels, phase_tables(): pl.pallas_call(kernel, in_specs=[smem, smem, vmem, vmem], out_specs=[vmem...  7.87 us
    all_to_all x1, starting transfers between devices, on_device(): lax.all_to_all(mixed, 'tile', split_axis=0, concat_axis=0, tiled=True)  6.35 us
  transfers between devices with their start and end apart: 5, of which 5 were waited for; matrix products, arithmetic and copies ran while one was open for 1% of the time, Pallas kernels for 17%

profile of v8, /device:TPU:1, one launch (start us, length us, event | category | flops | bytes accessed | tf_op | source)
XLA Modules:
  0.0 104.0 jit_solution(8267437122956409649)
XLA Ops:
  0.6 0.0 copy-start
  0.6 1.6 %copy-done = bf16[1024,1024]{1,0:T(8,128)(2,1)S(1)} copy-done((bf16[1024,1024]{1,0:T(8,128)(2,1)S(1)}, bf16[1024,1024]{1,0:T(8,128)(2,1)}, u32[]{:S(2)}) %copy-start) | copy-done | bytes 2097176
  2.2 0.0 copy-start.1
  2.2 0.7 copy-done.1
  2.9 0.0 copy-start.4
  2.9 0.7 copy-done.4
  3.6 3.2 %gather_rotated.1 = (bf16[256,1024]{1,0:T(8,128)(2,1)S(1)}, bf16[256,1024]{1,0:T(8,128)(2,1)S(1)}, bf16[256,1024]{1,0:T(8,128)(2,1)}) custom-call(bf16[1024,1024]{1,0:T(8,128)(2,1)S(1)} %copy-done, f32[1,64]{1,0:T(1,128)S(1)} %bitcast.15, s32[6,128]{1,0:T(8,128)S(1)} %bitcast.14), custom_call_target="tpu_custom_call" | custom-call | tf_op jit(solution)/shard_map/gather_rotated/pallas_call | solution.py:68
  6.8 12.0 %all-to-all-start.1 = ((bf16[32,8,1024]{2,1,0:T(8,128)(2,1)}), bf16[32,8,1024]{2,1,0:T(8,128)(2,1)S(1)}, u32[]{:S(2)}, u32[]{:S(2)}) async-start(bf16[32,8,1024]{2,1,0:T(8,128)(2,1)} %bitcast.7), calls=%async_computation.1 | async-start | bytes 1048576 | tf_op jit(solution)/shard_map/all_to_all | solution.py:432
  18.8 2.9 %collective-permute-start.1 = (bf16[32,8,1024]{2,1,0:T(8,128)(2,1)S(1)}, bf16[32,8,1024]{2,1,0:T(8,128)(2,1)S(1)}, u32[]{:S(2)}, u32[]{:S(2)}) collective-permute-start(bf16[32,8,1024]{2,1,0:T(8,128)(2,1)S(1)} %bitcast.17), channel_id=1, source_target_pairs={{32,0},{64,32},{96,64},{128,96},{160,128},{192,160},{224,192},{33,... | collective-permute-start | bytes 1572872 | tf_op jit(solution)/shard_map/ppermute | solution.py:19
  21.7 0.0 copy-start.2
  21.7 3.0 %collective-permute-start = (bf16[32,8,1024]{2,1,0:T(8,128)(2,1)S(1)}, bf16[32,8,1024]{2,1,0:T(8,128)(2,1)S(1)}, u32[]{:S(2)}, u32[]{:S(2)}) collective-permute-start(bf16[32,8,1024]{2,1,0:T(8,128)(2,1)S(1)} %bitcast.16), channel_id=1, source_target_pairs={{0,32},{32,64},{64,96},{96,128},{128,160},{160,192},{192,224},{1,3... | collective-permute-start | bytes 1572872 | tf_op jit(solution)/shard_map/ppermute | solution.py:19
  24.7 5.2 %collective-permute-done.1 = bf16[32,8,1024]{2,1,0:T(8,128)(2,1)S(1)} collective-permute-done((bf16[32,8,1024]{2,1,0:T(8,128)(2,1)S(1)}, bf16[32,8,1024]{2,1,0:T(8,128)(2,1)S(1)}, u32[]{:S(2)}, u32[]{:S(2)}) %collective-permute-start.1) | collective-permute-done | bytes 524320 | tf_op jit(solution)/shard_map/ppermute | solution.py:19
  29.9 0.9 collective-permute-done
  30.8 1.1 %pad_maximum_fusion = bf16[32,16,1024]{2,1,0:T(8,128)(2,1)} fusion(bf16[32,8,1024]{2,1,0:T(8,128)(2,1)S(1)} %collective-permute-done.1, bf16[32,8,1024]{2,1,0:T(8,128)(2,1)S(1)} %collective-permute-done), kind=kLoop, calls=%fused_computation | loop fusion | flops 2097152 | bytes 2097152 | tf_op jit(solution)/shard_map/concatenate | solution.py:435
  31.9 3.1 %all-to-all-done.1 = bf16[32,8,1024]{2,1,0:T(8,128)(2,1)S(1)} async-done(((bf16[32,8,1024]{2,1,0:T(8,128)(2,1)}), bf16[32,8,1024]{2,1,0:T(8,128)(2,1)S(1)}, u32[]{:S(2)}, u32[]{:S(2)}) %all-to-all-start.1) | async-done | bytes 524320 | tf_op jit(solution)/shard_map/all_to_all | solution.py:432
  35.1 0.0 copy-start.5
  35.1 6.4 %all-to-all-start = ((bf16[32,16,1024]{2,1,0:T(8,128)(2,1)}), bf16[32,16,1024]{2,1,0:T(8,128)(2,1)S(1)}, u32[]{:S(2)}, u32[]{:S(2)}) async-start(bf16[32,16,1024]{2,1,0:T(8,128)(2,1)} %pad_maximum_fusion), calls=%async_computation | async-start | bytes 2097152 | tf_op jit(solution)/shard_map/all_to_all | solution.py:436
  41.4 7.9 %phase_tables.1 = (f32[4,768,128]{2,1,0:T(8,128)}, f32[4,768,128]{2,1,0:T(8,128)}, f32[4,768,128]{2,1,0:T(8,128)}, f32[4,768,128]{2,1,0:T(8,128)}) custom-call(s32[1]{0:T(128)} %bitcast.6.base_ref, s32[4]{0:T(128)} %counts_ref.1, s32[4,512]{1,0:T(4,128)} %slot_ref.1, s32[4,512]{1,0:T(4,128)} %ping_ref.1), custom_call_target="tpu_custom_call" | custom-call | tf_op jit(solution)/shard_map/phase_tables/pallas_call | solution.py:154
  49.3 0.0 copy-done.2
  49.3 0.0 copy-done.5
  49.3 0.0 copy-start.3
  49.3 10.2 %own_forward.1 = (f32[4,264,1024]{2,1,0:T(8,128)}, f32[4,264,1024]{2,1,0:T(8,128)}) custom-call(s32[4]{0:T(128)} %class_ref.3, bf16[256,1024]{1,0:T(8,128)(2,1)} %bitcast.18, bf16[4,1024,512]{2,1,0:T(8,128)(2,1)} %weight_ref.3, f32[4,768,128]{2,1,0:T(8,128)} %get-tuple-element.15.base_c, f32[4,768,128]{2,1,0:T(8,128)} %get-tuple-element.16.base_s, ...), custom_call_target="tpu_custom_call" | custom-call | tf_op jit(solution)/shard_map/own_forward/pallas_call | solution.py:236
  59.5 8.1 %all-to-all-done = bf16[32,16,1024]{2,1,0:T(8,128)(2,1)S(1)} async-done(((bf16[32,16,1024]{2,1,0:T(8,128)(2,1)}), bf16[32,16,1024]{2,1,0:T(8,128)(2,1)S(1)}, u32[]{:S(2)}, u32[]{:S(2)}) %all-to-all-start) | async-done | bytes 1048608 | tf_op jit(solution)/shard_map/all_to_all | solution.py:436
  67.7 0.0 copy-done.3
  67.7 12.2 %focus.1 = (f32[4,2,1024]{2,1,0:T(2,128)}, f32[256,8]{1,0:T(8,128)}) custom-call(s32[4]{0:T(128)S(1)} %copy-done.3, s32[1]{0:T(128)} %bitcast.track_ref, bf16[512,1024]{1,0:T(8,128)(2,1)S(1)} %bitcast.13, bf16[4,1024,512]{2,1,0:T(8,128)(2,1)} %weight_ref.3, f32[4,768,128]{2,1,0:T(8,128)} %get-tuple-element.15.base_c, ...), custom_call_target="tpu_custom_call" | custom-call | tf_op jit(solution)/shard_map/focus/pallas_call | solution.py:386
  79.9 10.7 %all-to-all-start.2 = ((f32[256,1,8]{2,1,0:T(1,128)}), f32[256,1,8]{2,1,0:T(1,128)S(1)}, u32[]{:S(2)}, u32[]{:S(2)}) async-start(f32[256,1,8]{2,1,0:T(1,128)} %bitcast.10), calls=%async_computation.2 | async-start | bytes 262144 | tf_op jit(solution)/shard_map/all_to_all | solution.py:450
  90.6 12.6 %all-to-all-done.2 = f32[256,1,8]{2,1,0:T(1,128)S(1)} async-done(((f32[256,1,8]{2,1,0:T(1,128)}), f32[256,1,8]{2,1,0:T(1,128)S(1)}, u32[]{:S(2)}, u32[]{:S(2)}) %all-to-all-start.2) | async-done | bytes 8224 | tf_op jit(solution)/shard_map/all_to_all | solution.py:450
  103.2 0.1 broadcast_in_dim.15
  103.3 0.7 select_reduce_fusion
  (3 shorter events, 0.0 us)
Async XLA Ops:
  0.6 1.6 %copy-start = (bf16[1024,1024]{1,0:T(8,128)(2,1)S(1)}, bf16[1024,1024]{1,0:T(8,128)(2,1)}, u32[]{:S(2)}) copy-start(bf16[1024,1024]{1,0:T(8,128)(2,1)} %panels_ref.1) | copy-start | bytes 6291460
  2.2 0.7 copy-start.1
  2.9 0.7 copy-start.4
  6.8 28.3 %all-to-all-start.1 = ((bf16[32,8,1024]{2,1,0:T(8,128)(2,1)}), bf16[32,8,1024]{2,1,0:T(8,128)(2,1)S(1)}, u32[]{:S(2)}, u32[]{:S(2)}) async-start(bf16[32,8,1024]{2,1,0:T(8,128)(2,1)} %bitcast.7), calls=%async_computation.1 | async-start | bytes 1048576 | tf_op jit(solution)/shard_map/all_to_all | solution.py:432
  18.8 11.1 %collective-permute-start.1 = (bf16[32,8,1024]{2,1,0:T(8,128)(2,1)S(1)}, bf16[32,8,1024]{2,1,0:T(8,128)(2,1)S(1)}, u32[]{:S(2)}, u32[]{:S(2)}) collective-permute-start(bf16[32,8,1024]{2,1,0:T(8,128)(2,1)S(1)} %bitcast.17), channel_id=1, source_target_pairs={{32,0},{64,32},{96,64},{128,96},{160,128},{192,160},{224,192},{33,... | collective-permute-start | bytes 1572872 | tf_op jit(solution)/shard_map/ppermute | solution.py:19
  21.7 27.6 %copy-start.2 = (s32[768]{0:T(1024)S(1)}, s32[768]{0:T(1024)}, u32[]{:S(2)}) copy-start(s32[768]{0:T(1024)} %param.12) | copy-start | bytes 9220
  21.7 9.1 %collective-permute-start = (bf16[32,8,1024]{2,1,0:T(8,128)(2,1)S(1)}, bf16[32,8,1024]{2,1,0:T(8,128)(2,1)S(1)}, u32[]{:S(2)}, u32[]{:S(2)}) collective-permute-start(bf16[32,8,1024]{2,1,0:T(8,128)(2,1)S(1)} %bitcast.16), channel_id=1, source_target_pairs={{0,32},{32,64},{64,96},{96,128},{128,160},{160,192},{192,224},{1,3... | collective-permute-start | bytes 1572872 | tf_op jit(solution)/shard_map/ppermute | solution.py:19
  35.1 14.3 %copy-start.5 = (bf16[32,8,1024]{2,1,0:T(8,128)(2,1)}, bf16[32,8,1024]{2,1,0:T(8,128)(2,1)S(1)}, u32[]{:S(2)}) copy-start(bf16[32,8,1024]{2,1,0:T(8,128)(2,1)S(1)} %all-to-all-done.1) | copy-start | bytes 1572868
  35.1 32.6 %all-to-all-start = ((bf16[32,16,1024]{2,1,0:T(8,128)(2,1)}), bf16[32,16,1024]{2,1,0:T(8,128)(2,1)S(1)}, u32[]{:S(2)}, u32[]{:S(2)}) async-start(bf16[32,16,1024]{2,1,0:T(8,128)(2,1)} %pad_maximum_fusion), calls=%async_computation | async-start | bytes 2097152 | tf_op jit(solution)/shard_map/all_to_all | solution.py:436
  49.3 18.3 %copy-start.3 = (s32[4]{0:T(128)S(1)}, s32[4]{0:T(128)}, u32[]{:S(2)}) copy-start(s32[4]{0:T(128)} %class_ref.3) | copy-start | bytes 52
  79.9 23.3 %all-to-all-start.2 = ((f32[256,1,8]{2,1,0:T(1,128)}), f32[256,1,8]{2,1,0:T(1,128)S(1)}, u32[]{:S(2)}, u32[]{:S(2)}) async-start(f32[256,1,8]{2,1,0:T(1,128)} %bitcast.10), calls=%async_computation.2 | async-start | bytes 262144 | tf_op jit(solution)/shard_map/all_to_all | solution.py:450
